TPU v7x, 32 devices: a whole 2x2x4 slice. The times are simulated.
32 devices in a mesh: dp: 8 (over z, y), expert: 4 (over x, core).
Axes of the slice: x: 2, y: 2, z: 4, core: 2. Of those that a mesh axis runs over, the one named last changes fastest.
Arguments:
- tokens: bfloat16 [32768, 768], P(('dp', 'expert')), may hold values from -6 to 6
- prev_logits: float32 [32768, 12], P(('dp', 'expert')), may hold values from -4 to 4
- routes: int32 [32768, 2], P(('dp', 'expert')), may hold values from 0 to 11, all different within a row
- priority: int32 [32768], P(('dp', 'expert')), may hold values from 0 to 1023, as said below
- norm_attn: float32 [768], replicated, may hold values from 0.5 to 1.5
- w_query: bfloat16 [768, 768], replicated, may hold values from -0.21875 to 0.21875
- w_key: bfloat16 [768, 768], replicated, may hold values from -0.21875 to 0.21875
- w_value: bfloat16 [768, 768], replicated, may hold values from -0.21875 to 0.21875
- w_out: bfloat16 [768, 768], replicated, may hold values from -6 to 6
- norm_ffn: float32 [768], replicated, may hold values from 0.5 to 1.5
- router: bfloat16 [768, 12], replicated, may hold values from -0.109375 to 0.109375
- const_w: bfloat16 [2, 768, 2], replicated, may hold values from -0.21875 to 0.21875
- const_v: float32 [2, 768], replicated, may hold values from -6 to 6
- w_gate: bfloat16 [8, 768, 2048], P('expert'), may hold values from -0.21875 to 0.21875
- w_up: bfloat16 [8, 768, 2048], P('expert'), may hold values from -0.21875 to 0.21875
- w_down: bfloat16 [8, 2048, 768], P('expert'), may hold values from -0.125 to 0.125
- cotangent: bfloat16 [32768, 768], P(('dp', 'expert')), may hold values from -6 to 6
Outputs:
- mixed_out: bfloat16 [32768, 768], P(('dp', 'expert'))
- grad_tokens: float32 [32768, 768], P(('dp', 'expert'))
- grad_prev: float32 [32768, 12], P(('dp', 'expert'))
- grad_norm_attn: float32 [768], replicated
- grad_query: float32 [768, 768], replicated
- grad_key: float32 [768, 768], replicated
- grad_value: float32 [768, 768], replicated
- grad_out_proj: float32 [768, 768], replicated
- grad_norm_ffn: float32 [768], replicated
- grad_router: float32 [768, 12], replicated
- grad_const_w: float32 [2, 768, 2], replicated
- grad_const_v: float32 [2, 768], replicated
- grad_w_gate: float32 [8, 768, 2048], P('expert', None, 'dp')
- grad_w_up: float32 [8, 768, 2048], P('expert', None, 'dp')
- grad_w_down: float32 [8, 2048, 768], P('expert', 'dp')
Inputs may be any that keep to these rules, and one draw needn't show every extreme that they name: `routes`: each row names two different experts; every expert is named somewhere. `priority`: in each aligned block of 1024 rows the values are a permutation of 0 to 1023.
All inputs are finite; a program needn't handle non-finite values.
Results may differ from a plain program's by a relative error of at most 0.015.
Values may be sent and summed in bfloat16 or wider, within the bound.
A program may use at most 384 MiB of HBM per device.

v0:
```python
import jax
import jax.numpy as jnp
from jax import lax
from jax.sharding import PartitionSpec as P

HEADS = 12
FFN_EXP = 8
PROMPT = 2048
NCONT = 8
CONT = 256


epsilon = 1e-06
neg_fill = -1000000000.0


def rms_scale(values_in):
    return lax.rsqrt(jnp.mean(values_in * values_in, axis=-1, keepdims=True) + epsilon)


def rotate(values_in, positions, turn_sign):
    head_width = values_in.shape[-1]
    half_width = head_width // 2
    frequency = jnp.exp(
        -jnp.log(10000.0) * jnp.arange(half_width, dtype=jnp.float32) * 2.0 / head_width
    )
    angle = positions.astype(jnp.float32)[:, None] * frequency[None, :]
    cosine = jnp.cos(angle)[:, None, :]
    sine_part = turn_sign * jnp.sin(angle)[:, None, :]
    first_half = values_in[..., :half_width]
    second_half = values_in[..., half_width:]
    return jnp.concatenate(
        [
            first_half * cosine - second_half * sine_part,
            second_half * cosine + first_half * sine_part,
        ],
        axis=-1,
    )


def block_layout(device, row_count, prompt_dev, cont_dev):
    row_index = jnp.arange(row_count, dtype=jnp.int32)
    offset = jnp.maximum(row_index - prompt_dev, 0)
    in_prompt = row_index < prompt_dev
    positions = jnp.where(in_prompt, device * prompt_dev + row_index, PROMPT + offset % CONT)
    segments = jnp.where(in_prompt, 0, 1 + device * cont_dev + offset // CONT)
    return (positions, segments)


def slot_table(route_ids, priority, expert_count, capacity):
    row_count, pick_count = route_ids.shape
    earlier = (priority[None, :] < priority[:, None]).astype(jnp.bfloat16)
    expert_ids = jnp.arange(expert_count, dtype=jnp.int32)
    picked = route_ids[:, :, None] == expert_ids[None, None, :]
    assigned = jnp.any(picked, axis=1).astype(jnp.bfloat16)
    rank_table = jnp.dot(earlier, assigned, preferred_element_type=jnp.float32)
    pick_rank = jnp.sum(jnp.where(picked, rank_table[:, None, :], 0.0), axis=-1).astype(jnp.int32)
    kept_pick = (route_ids < expert_count) & (pick_rank < capacity)
    slot_index = jnp.where(kept_pick, route_ids * capacity + pick_rank, -1)
    slot_ids = jnp.arange(expert_count * capacity, dtype=jnp.int32)
    matched = slot_index.reshape(-1)[None, :] == slot_ids[:, None]
    flat_index = jnp.arange(row_count * pick_count, dtype=jnp.int32)
    owner_pick = jnp.sum(jnp.where(matched, flat_index[None, :], 0), axis=1)
    filled = jnp.any(matched, axis=1)
    return (slot_index, kept_pick, owner_pick, filled)


def local(
    tokens,
    prev_logits,
    routes,
    priority,
    norm_attn,
    w_query,
    w_key,
    w_value,
    w_out,
    norm_ffn,
    router,
    const_w,
    const_v,
    w_gate,
    w_up,
    w_down,
    cotangent,
):
    row_count, width = tokens.shape
    head_count = HEADS
    head_width = width // head_count
    expert_devices = lax.axis_size("expert")
    device = lax.axis_index("expert")
    prompt_dev = PROMPT // expert_devices
    cont_dev = NCONT // expert_devices
    expert_total = prev_logits.shape[1]
    local_experts = w_gate.shape[0]
    pick_count = routes.shape[1]
    capacity = 9 * row_count * pick_count // (8 * expert_total)
    score_scale = head_width ** (-0.5)
    block_rows = min(512, row_count)
    block_count = row_count // block_rows
    key_total = PROMPT + row_count - prompt_dev
    tokens_f = tokens.astype(jnp.float32)
    inverse_one = rms_scale(tokens_f)
    normed_one = (tokens_f * inverse_one * norm_attn).astype(jnp.bfloat16)
    query_proj = jnp.dot(normed_one, w_query, preferred_element_type=jnp.float32).reshape(
        row_count, head_count, head_width
    )
    key_proj = jnp.dot(normed_one, w_key, preferred_element_type=jnp.float32).reshape(
        row_count, head_count, head_width
    )
    value_proj = jnp.dot(normed_one, w_value, preferred_element_type=jnp.float32)
    positions, segments = block_layout(device, row_count, prompt_dev, cont_dev)
    queries = rotate(query_proj, positions, 1.0).astype(jnp.bfloat16)
    key_local = rotate(key_proj, positions, 1.0).astype(jnp.bfloat16).reshape(row_count, width)
    value_local = value_proj.astype(jnp.bfloat16)
    prompt_keys, prompt_values = (
        lax.all_gather(key_local[:prompt_dev], "expert", axis=0, tiled=True),
        lax.all_gather(value_local[:prompt_dev], "expert", axis=0, tiled=True),
    )
    key_rows = jnp.concatenate([prompt_keys, key_local[prompt_dev:]], axis=0).reshape(
        key_total, head_count, head_width
    )
    value_rows = jnp.concatenate([prompt_values, value_local[prompt_dev:]], axis=0).reshape(
        key_total, head_count, head_width
    )
    key_pos = jnp.concatenate([jnp.arange(PROMPT, dtype=jnp.int32), positions[prompt_dev:]])
    key_seg = jnp.concatenate([jnp.zeros((PROMPT,), jnp.int32), segments[prompt_dev:]])

    def masked_scores(query_block, query_pos, query_seg):
        raw_scores = jnp.einsum(
            "qhd,khd->hqk", query_block, key_rows, preferred_element_type=jnp.float32
        )
        allowed = ((key_seg[None, :] == 0) | (key_seg[None, :] == query_seg[:, None])) & (
            key_pos[None, :] <= query_pos[:, None]
        )
        return (jnp.where(allowed[None], raw_scores * score_scale, neg_fill), allowed)

    def attend_block(inputs):
        query_block, query_pos, query_seg = inputs
        scores, allowed = masked_scores(query_block, query_pos, query_seg)
        row_max = jnp.max(scores, axis=-1, keepdims=True)
        shifted = jnp.exp(scores - row_max)
        row_total = jnp.sum(shifted, axis=-1, keepdims=True)
        probs_low = (shifted / row_total).astype(jnp.bfloat16)
        attended = jnp.einsum(
            "hqk,khd->qhd", probs_low, value_rows, preferred_element_type=jnp.float32
        )
        return (attended, (row_max + jnp.log(row_total))[..., 0])

    query_blocks = queries.reshape(block_count, block_rows, head_count, head_width)
    pos_blocks = positions.reshape(block_count, block_rows)
    seg_blocks = segments.reshape(block_count, block_rows)
    attended, log_totals = lax.map(attend_block, (query_blocks, pos_blocks, seg_blocks))
    attn_low = attended.reshape(row_count, width).astype(jnp.bfloat16)
    residual_two = tokens_f + jnp.dot(attn_low, w_out, preferred_element_type=jnp.float32)
    inverse_two = rms_scale(residual_two)
    normed_two = (residual_two * inverse_two * norm_ffn).astype(jnp.bfloat16)
    normed_wide = normed_two.astype(jnp.float32)
    logits = jnp.dot(normed_two, router, preferred_element_type=jnp.float32) + prev_logits
    pick_hot = (
        routes[:, :, None] == jnp.arange(expert_total, dtype=jnp.int32)[None, None, :]
    ).astype(jnp.float32)
    picked_logits = jnp.sum(logits[:, None, :] * pick_hot, axis=-1)
    gate_probs = jax.nn.softmax(picked_logits, axis=-1)
    const_mix = jnp.einsum("td,cdk->tck", normed_two, const_w, preferred_element_type=jnp.float32)
    mix_weight = jax.nn.softmax(const_mix, axis=-1)
    const_out = (
        mix_weight[..., 0:1] * normed_wide[:, None, :] + mix_weight[..., 1:2] * const_v[None]
    )
    const_ids = FFN_EXP + 2 + jnp.arange(const_v.shape[0], dtype=jnp.int32)
    const_pick = (routes[:, :, None] == const_ids[None, None, :]).astype(jnp.float32)
    copy_pick = (routes == FFN_EXP + 1).astype(jnp.float32)
    slot_index, kept_pick, owner_pick, filled = slot_table(routes, priority, FFN_EXP, capacity)
    slot_safe = jnp.maximum(slot_index, 0)
    send_rows = jnp.where(
        filled[:, None],
        jnp.take(normed_two, owner_pick // pick_count, axis=0),
        jnp.zeros((), jnp.bfloat16),
    )
    send_rows = send_rows.reshape(expert_devices, local_experts, capacity, width)
    arrived = lax.all_to_all(send_rows, "expert", split_axis=0, concat_axis=0, tiled=True)
    gate_pre = jnp.einsum("secd,edf->secf", arrived, w_gate, preferred_element_type=jnp.float32)
    up_pre = jnp.einsum("secd,edf->secf", arrived, w_up, preferred_element_type=jnp.float32)
    hidden = (gate_pre * jax.nn.sigmoid(gate_pre) * up_pre).astype(jnp.bfloat16)
    produced = jnp.einsum(
        "secf,efd->secd", hidden, w_down, preferred_element_type=jnp.float32
    ).astype(jnp.bfloat16)
    expert_results = (produced, arrived, gate_pre, up_pre)
    returned = lax.all_to_all(
        expert_results[0], "expert", split_axis=0, concat_axis=0, tiled=True
    ).reshape(FFN_EXP * capacity, width)
    arrived = expert_results[1]
    ffn_branch = jnp.where(
        kept_pick[:, :, None], jnp.take(returned, slot_safe, axis=0), jnp.zeros((), jnp.bfloat16)
    ).astype(jnp.float32)
    branch = (
        ffn_branch
        + copy_pick[:, :, None] * normed_wide[:, None, :]
        + jnp.sum(const_pick[:, :, :, None] * const_out[:, None, :, :], axis=2)
    )
    residual_three = residual_two + jnp.sum(gate_probs[:, :, None] * branch, axis=1)
    mixed_out = residual_three.astype(jnp.bfloat16)
    upstream = cotangent.astype(jnp.float32)
    grad_gate = jnp.sum(upstream[:, None, :] * branch, axis=-1)
    grad_pick = gate_probs * (grad_gate - jnp.sum(gate_probs * grad_gate, axis=-1, keepdims=True))
    grad_prev = jnp.sum(grad_pick[:, :, None] * pick_hot, axis=1)
    logit_low = grad_prev.astype(jnp.bfloat16)
    grad_router = jnp.dot(normed_two.T, logit_low, preferred_element_type=jnp.float32)
    grad_normed = jnp.dot(logit_low, router.T, preferred_element_type=jnp.float32)
    weighted = gate_probs[:, :, None] * upstream[:, None, :]
    grad_normed = grad_normed + jnp.sum(copy_pick[:, :, None] * weighted, axis=1)
    const_weight = jnp.sum(gate_probs[:, :, None] * const_pick, axis=1)
    grad_const = const_weight[:, :, None] * upstream[:, None, :]
    grad_first = jnp.sum(grad_const * normed_wide[:, None, :], axis=-1)
    grad_second = jnp.sum(grad_const * const_v[None], axis=-1)
    grad_normed = grad_normed + jnp.sum(mix_weight[..., 0:1] * grad_const, axis=1)
    grad_const_v = jnp.sum(mix_weight[..., 1:2] * grad_const, axis=0)
    grad_mix = jnp.stack([grad_first, grad_second], axis=-1)
    mix_low = (
        mix_weight * (grad_mix - jnp.sum(mix_weight * grad_mix, axis=-1, keepdims=True))
    ).astype(jnp.bfloat16)
    grad_const_w = jnp.einsum(
        "td,tck->cdk", normed_two, mix_low, preferred_element_type=jnp.float32
    )
    grad_normed = grad_normed + jnp.einsum(
        "tck,cdk->td", mix_low, const_w, preferred_element_type=jnp.float32
    )
    grad_send = jnp.where(
        filled[:, None],
        jnp.take(weighted.reshape(row_count * pick_count, width), owner_pick, axis=0),
        0.0,
    )
    grad_send = grad_send.astype(jnp.bfloat16).reshape(
        expert_devices, local_experts, capacity, width
    )
    grad_arrived = lax.all_to_all(grad_send, "expert", split_axis=0, concat_axis=0, tiled=True)
    gate_pre = expert_results[2]
    up_pre = expert_results[3]
    sigmoid_gate = jax.nn.sigmoid(gate_pre)
    activated = gate_pre * sigmoid_gate
    hidden = (activated * up_pre).astype(jnp.bfloat16)
    down_local = jnp.einsum(
        "secf,secd->efd", hidden, grad_arrived, preferred_element_type=jnp.float32
    )
    grad_hidden = jnp.einsum(
        "secd,efd->secf", grad_arrived, w_down, preferred_element_type=jnp.float32
    )
    up_low = (grad_hidden * activated).astype(jnp.bfloat16)
    gate_low = (
        grad_hidden * up_pre * sigmoid_gate * (1.0 + gate_pre * (1.0 - sigmoid_gate))
    ).astype(jnp.bfloat16)
    gate_local = jnp.einsum("secd,secf->edf", arrived, gate_low, preferred_element_type=jnp.float32)
    up_local = jnp.einsum("secd,secf->edf", arrived, up_low, preferred_element_type=jnp.float32)
    grad_rows = jnp.einsum("secf,edf->secd", gate_low, w_gate, preferred_element_type=jnp.float32)
    grad_rows = (
        grad_rows + jnp.einsum("secf,edf->secd", up_low, w_up, preferred_element_type=jnp.float32)
    ).astype(jnp.bfloat16)
    rows_back = lax.all_to_all(
        grad_rows, "expert", split_axis=0, concat_axis=0, tiled=True
    ).reshape(FFN_EXP * capacity, width)
    grad_normed = grad_normed + jnp.sum(
        jnp.where(
            kept_pick[:, :, None],
            jnp.take(rows_back, slot_safe, axis=0),
            jnp.zeros((), jnp.bfloat16),
        ).astype(jnp.float32),
        axis=1,
    )
    grad_w_gate, grad_w_up, grad_w_down = (
        lax.psum_scatter(gate_local, "dp", scatter_dimension=2, tiled=True),
        lax.psum_scatter(up_local, "dp", scatter_dimension=2, tiled=True),
        lax.psum_scatter(down_local, "dp", scatter_dimension=1, tiled=True),
    )
    scaled_two = grad_normed * norm_ffn
    grad_norm_ffn = jnp.sum(grad_normed * residual_two * inverse_two, axis=0)
    grad_two = upstream + inverse_two * (
        scaled_two
        - residual_two
        * inverse_two
        * inverse_two
        * jnp.mean(scaled_two * residual_two, axis=-1, keepdims=True)
    )
    attn_grad_low = grad_two.astype(jnp.bfloat16)
    grad_out_proj = jnp.dot(attn_low.T, attn_grad_low, preferred_element_type=jnp.float32)
    out_grad_low = jnp.dot(attn_grad_low, w_out.T, preferred_element_type=jnp.float32).astype(
        jnp.bfloat16
    )
    out_grad_low = out_grad_low.reshape(block_count, block_rows, head_count, head_width)

    def backward_block(running, inputs):
        key_sum, value_sum = running
        query_block, query_pos, query_seg, grad_block, log_block = inputs
        scores, allowed = masked_scores(query_block, query_pos, query_seg)
        prob_rows = jnp.where(allowed[None], jnp.exp(scores - log_block[..., None]), 0.0)
        grad_probs = jnp.einsum(
            "qhd,khd->hqk", grad_block, value_rows, preferred_element_type=jnp.float32
        )
        row_dot = jnp.sum(prob_rows * grad_probs, axis=-1, keepdims=True)
        score_low = (prob_rows * (grad_probs - row_dot) * score_scale).astype(jnp.bfloat16)
        query_grad = jnp.einsum(
            "hqk,khd->qhd", score_low, key_rows, preferred_element_type=jnp.float32
        )
        key_sum = key_sum + jnp.einsum(
            "hqk,qhd->khd", score_low, query_block, preferred_element_type=jnp.float32
        )
        value_sum = value_sum + jnp.einsum(
            "hqk,qhd->khd",
            prob_rows.astype(jnp.bfloat16),
            grad_block,
            preferred_element_type=jnp.float32,
        )
        return ((key_sum, value_sum), query_grad)

    zero_keys = jnp.zeros((key_total, head_count, head_width), jnp.float32)
    (key_sum, value_sum), query_grads = lax.scan(
        backward_block,
        (zero_keys, zero_keys),
        (query_blocks, pos_blocks, seg_blocks, out_grad_low, log_totals),
    )
    prompt_kgrad, prompt_vgrad = (
        lax.psum_scatter(
            key_sum[:PROMPT].reshape(PROMPT, width), "expert", scatter_dimension=0, tiled=True
        ),
        lax.psum_scatter(
            value_sum[:PROMPT].reshape(PROMPT, width), "expert", scatter_dimension=0, tiled=True
        ),
    )
    key_grad = jnp.concatenate([prompt_kgrad, key_sum[PROMPT:].reshape(-1, width)], axis=0).reshape(
        row_count, head_count, head_width
    )
    value_grad = jnp.concatenate([prompt_vgrad, value_sum[PROMPT:].reshape(-1, width)], axis=0)
    query_low = (
        rotate(query_grads.reshape(row_count, head_count, head_width), positions, -1.0)
        .reshape(row_count, width)
        .astype(jnp.bfloat16)
    )
    key_low = rotate(key_grad, positions, -1.0).reshape(row_count, width).astype(jnp.bfloat16)
    value_low = value_grad.astype(jnp.bfloat16)
    grad_query = jnp.dot(normed_one.T, query_low, preferred_element_type=jnp.float32)
    grad_key = jnp.dot(normed_one.T, key_low, preferred_element_type=jnp.float32)
    grad_value = jnp.dot(normed_one.T, value_low, preferred_element_type=jnp.float32)
    grad_one = jnp.dot(query_low, w_query.T, preferred_element_type=jnp.float32)
    grad_one = grad_one + jnp.dot(key_low, w_key.T, preferred_element_type=jnp.float32)
    grad_one = grad_one + jnp.dot(value_low, w_value.T, preferred_element_type=jnp.float32)
    scaled_one = grad_one * norm_attn
    grad_norm_attn = jnp.sum(grad_one * tokens_f * inverse_one, axis=0)
    grad_tokens = grad_two + inverse_one * (
        scaled_one
        - tokens_f
        * inverse_one
        * inverse_one
        * jnp.mean(scaled_one * tokens_f, axis=-1, keepdims=True)
    )
    shared = lax.psum(
        (
            grad_norm_attn,
            grad_query,
            grad_key,
            grad_value,
            grad_out_proj,
            grad_norm_ffn,
            grad_router,
            grad_const_w,
            grad_const_v,
        ),
        ("dp", "expert"),
    )
    return (
        mixed_out,
        grad_tokens,
        grad_prev,
        shared[0],
        shared[1],
        shared[2],
        shared[3],
        shared[4],
        shared[5],
        shared[6],
        shared[7],
        shared[8],
        grad_w_gate,
        grad_w_up,
        grad_w_down,
    )


def solution(mesh):
    in_specs = (
        P(("dp", "expert"), None),
        P(("dp", "expert"), None),
        P(("dp", "expert"), None),
        P(("dp", "expert")),
        P(),
        P(),
        P(),
        P(),
        P(),
        P(),
        P(),
        P(),
        P(),
        P("expert", None, None),
        P("expert", None, None),
        P("expert", None, None),
        P(("dp", "expert"), None),
    )
    out_specs = (
        P(("dp", "expert"), None),
        P(("dp", "expert"), None),
        P(("dp", "expert"), None),
        P(),
        P(),
        P(),
        P(),
        P(),
        P(),
        P(),
        P(),
        P(),
        P("expert", None, "dp"),
        P("expert", None, "dp"),
        P("expert", "dp", None),
    )
    return jax.shard_map(local, mesh=mesh, in_specs=in_specs, out_specs=out_specs, check_vma=False)
```

profile of v0, /device:TPU:9, one launch (start us, length us, event | category | flops | bytes accessed | tf_op | source)
XLA Modules:
  0.0 2029.5 jit_solution(6097414833049952933)
XLA Ops:
  79.5 152.5 %while.27 = (s32[]{:T(128)}, bf16[2,512,12,64]{1,3,2,0:T(8,128)(2,1)}, f32[2,12,512]{2,1,0:T(8,128)}, s32[2560]{0:T(1024)S(1)}, s32[2,512]{1,0:T(2,128)S(1)}, /*...) while((s32[]{:T(128)}, ...), condition=%wide.region_4.5_spmd, body=%wide.region_1.4_spmd.sunk | while | flops 4220514816 | bytes 204463248 | solution.py:153
  81.4 25.9 %fusion.225 = (f32[12,512]{1,0:T(8,128)S(1)}, f32[12,512,2560]{2,1,0:T(8,128)}) fusion(pred[512,2560]{1,0:T(8,128)(4,1)S(1)} %compare_and_fusion.7, bf16[2560,12,64]{0,2,1:T(8,128)(2,1)} %get-tuple-element.608, bf16[2,512,12,64]{1,3,2,0:T(8,128)(2,1)} %get-tuple-element.607, s32[]{:T(128)S(6)} %copy.288), kind=kOutput, calls=%fused_computation.7.clone.1 | convolution fusion | flops 2060445696 | bytes 68968448 | tf_op jit(solution)/shard_map/while/body/eval_jaxpr/qhd,khd->hqk/dot_general | solution.py:130
  128.0 27.0 %bitcast_dynamic-update-slice_fusion.6 = bf16[2,512,12,64]{1,3,2,0:T(8,128)(2,1)} fusion(bf16[2,512,12,64]{1,3,2,0:T(8,128)(2,1)} %get-tuple-element.590, s32[]{:T(128)S(6)} %copy.288, bf16[2560,12,64]{0,2,1:T(8,128)(2,1)} %get-tuple-element.609, f32[12,512,2560]{2,1,0:T(8,128)} %get-tuple-element.561, f32[12,512]{1,0:T(8,128)S(1)} %fusion.226, ...), kind=kOutput, calls=%fused_computation.11.clone.1 | convolution fusion | flops 2091909120 | bytes 69779456 | tf_op jit(solution)/shard_map/while/body/eval_jaxpr/hqk,khd->qhd/dot_general | solution.py:145
  157.5 25.9 %fusion.225 = (f32[12,512]{1,0:T(8,128)S(1)}, f32[12,512,2560]{2,1,0:T(8,128)}) fusion(pred[512,2560]{1,0:T(8,128)(4,1)S(1)} %compare_and_fusion.7, bf16[2560,12,64]{0,2,1:T(8,128)(2,1)} %get-tuple-element.608, bf16[2,512,12,64]{1,3,2,0:T(8,128)(2,1)} %get-tuple-element.607, s32[]{:T(128)S(6)} %copy.288), kind=kOutput, calls=%fused_computation.7.clone.1 | convolution fusion | flops 2060445696 | bytes 68968448 | tf_op jit(solution)/shard_map/while/body/eval_jaxpr/qhd,khd->hqk/dot_general | solution.py:130
  204.0 27.0 %bitcast_dynamic-update-slice_fusion.6 = bf16[2,512,12,64]{1,3,2,0:T(8,128)(2,1)} fusion(bf16[2,512,12,64]{1,3,2,0:T(8,128)(2,1)} %get-tuple-element.590, s32[]{:T(128)S(6)} %copy.288, bf16[2560,12,64]{0,2,1:T(8,128)(2,1)} %get-tuple-element.609, f32[12,512,2560]{2,1,0:T(8,128)} %get-tuple-element.561, f32[12,512]{1,0:T(8,128)S(1)} %fusion.226, ...), kind=kOutput, calls=%fused_computation.11.clone.1 | convolution fusion | flops 2091909120 | bytes 69779456 | tf_op jit(solution)/shard_map/while/body/eval_jaxpr/hqk,khd->qhd/dot_general | solution.py:145
  515.3 538.5 %while.28 = (s32[]{:T(128)}, f32[2560,12,64]{0,2,1:T(8,128)}, f32[2560,12,64]{0,2,1:T(8,128)}, f32[2,512,12,64]{1,0,3,2:T(2,128)}, bf16[2,512,12,64]{1,3,2,0:T(8...) while((s32[]{:T(128)}, f32[2560,12,64]{0,2,1:T(8,128)}, ...), condition=%wide.region_30.32_spmd.clone, body=%wide.region_28.31_spmd.clone.sunk | while | flops 10315386880 | bytes 638966976 | solution.py:315
  517.3 28.5 %exponential_select_fusion.2 = f32[12,512,2560]{2,1,0:T(8,128)} fusion(f32[12,512]{1,0:T(8,128)S(1)} %dynamic-slice_bitcast_fusion.2, pred[512,2560]{1,0:T(8,128)(4,1)S(1)} %compare_and_fusion.8, bf16[2560,12,64]{0,2,1:T(8,128)(2,1)} %get-tuple-element.650, bf16[2,512,12,64]{1,3,2,0:T(8,128)(2,1)} %get-tuple-element.645, s32[]{:T(128)S(6)} %copy.298), kind=kOutput, calls=%fused_computation.26.clone.1 | convolution fusion | flops 2076180480 | bytes 68968448 | tf_op jit(solution)/shard_map/while/body/eval_jaxpr/qhd,khd->hqk/dot_general | solution.py:130
  545.8 24.6 %bitcast_add_fusion.6 = f32[2560,12,64]{0,2,1:T(8,128)} fusion(f32[2560,12,64]{0,2,1:T(8,128)} %get-tuple-element.628, f32[12,512,2560]{2,1,0:T(8,128)} %exponential_select_fusion.2, pred[]{:T(512)S(6)} %compare.43, bf16[2,512,12,64]{1,3,2,0:T(8,128)(2,1)} %get-tuple-element.652, s32[]{:T(128)S(6)} %copy.298), kind=kOutput, calls=%fused_computation.31.clone.1 | convolution fusion | flops 2032926720 | bytes 79429640 | tf_op jit(solution)/shard_map/while/body/eval_jaxpr/hqk,qhd->khd/dot_general | solution.py:306
  593.7 78.2 %fusion.238 = f32[1,512,12,64]{1,3,2,0:T(8,128)} fusion(bf16[2560,12,64]{0,2,1:T(8,128)(2,1)} %get-tuple-element.650, f32[12,512,2560]{2,1,0:T(8,128)} %exponential_select_fusion.2, f32[12,512,2560]{2,1,0:T(8,128)} %fusion.237), kind=kOutput, calls=%fused_computation.34.clone.1 | convolution fusion | flops 2091917824 | bytes 131334144 | tf_op jit(solution)/shard_map/while/body/eval_jaxpr/hqk,khd->qhd/dot_general | solution.py:300
  671.9 78.3 %bitcast_add_fusion.5 = f32[2560,12,64]{0,2,1:T(8,128)} fusion(f32[2560,12,64]{0,2,1:T(8,128)} %get-tuple-element.627, f32[12,512,2560]{2,1,0:T(8,128)} %exponential_select_fusion.2, f32[12,512,2560]{2,1,0:T(8,128)} %fusion.237, pred[]{:T(512)S(6)} %compare.43, bf16[2,512,12,64]{1,3,2,0:T(8,128)(2,1)} %get-tuple-element.645, s32[]{:T(128)S(6)} %copy.298), kind=kOutput, calls=%fused_computation.32.clone.2 | convolution fusion | flops 2095849984 | bytes 268173312 | tf_op jit(solution)/shard_map/while/body/eval_jaxpr/hqk,qhd->khd/dot_general | solution.py:303
  753.2 28.8 %dynamic_update_slice.19 = f32[2,512,12,64]{1,0,3,2:T(2,128)} dynamic-update-slice(f32[2,512,12,64]{1,0,3,2:T(2,128)} %get-tuple-element.629, f32[1,512,12,64]{1,0,3,2:T(1,128)S(1)} %copy.280, s32[]{:T(128)S(6)} %copy.298, s32[]{:T(128)} %constant.168.clone.1..sunk, s32[]{:T(128)} %constant.168.clone.1..sunk, s32[]{:T(128)} %constant.168.clone.1..sunk) | dynamic-update-slice | bytes 3145732 | tf_op jit(solution)/shard_map/while/body/jit(dynamic_update_index_in_dim)/dynamic_update_slice | solution.py:153
  784.0 28.5 %exponential_select_fusion.2 = f32[12,512,2560]{2,1,0:T(8,128)} fusion(f32[12,512]{1,0:T(8,128)S(1)} %dynamic-slice_bitcast_fusion.2, pred[512,2560]{1,0:T(8,128)(4,1)S(1)} %compare_and_fusion.8, bf16[2560,12,64]{0,2,1:T(8,128)(2,1)} %get-tuple-element.650, bf16[2,512,12,64]{1,3,2,0:T(8,128)(2,1)} %get-tuple-element.645, s32[]{:T(128)S(6)} %copy.298), kind=kOutput, calls=%fused_computation.26.clone.1 | convolution fusion | flops 2076180480 | bytes 68968448 | tf_op jit(solution)/shard_map/while/body/eval_jaxpr/qhd,khd->hqk/dot_general | solution.py:130
  812.5 26.8 %bitcast_add_fusion.6 = f32[2560,12,64]{0,2,1:T(8,128)} fusion(f32[2560,12,64]{0,2,1:T(8,128)} %get-tuple-element.628, f32[12,512,2560]{2,1,0:T(8,128)} %exponential_select_fusion.2, pred[]{:T(512)S(6)} %compare.43, bf16[2,512,12,64]{1,3,2,0:T(8,128)(2,1)} %get-tuple-element.652, s32[]{:T(128)S(6)} %copy.298), kind=kOutput, calls=%fused_computation.31.clone.1 | convolution fusion | flops 2032926720 | bytes 79429640 | tf_op jit(solution)/shard_map/while/body/eval_jaxpr/hqk,qhd->khd/dot_general | solution.py:306
  839.3 23.3 %fusion.237 = f32[12,512,2560]{2,1,0:T(8,128)} fusion(bf16[2560,12,64]{0,2,1:T(8,128)(2,1)S(1)} %copy-done.1, bf16[2,512,12,64]{1,3,2,0:T(8,128)(2,1)} %get-tuple-element.652, s32[]{:T(128)S(6)} %copy.298), kind=kOutput, calls=%fused_computation.36.clone.1 | convolution fusion | flops 2013265920 | bytes 67633152 | tf_op jit(solution)/shard_map/while/body/eval_jaxpr/qhd,khd->hqk/dot_general | solution.py:295
  862.7 78.2 %fusion.238 = f32[1,512,12,64]{1,3,2,0:T(8,128)} fusion(bf16[2560,12,64]{0,2,1:T(8,128)(2,1)} %get-tuple-element.650, f32[12,512,2560]{2,1,0:T(8,128)} %exponential_select_fusion.2, f32[12,512,2560]{2,1,0:T(8,128)} %fusion.237), kind=kOutput, calls=%fused_computation.34.clone.1 | convolution fusion | flops 2091917824 | bytes 131334144 | tf_op jit(solution)/shard_map/while/body/eval_jaxpr/hqk,khd->qhd/dot_general | solution.py:300
  940.8 80.7 %bitcast_add_fusion.5 = f32[2560,12,64]{0,2,1:T(8,128)} fusion(f32[2560,12,64]{0,2,1:T(8,128)} %get-tuple-element.627, f32[12,512,2560]{2,1,0:T(8,128)} %exponential_select_fusion.2, f32[12,512,2560]{2,1,0:T(8,128)} %fusion.237, pred[]{:T(512)S(6)} %compare.43, bf16[2,512,12,64]{1,3,2,0:T(8,128)(2,1)} %get-tuple-element.645, s32[]{:T(128)S(6)} %copy.298), kind=kOutput, calls=%fused_computation.32.clone.2 | convolution fusion | flops 2095849984 | bytes 268173312 | tf_op jit(solution)/shard_map/while/body/eval_jaxpr/hqk,qhd->khd/dot_general | solution.py:303
  1024.6 28.8 %dynamic_update_slice.19 = f32[2,512,12,64]{1,0,3,2:T(2,128)} dynamic-update-slice(f32[2,512,12,64]{1,0,3,2:T(2,128)} %get-tuple-element.629, f32[1,512,12,64]{1,0,3,2:T(1,128)S(1)} %copy.280, s32[]{:T(128)S(6)} %copy.298, s32[]{:T(128)} %constant.168.clone.1..sunk, s32[]{:T(128)} %constant.168.clone.1..sunk, s32[]{:T(128)} %constant.168.clone.1..sunk) | dynamic-update-slice | bytes 3145732 | tf_op jit(solution)/shard_map/while/body/jit(dynamic_update_index_in_dim)/dynamic_update_slice | solution.py:153
  1081.1 38.4 %reduce-scatter.6.cloned.1.call-done = f32[512,768]{0,1:T(8,128)} async-done(((f32[2048,768]{0,1:T(8,128)}), f32[512,768]{0,1:T(8,128)}) %reduce-scatter.6.cloned.1.call-update) | async-done | bytes 1572880 | tf_op jit(solution)/shard_map/reduce_scatter | solution.py:321
  1130.7 49.8 %reduce-scatter.8.cloned.1.call-done = f32[512,768]{0,1:T(8,128)} async-done(((f32[2048,768]{0,1:T(8,128)}), f32[512,768]{0,1:T(8,128)}) %reduce-scatter.8.cloned.1.call-update) | async-done | bytes 1572880 | tf_op jit(solution)/shard_map/reduce_scatter | solution.py:324
  1237.2 41.0 %all-reduce.1 = (f32[768]{0:T(1024)}, f32[768]{0:T(1024)}, f32[768,12]{0,1:T(8,128)}, f32[2,768,2]{1,2,0:T(2,128)}, f32[2,768]{1,0:T(2,128)}) all-reduce(f32[768]{0:T(1024)S(1)} %get-tuple-element.312, f32[768]{0:T(1024)S(1)} %copy-done.88, f32[768,12]{0,1:T(8,128)S(1)} %copy-done.43, ...), channel_id=1, replica_groups=mesh['dp'=8,'expert'=4] {'dp','expert'}, use_global_device_ids=true, to_apply=%region_35.37 | all-reduce | flops 15360 | bytes 122880 | tf_op jit(solution)/shard_map/psum | solution.py:354
  1278.2 101.5 %all-reduce.5.cloned.1.call-done = (f32[768,768]{1,0:T(8,128)}, f32[768,768]{1,0:T(8,128)}, f32[768,768]{1,0:T(8,128)}, f32[768,768]{1,0:T(8,128)}) async-done(((f32[768,768]{1,0:T(8,128)}, f32[768,768]{1,0:T(8,128)}, f32[768,768]{1,0:T(8,128)}, f32[768,768]{1,0:T(8,128)}), (f32[768,768]{1,0:T(8,128)}, f32[768,768]{1,0:T(8,128)}, f32[768,768]{1,0:T(8,128)}, ...) | async-done | bytes 9437200 | tf_op jit(solution)/shard_map/psum | solution.py:354
  1379.8 210.1 %reduce-scatter.14.cloned.1.call-done = f32[2,256,768]{2,1,0:T(8,128)} async-done(((f32[2,2048,768]{2,1,0:T(8,128)}), f32[2,256,768]{2,1,0:T(8,128)}) %reduce-scatter.14.cloned.1.call-update) | async-done | bytes 1572880 | tf_op jit(solution)/shard_map/reduce_scatter | solution.py:272
  1589.9 211.4 %reduce-scatter.10.cloned.1.call-done = f32[2,768,256]{2,1,0:T(8,128)} async-done(((f32[2,768,2048]{2,1,0:T(8,128)}), f32[2,768,256]{2,1,0:T(8,128)}) %reduce-scatter.10.cloned.1.call-update) | async-done | bytes 1572880 | tf_op jit(solution)/shard_map/reduce_scatter | solution.py:270
  1801.3 211.5 %reduce-scatter.12.cloned.1.call-done = f32[2,768,256]{2,1,0:T(8,128)} async-done(((f32[2,768,2048]{2,1,0:T(8,128)}), f32[2,768,256]{2,1,0:T(8,128)}) %reduce-scatter.12.cloned.1.call-update) | async-done | bytes 1572880 | tf_op jit(solution)/shard_map/reduce_scatter | solution.py:271
  (385 shorter events, 538.6 us)
Async XLA Ops:
  7.2 58.6 %all-gather.5.cloned.1.call-start = ((), (), s32[]{:S(2)}) async-start(), calls=%async_computation.10 | async-start | bytes 3932160 | tf_op jit(solution)/shard_map/all_gather | solution.py:118
  12.3 63.8 %all-gather.3.cloned.1.call-start = ((), (), s32[]{:S(2)}) async-start(), calls=%async_computation.9 | async-start | bytes 3932160 | tf_op jit(solution)/shard_map/all_gather | solution.py:117
  40.8 9.0 copy-start.9
  255.7 9.1 copy-start.14
  269.9 32.0 %all-to-all-start = ((bf16[4,2,192,768]{3,2,1,0:T(8,128)(2,1)}), bf16[4,2,192,768]{3,2,1,0:T(8,128)(2,1)S(1)}, u32[]{:S(2)}, u32[]{:S(2)}) async-start(bf16[4,2,192,768]{3,2,1,0:T(8,128)(2,1)} %get-tuple-element.413), calls=%async_computation | async-start | bytes 4718592 | tf_op jit(solution)/shard_map/all_to_all | solution.py:181
  278.5 39.7 %copy-start.91 = (s32[2]{0:T(128)}, s32[2]{0:T(128)S(1)}, u32[]{:S(2)}) copy-start(s32[2]{0:T(128)S(1)} %iota_add_fusion) | copy-start | bytes 28
  301.9 16.2 copy-start.22
  301.9 33.3 %all-to-all-start.2 = ((bf16[4,2,192,768]{3,2,1,0:T(8,128)(2,1)}), bf16[4,2,192,768]{3,2,1,0:T(8,128)(2,1)}, u32[]{:S(2)}, u32[]{:S(2)}) async-start(bf16[4,2,192,768]{3,2,1,0:T(8,128)(2,1)} %get-tuple-element.412), calls=%async_computation.2 | async-start | bytes 4718592 | tf_op jit(solution)/shard_map/all_to_all | solution.py:236
  367.8 32.1 %all-to-all-start.1 = ((bf16[4,2,192,768]{3,2,1,0:T(8,128)(2,1)}), bf16[4,2,192,768]{3,2,1,0:T(8,128)(2,1)S(1)}, u32[]{:S(2)}, u32[]{:S(2)}) async-start(bf16[4,2,192,768]{3,2,1,0:T(8,128)(2,1)} %copy.156), calls=%async_computation.1 | async-start | bytes 4718592 | tf_op jit(solution)/shard_map/all_to_all | solution.py:189
  399.9 39.4 %all-to-all-start.3 = ((bf16[4,2,192,768]{3,2,1,0:T(8,128)(2,1)}), bf16[4,2,192,768]{3,2,1,0:T(8,128)(2,1)}, u32[]{:S(2)}, u32[]{:S(2)}) async-start(bf16[4,2,192,768]{3,2,1,0:T(8,128)(2,1)} %copy.177), calls=%async_computation.3 | async-start | bytes 4718592 | tf_op jit(solution)/shard_map/all_to_all | solution.py:258
  405.3 714.3 %reduce-scatter.6.cloned.1.call-start = ((), (), s32[]{:S(2)}) async-start(), calls=%async_computation.11 | async-start | bytes 7864320 | tf_op jit(solution)/shard_map/reduce_scatter | solution.py:321
  480.1 13.8 copy-start.49
  480.5 13.4 copy-start.50
  493.9 7.7 copy-start.57
  493.9 7.7 copy-start.4
  494.0 7.8 copy-start.11
  545.8 24.6 %copy-start.1 = (bf16[2560,12,64]{0,2,1:T(8,128)(2,1)S(1)}, bf16[2560,12,64]{0,2,1:T(8,128)(2,1)}, u32[]{:S(2)}) copy-start(bf16[2560,12,64]{0,2,1:T(8,128)(2,1)} %get-tuple-element.653) | copy-start | bytes 11796484 | tf_op jit(solution)/shard_map/while
  812.5 26.8 %copy-start.1 = (bf16[2560,12,64]{0,2,1:T(8,128)(2,1)S(1)}, bf16[2560,12,64]{0,2,1:T(8,128)(2,1)}, u32[]{:S(2)}) copy-start(bf16[2560,12,64]{0,2,1:T(8,128)(2,1)} %get-tuple-element.653) | copy-start | bytes 11796484 | tf_op jit(solution)/shard_map/while
  1060.0 120.4 %reduce-scatter.8.cloned.1.call-start = ((), (), s32[]{:S(2)}) async-start(), calls=%async_computation.12 | async-start | bytes 7864320 | tf_op jit(solution)/shard_map/reduce_scatter | solution.py:324
  1066.3 313.4 %all-reduce.5.cloned.1.call-start = ((), (), s32[]{:S(2)}) async-start(), calls=%async_computation.16 | async-start | bytes 18874368 | tf_op jit(solution)/shard_map/psum | solution.py:354
  1185.8 404.1 %reduce-scatter.14.cloned.1.call-start = ((), (), s32[]{:S(2)}) async-start(), calls=%async_computation.15 | async-start | bytes 14155776 | tf_op jit(solution)/shard_map/reduce_scatter | solution.py:272
  1196.7 604.7 %reduce-scatter.10.cloned.1.call-start = ((), (), s32[]{:S(2)}) async-start(), calls=%async_computation.13 | async-start | bytes 14155776 | tf_op jit(solution)/shard_map/reduce_scatter | solution.py:270
  1207.8 805.0 %reduce-scatter.12.cloned.1.call-start = ((), (), s32[]{:S(2)}) async-start(), calls=%async_computation.14 | async-start | bytes 14155776 | tf_op jit(solution)/shard_map/reduce_scatter | solution.py:271
  1379.8 636.3 %copy-start.25 = (f32[768,768]{1,0:T(8,128)S(1)}, f32[768,768]{1,0:T(8,128)}, u32[]{:S(2)}) copy-start(f32[768,768]{1,0:T(8,128)} %get-tuple-element.661) | copy-start | bytes 7077892
  (87 other events, 336.2 us)
Sparse Core Ops, SparseCore 0:
  12.4 30.0 all-gather.4
  44.7 28.5 all-gather.2
  1060.2 59.3 reduce-scatter.5
  1122.1 58.3 reduce-scatter.7
  1187.2 192.5 all-reduce.4
  1384.2 205.6 reduce-scatter.13
  1594.5 206.7 reduce-scatter.9
  1805.9 206.8 reduce-scatter.11
where the time goes:
time: 2050 us; the launch traced here: 2030 us
  waiting for transfers between devices  860 us (42%)
  matrix products  728 us (36%)
  local copies, waits for them, and re-layouts  245 us (12%)
  other arithmetic  119 us (6%)
  blocking collectives  41 us (2%)
    reduce_scatter x1, waiting for transfers between devices, local(): lax.psum_scatter(up_local, 'dp', scatter_dimension=2, tiled=True)  211 us
    reduce_scatter x1, waiting for transfers between devices, local(): lax.psum_scatter(gate_local, 'dp', scatter_dimension=2, tiled=True)  211 us
    reduce_scatter x1, waiting for transfers between devices, local(): lax.psum_scatter(down_local, 'dp', scatter_dimension=1, tiled=True)  210 us
    dot_general x2, matrix products, backward_block(): jnp.einsum('hqk,qhd->khd', score_low, query_block, preferred_element_type...  159 us
    dot_general x2, matrix products, backward_block(): jnp.einsum('hqk,khd->qhd', score_low, key_rows, preferred_element_type=jn...  156 us
    dot_general x4, matrix products, masked_scores(): jnp.einsum('qhd,khd->hqk', query_block, key_rows, preferred_element_type=...  109 us
    psum x1, waiting for transfers between devices, local(): lax.psum((grad_norm_attn, grad_query, grad_key, grad_value, grad_out_proj...  102 us
    dynamic_update_slice x4, local copies, waits for them, and re-layouts, local(): lax.map(attend_block, (query_blocks, pos_blocks, seg_blocks))  63.7 us
  transfers between devices with their start and end apart: 12, of which 9 were waited for; matrix products, arithmetic and copies ran while one was open for 11% of the time, Pallas kernels for 0%

commit v1 on v0

v1 whole, which is shorter than its diff:
```python
import functools

import jax
import jax.numpy as jnp
import numpy as np
from jax import lax
from jax.experimental import pallas as pl
from jax.experimental.pallas import tpu as pltpu
from jax.sharding import PartitionSpec as P

HEADS = 12
FFN_EXP = 8
PROMPT = 2048
NCONT = 8
CONT = 256

epsilon = 1e-06
LOG2E = 1.4426950408889634
F32 = jnp.float32
BF = jnp.bfloat16
NN = (((1,), (0,)), ((), ()))
NT = (((1,), (1,)), ((), ()))
VMEM_LIMIT = 56 << 20


def dot(a, b, dims=NN):
    return lax.dot_general(a, b, dims, preferred_element_type=F32)


def params(**kw):
    return pltpu.CompilerParams(vmem_limit_bytes=VMEM_LIMIT, **kw)


def whole(shape):
    return pl.BlockSpec(shape, lambda *_: (0,) * len(shape))


def rms_scale(x):
    return lax.rsqrt(jnp.mean(x * x, axis=-1, keepdims=True) + epsilon)


def angle_tables():
    positions = np.arange(PROMPT + CONT, dtype=np.float32)
    frequency = np.exp(
        np.float32(-np.log(10000.0)) * np.arange(32, dtype=np.float32) * np.float32(2.0) / np.float32(64)
    ).astype(np.float32)
    angle = (positions[:, None] * frequency[None, :]).astype(np.float64)
    cosine = np.cos(angle).astype(np.float32)
    sine = np.sin(angle).astype(np.float32)
    return (
        np.concatenate([cosine] * 4, axis=1),
        np.concatenate([-sine, sine, -sine, sine], axis=1),
    )


def lane_iota(width=128):
    return lax.broadcasted_iota(jnp.int32, (1, width), 1)


def swap_halves(x):
    return jnp.where(lane_iota() % 64 < 32, pltpu.roll(x, 96, 1), pltpu.roll(x, 32, 1))


def project_kernel(e_ref, x_ref, gain_ref, *refs, count):
    weights, (cos_ref, sin_ref), (h_ref, *outs) = refs[:count], refs[count:count + 2], refs[count + 2:]
    x = x_ref[...].astype(F32)
    h = (x * rms_scale(x) * gain_ref[...]).astype(BF)
    h_ref[...] = h
    cosine, sine = cos_ref[...], sin_ref[...]
    for n, (w_ref, out_ref) in enumerate(zip(weights, outs)):
        full = dot(h, w_ref[...])
        if n == count - 1:
            out_ref[...] = full.astype(BF)
            continue
        for i in range(full.shape[1] // 128):
            part = full[:, i * 128:(i + 1) * 128]
            out_ref[:, i * 128:(i + 1) * 128] = (part * cosine + swap_halves(part) * sine).astype(BF)


def project(e, x, gain, weights, cos, sin, own, tile=256):
    rows, width = x.shape
    block = pl.BlockSpec((tile, width), lambda i, *_: (i, 0))
    half = rows // 2 // tile

    def position(i, e_ref):
        if not own:
            return (i, 0)
        return (jnp.where(i < half, e_ref[0] * half + i, PROMPT // tile), 0)

    table = pl.BlockSpec((tile, 128), position)
    return pl.pallas_call(
        functools.partial(project_kernel, count=len(weights)),
        grid_spec=pltpu.PrefetchScalarGridSpec(
            num_scalar_prefetch=1,
            grid=(rows // tile,),
            in_specs=[block, whole((1, width))] + [whole(weights[0].shape)] * len(weights) + [table, table],
            out_specs=[block] * (len(weights) + 1),
        ),
        out_shape=[jax.ShapeDtypeStruct((rows, width), BF)] * (len(weights) + 1),
        compiler_params=params(),
        cost_estimate=pl.CostEstimate(
            flops=2 * rows * width * width * len(weights), bytes_accessed=2 * rows * width * 6, transcendentals=0
        ),
        name="project_own" if own else "project_prompt",
    )(e, x, gain, *weights, cos, sin)


def attn_fwd_kernel(e_ref, q_ref, ko_ref, vo_ref, kp_ref, vp_ref, o_ref, lse_ref, vt_ref, qm_ref, m_ref, acc_ref, *, chunk, tile, scale):
    e = e_ref[0]
    rows = q_ref.shape[0]
    half = rows // 2
    npr = kp_ref.shape[0]
    nchunk = npr // chunk
    lane = lax.broadcasted_iota(jnp.int32, (1, 128), 1)
    low = lane < 64
    c = scale * LOG2E
    zero = jnp.zeros((), BF)
    q = q_ref[...]
    qm_ref[0] = jnp.where(low, q, zero)
    qm_ref[1] = jnp.where(low, zero, q)
    ones = jnp.ones((16, npr + rows), BF)
    for r, n, ref in ((0, npr, vp_ref), (npr, rows, vo_ref)):
        vt = ref[...].T
        vt_ref[0, :64, r:r + n] = vt[:64]
        vt_ref[1, :64, r:r + n] = vt[64:]
    vt_ref[0, 64:, :] = ones
    vt_ref[1, 64:, :] = ones
    tri = lax.broadcasted_iota(jnp.int32, (tile, tile), 0) <= lax.broadcasted_iota(jnp.int32, (tile, tile), 1)

    def first(q0, qn, k, vts):
        for h in range(2):
            s = dot(k, qm_ref[h, q0:q0 + qn, :], NT)
            s = s * c
            s = jnp.where(tri, s, -1e30)
            mx = jnp.max(s, axis=0, keepdims=True)
            p = jnp.exp2(s - mx).astype(BF)
            m_ref[h, 0:1, q0:q0 + qn] = mx
            acc_ref[h, :, q0:q0 + qn] = dot(vts[h], p)

    def step(blocks, k, vts):
        ss = [[dot(k, qm_ref[h, q0:q0 + qn, :], NT) for h in range(2)] for q0, qn in blocks]
        for (q0, qn), sb in zip(blocks, ss):
            for h in range(2):
                s = sb[h] * c
                mx = jnp.max(s, axis=0, keepdims=True)
                m = m_ref[h, 0:1, q0:q0 + qn]
                mn = jnp.maximum(m, mx)
                p = jnp.exp2(s - mn).astype(BF)
                m_ref[h, 0:1, q0:q0 + qn] = mn
                acc_ref[h, :, q0:q0 + qn] = acc_ref[h, :, q0:q0 + qn] * jnp.exp2(m - mn) + dot(vts[h], p)

    for j in range(rows // tile):
        r0 = j * tile
        first(r0, tile, ko_ref[r0:r0 + tile, :], [vt_ref[h, :, npr + r0:npr + r0 + tile] for h in range(2)])
    for j in range(1, half // tile):
        for i in range(j):
            r0 = i * tile
            step([(j * tile, tile)], ko_ref[r0:r0 + tile, :], [vt_ref[h, :, npr + r0:npr + r0 + tile] for h in range(2)])

    def body(ci, blocks):
        r0 = pl.multiple_of(ci * chunk, chunk)
        step(blocks, kp_ref[pl.ds(r0, chunk), :], [vt_ref[h, :, pl.ds(r0, chunk)] for h in range(2)])

    ne = e * half // chunk

    @pl.loop(0, ne)
    def _(ci):
        body(ci, [(0, half), (half, half)])

    @pl.loop(ne, nchunk)
    def _(ci):
        body(ci, [(half, half)])

    outs = []
    for h in range(2):
        l = acc_ref[h, 64:65, :]
        outs.append(acc_ref[h, :64, :] / l)
        lse_ref[0, h:h + 1, :] = m_ref[h, 0:1, :] + jnp.log2(l)
    o_ref[...] = jnp.concatenate(outs, axis=0).T.astype(BF)


def attn_fwd(e, q, ko, vo, kp, vp, *, chunk=512, tile=256):
    rows, width = q.shape
    npr = kp.shape[0]
    pairs = width // 128
    own = pl.BlockSpec((rows, 128), lambda i, *_: (0, i))
    pr = pl.BlockSpec((npr, 128), lambda i, *_: (0, i))
    return pl.pallas_call(
        functools.partial(attn_fwd_kernel, chunk=chunk, tile=tile, scale=0.125),
        grid_spec=pltpu.PrefetchScalarGridSpec(
            num_scalar_prefetch=1, grid=(pairs,),
            in_specs=[own, own, own, pr, pr],
            out_specs=[own, pl.BlockSpec((1, 2, rows), lambda i, *_: (i, 0, 0))],
            scratch_shapes=[pltpu.VMEM((2, 80, npr + rows), BF), pltpu.VMEM((2, rows, 128), BF),
            pltpu.VMEM((2, 8, rows), F32), pltpu.VMEM((2, 80, rows), F32)]),
        out_shape=[jax.ShapeDtypeStruct((rows, width), BF), jax.ShapeDtypeStruct((pairs, 2, rows), F32)],
        compiler_params=params(),
        cost_estimate=pl.CostEstimate(flops=4 * rows * npr * width * 2, bytes_accessed=2 * npr * width * 4, transcendentals=rows * npr * 12),
        name="attn_fwd",
    )(e, q, ko, vo, kp, vp)


def attn_bwd_kernel(e_ref, q_ref, do_ref, o_ref, lse_ref, ko_ref, vo_ref, kp_ref, vp_ref, cos_ref, sin_ref,
               dq_ref, dk_ref, dv_ref,
               kt_ref, dqt_ref, qm_ref, dom_ref, dl_ref, dks_ref, dvs_ref, *, tile, scale):
    e = e_ref[0]
    rows = q_ref.shape[0]
    half = rows // 2
    chunk = half
    npr = kp_ref.shape[0]
    nchunk = npr // chunk
    cont = cos_ref.shape[0] - npr
    lane = lax.broadcasted_iota(jnp.int32, (1, 128), 1)
    low = lane < 64
    c = scale * LOG2E
    zero = jnp.zeros((), BF)
    q = q_ref[...]
    do = do_ref[...]
    qm_ref[0] = jnp.where(low, q, zero)
    qm_ref[1] = jnp.where(low, zero, q)
    dom_ref[0] = jnp.where(low, do, zero)
    dom_ref[1] = jnp.where(low, zero, do)
    prod = (do.astype(F32) * o_ref[...].astype(F32)).T
    dl_ref[0:1, :] = jnp.sum(prod[:64], axis=0, keepdims=True)
    dl_ref[1:2, :] = jnp.sum(prod[64:], axis=0, keepdims=True)
    kt_ref[:, :npr] = kp_ref[...].T
    kt_ref[:, npr:] = ko_ref[...].T
    tri = lax.broadcasted_iota(jnp.int32, (tile, tile), 0) <= lax.broadcasted_iota(jnp.int32, (tile, tile), 1)

    def unrope(x, pos, n):
        first = (lane % 64) < 32
        sw = jnp.where(first, pltpu.roll(x, 96, 1), pltpu.roll(x, 32, 1))
        return x * cos_ref[pl.ds(pos, n), :] - sw * sin_ref[pl.ds(pos, n), :]

    def block(k, v, kt, q0, qn, mask):
        dk = dv = None
        dqs = []
        qs = [qm_ref[h, q0:q0 + qn, :] for h in range(2)]
        dos = [dom_ref[h, q0:q0 + qn, :] for h in range(2)]
        sts = [dot(k, qs[h], NT) for h in range(2)]
        dps = [dot(v, dos[h], NT) for h in range(2)]
        for h in range(2):
            p = jnp.exp2(sts[h] * c - lse_ref[0, h:h + 1, q0:q0 + qn])
            if mask is not None:
                p = jnp.where(mask, p, 0.0)
            ds = (p * (dps[h] - dl_ref[h:h + 1, q0:q0 + qn])).astype(BF)
            dvh = dot(p.astype(BF), dos[h])
            dkh = dot(ds, qs[h])
            dk, dv = (dkh, dvh) if dk is None else (dk + dkh, dv + dvh)
            dqs.append(dot(kt[h * 64:(h + 1) * 64], ds))
        return dk, dv, jnp.concatenate(dqs, axis=0)

    nt = rows // tile
    for i in range(nt):
        r0 = i * tile
        k = ko_ref[r0:r0 + tile, :]
        v = vo_ref[r0:r0 + tile, :]
        kt = kt_ref[:, npr + r0:npr + r0 + tile]
        prompt = r0 < half
        dk = dv = None
        for j in (range(i, nt // 2) if prompt else [i]):
            a, b, dq = block(k, v, kt, j * tile, tile, tri if i == j else None)
            dk, dv = (a, b) if dk is None else (dk + a, dv + b)
            sl = slice(j * tile, (j + 1) * tile)
            if i == 0 or not prompt:
                dqt_ref[:, sl] = dq
            else:
                dqt_ref[:, sl] += dq
        if prompt:
            dks_ref[r0:r0 + tile, :] = dk
            dvs_ref[r0:r0 + tile, :] = dv
        else:
            o0 = npr + r0 - half
            dk_ref[o0:o0 + tile, :] = (unrope(dk, npr, tile) * scale).astype(BF)
            dv_ref[o0:o0 + tile, :] = dv.astype(BF)

    def chunk_step(ci, kind):
        r0 = pl.multiple_of(ci * chunk, chunk)
        k = kp_ref[pl.ds(r0, chunk), :]
        v = vp_ref[pl.ds(r0, chunk), :]
        kt = kt_ref[:, pl.ds(r0, chunk)]
        dk, dv, dq = block(k, v, kt, half, half, None)
        dqt_ref[:, half:] += dq
        if kind == 0:
            a, b, dq = block(k, v, kt, 0, half, None)
            dk, dv = dk + a, dv + b
            dqt_ref[:, :half] += dq
        elif kind == 1:
            dk, dv = dk + dks_ref[...], dv + dvs_ref[...]
        dk_ref[pl.ds(r0, chunk), :] = (unrope(dk, r0, chunk) * scale).astype(BF)
        dv_ref[pl.ds(r0, chunk), :] = dv.astype(BF)

    @pl.loop(0, e)
    def _(ci):
        chunk_step(ci, 0)

    chunk_step(e, 1)

    @pl.loop(e + 1, nchunk)
    def _(ci):
        chunk_step(ci, 2)

    dq = dqt_ref[...].T
    base = pl.multiple_of(e * half, half)
    dq_ref[:half, :] = (unrope(dq[:half], base, half) * scale).astype(BF)
    for r in range(half, rows, cont):
        dq_ref[r:r + cont, :] = (unrope(dq[r:r + cont], npr, cont) * scale).astype(BF)


def attn_bwd(e, q, do, o, lse, ko, vo, kp, vp, cos, sin, *, tile=256):
    rows, width = q.shape
    npr = kp.shape[0]
    keys = npr + rows // 2
    pairs = width // 128
    own = pl.BlockSpec((rows, 128), lambda i, *_: (0, i))
    pr = pl.BlockSpec((npr, 128), lambda i, *_: (0, i))
    al = pl.BlockSpec((keys, 128), lambda i, *_: (0, i))
    tab = pl.BlockSpec(cos.shape, lambda i, *_: (0, 0))
    return pl.pallas_call(
        functools.partial(attn_bwd_kernel, tile=tile, scale=0.125),
        grid_spec=pltpu.PrefetchScalarGridSpec(
            num_scalar_prefetch=1, grid=(pairs,),
            in_specs=[own, own, own, pl.BlockSpec((1, 2, rows), lambda i, *_: (i, 0, 0)), own, own, pr, pr, tab, tab],
            out_specs=[own, al, al],
            scratch_shapes=[pltpu.VMEM((128, npr + rows), BF), pltpu.VMEM((128, rows), F32),
                            pltpu.VMEM((2, rows, 128), BF), pltpu.VMEM((2, rows, 128), BF),
                            pltpu.VMEM((8, rows), F32),
                            pltpu.VMEM((rows // 2, 128), F32), pltpu.VMEM((rows // 2, 128), F32)]),
        out_shape=[jax.ShapeDtypeStruct((rows, width), BF), jax.ShapeDtypeStruct((keys, width), BF),
                   jax.ShapeDtypeStruct((keys, width), BF)],
        compiler_params=params(),
        cost_estimate=pl.CostEstimate(flops=10 * rows * npr * width * 2, bytes_accessed=2 * npr * width * 8, transcendentals=rows * npr * 12),
        name="attn_bwd",
    )(e, q, do, o, lse, ko, vo, kp, vp, cos, sin)


def pick(values, lane, index):
    return jnp.sum(jnp.where(lane == index, values, 0.0), axis=1, keepdims=True)


def softmax_pair(a, b):
    top = jnp.maximum(a, b)
    ea, eb = jnp.exp(a - top), jnp.exp(b - top)
    total = ea + eb
    return ea / total, eb / total


def gate_kernel(x_ref, o_ref, w_ref, gain_ref, wcat_ref, prev_ref, routes_ref, x2_ref, h2_ref, aux_ref, ext_ref, *, experts):
    x2 = x_ref[...].astype(F32) + dot(o_ref[...], w_ref[...])
    x2_ref[...] = x2
    h2 = (x2 * rms_scale(x2) * gain_ref[...]).astype(BF)
    h2_ref[...] = h2
    logits = dot(h2, wcat_ref[...]) + prev_ref[...]
    lane = lane_iota()
    gates = softmax_pair(*[pick(logits, lane, routes_ref[:, k:k + 1]) for k in range(2)])
    aux = logits
    for k in range(2):
        aux = jnp.where(lane == experts + k, gates[k], aux)
    at = experts + 2
    for c in range(2):
        alpha = softmax_pair(*[pick(logits, lane, experts + 2 * c + k) for k in range(2)])
        for k in range(2):
            aux = jnp.where(lane == at + 2 * c + k, alpha[k], aux)
    aux_ref[...] = aux
    for k in range(2):
        parts, left = [], gates[k]
        for _ in range(3):
            part = left.astype(BF)
            parts.append(part.astype(F32))
            left = left - parts[-1]
        spread = jnp.where(lane == 0, parts[0], jnp.where(lane == 1, parts[1], jnp.where(lane == 2, parts[2], 0.0)))
        ext_ref[:, k * 128:(k + 1) * 128] = spread.astype(BF)


def gates(x, o, w_out, gain, wcat, prev, routes, experts, tile=256):
    rows, width = x.shape
    block = pl.BlockSpec((tile, width), lambda i: (i, 0))
    thin = pl.BlockSpec((tile, 128), lambda i: (i, 0))
    return pl.pallas_call(
        functools.partial(gate_kernel, experts=experts),
        grid=(rows // tile,),
        in_specs=[block, block, whole(w_out.shape), whole(gain.shape), whole(wcat.shape), thin,
                  pl.BlockSpec((tile, 2), lambda i: (i, 0))],
        out_specs=[block, block, thin, pl.BlockSpec((tile, 256), lambda i: (i, 0))],
        out_shape=[jax.ShapeDtypeStruct((rows, width), F32), jax.ShapeDtypeStruct((rows, width), BF),
                   jax.ShapeDtypeStruct((rows, 128), F32), jax.ShapeDtypeStruct((rows, 256), BF)],
        compiler_params=params(),
        cost_estimate=pl.CostEstimate(flops=2 * rows * width * width, bytes_accessed=12 * rows * width, transcendentals=0),
        name="gates",
    )(x, o, w_out, gain, wcat, prev, routes)


def dispatch_kernel(slot_ref, rows_ref, *refs, capacity):
    out_ref = refs[-1]
    width = rows_ref.shape[1]
    ids = pl.program_id(0) * capacity + lax.broadcasted_iota(jnp.int32, (capacity, 1), 0)
    hot = [jnp.where(ids == slot_ref[k:k + 1, :], 1.0, 0.0).astype(BF) for k in range(2)]
    out_ref[0, :, :width] = dot(hot[0] + hot[1], rows_ref[...]).astype(BF)
    if len(refs) > 1:
        out_ref[0, :, width:] = (dot(hot[0], refs[0][:, :128]) + dot(hot[1], refs[0][:, 128:])).astype(BF)


def dispatch(slots, rows, ext, destinations, capacity):
    count, width = rows.shape
    extra = () if ext is None else (ext,)
    out_width = width + (128 if extra else 0)
    return pl.pallas_call(
        functools.partial(dispatch_kernel, capacity=capacity),
        grid=(destinations,),
        in_specs=[whole(slots.shape), whole(rows.shape)] + [whole(a.shape) for a in extra],
        out_specs=pl.BlockSpec((1, capacity, out_width), lambda i: (i, 0, 0)),
        out_shape=jax.ShapeDtypeStruct((destinations, capacity, out_width), BF),
        compiler_params=params(),
        cost_estimate=pl.CostEstimate(flops=2 * destinations * capacity * count * width, bytes_accessed=4 * count * width,
                                      transcendentals=0),
        name="dispatch_rows" if extra else "dispatch_grads",
    )(slots, rows, *extra)


def ffn_fwd_kernel(j_ref, a_ref, wg_ref, wu_ref, wd_ref, hid_ref, act_ref, slope_ref, out_ref, acc_ref):
    width = wg_ref.shape[1]
    a = a_ref[:, :width]
    gate, up = dot(a, wg_ref[0]), dot(a, wu_ref[0])
    sig = jax.nn.sigmoid(gate)
    act = gate * sig
    hidden = (act * up).astype(BF)
    hid_ref[...] = hidden
    act_ref[...] = act.astype(BF)
    slope_ref[...] = (up * sig * (1.0 + gate * (1.0 - sig))).astype(BF)
    made = dot(hidden, wd_ref[0])
    step = pl.program_id(0)

    @pl.when(step == 0)
    def _():
        acc_ref[...] = made

    @pl.when(step > 0)
    def _():
        acc_ref[...] += made

    @pl.when(step == pl.num_programs(0) - 1)
    def _():
        out_ref[...] = acc_ref[...].astype(BF)


def ffn_fwd(j, a, w_gate, w_up, w_down, tile=256):
    rows = a.shape[0]
    _, width, ff = w_gate.shape
    col = pl.BlockSpec((1, width, tile), lambda i, j: (j[0], 0, i))
    row = pl.BlockSpec((1, tile, width), lambda i, j: (j[0], i, 0))
    mid = pl.BlockSpec((rows, tile), lambda i, j: (0, i))
    return pl.pallas_call(
        ffn_fwd_kernel,
        grid_spec=pltpu.PrefetchScalarGridSpec(
            num_scalar_prefetch=1, grid=(ff // tile,),
            in_specs=[whole(a.shape), col, col, row],
            out_specs=[mid, mid, mid, whole((rows, width))],
            scratch_shapes=[pltpu.VMEM((rows, width), F32)]),
        out_shape=[jax.ShapeDtypeStruct((rows, ff), BF)] * 3 + [jax.ShapeDtypeStruct((rows, width), BF)],
        compiler_params=params(),
        cost_estimate=pl.CostEstimate(flops=6 * rows * width * ff, bytes_accessed=6 * rows * ff + 6 * width * ff,
                                      transcendentals=rows * ff),
        name="ffn_fwd",
    )(j, a, w_gate, w_up, w_down)


def ffn_bwd_kernel(j_ref, g_ref, a_ref, act_ref, slope_ref, wg_ref, wu_ref, wd_ref, dg_ref, du_ref, dout_ref, drow_ref, acc_ref):
    width = g_ref.shape[1]
    step = pl.program_id(0)

    @pl.when(step == 0)
    def _():
        gate = jnp.sum(a_ref[...].astype(F32), axis=1, keepdims=True)
        dout_ref[...] = (g_ref[...].astype(F32) * gate).astype(BF)

    dh = dot(dout_ref[...], wd_ref[0], NT)
    du = (dh * act_ref[...].astype(F32)).astype(BF)
    dg = (dh * slope_ref[...].astype(F32)).astype(BF)
    du_ref[...] = du
    dg_ref[...] = dg
    back = dot(dg, wg_ref[0], NT) + dot(du, wu_ref[0], NT)

    @pl.when(step == 0)
    def _():
        acc_ref[...] = back

    @pl.when(step > 0)
    def _():
        acc_ref[...] += back

    @pl.when(step == pl.num_programs(0) - 1)
    def _():
        drow_ref[...] = acc_ref[...].astype(BF)


def ffn_bwd(j, g, a, act, slope, w_gate, w_up, w_down, tile=256):
    rows, width = g.shape
    ff = w_gate.shape[2]
    col = pl.BlockSpec((1, width, tile), lambda i, j: (j[0], 0, i))
    row = pl.BlockSpec((1, tile, width), lambda i, j: (j[0], i, 0))
    mid = pl.BlockSpec((rows, tile), lambda i, j: (0, i))
    gate = pl.BlockSpec((rows, 128), lambda i, j: (0, width // 128))
    return pl.pallas_call(
        ffn_bwd_kernel,
        grid_spec=pltpu.PrefetchScalarGridSpec(
            num_scalar_prefetch=1, grid=(ff // tile,),
            in_specs=[whole(g.shape), gate, mid, mid, col, col, row],
            out_specs=[mid, mid, whole((rows, width)), whole((rows, width))],
            scratch_shapes=[pltpu.VMEM((rows, width), F32)]),
        out_shape=[jax.ShapeDtypeStruct((rows, ff), BF)] * 2 + [jax.ShapeDtypeStruct((rows, width), BF)] * 2,
        compiler_params=params(),
        cost_estimate=pl.CostEstimate(flops=6 * rows * width * ff, bytes_accessed=8 * rows * ff + 6 * width * ff,
                                      transcendentals=0),
        name="ffn_bwd",
    )(j, g, a, act, slope, w_gate, w_up, w_down)


def ffn_grad_kernel(a_ref, dout_ref, hid_ref, dg_ref, du_ref, out_ref, at_ref, dt_ref):
    width = dout_ref.shape[1]

    @pl.when(pl.program_id(0) == 0)
    def _():
        at_ref[...] = a_ref[:, :width].T
        dt_ref[...] = dout_ref[...].T

    out_ref[0] = dot(at_ref[...], dg_ref[...]).astype(BF)
    out_ref[1] = dot(at_ref[...], du_ref[...]).astype(BF)
    out_ref[2] = dot(dt_ref[...], hid_ref[...]).astype(BF)


def ffn_grad(a, dout, hidden, dg, du, tile=256):
    rows, width = dout.shape
    ff = dg.shape[1]
    mid = pl.BlockSpec((rows, tile), lambda i: (0, i))
    return pl.pallas_call(
        ffn_grad_kernel,
        grid=(ff // tile,),
        in_specs=[whole(a.shape), whole(dout.shape), mid, mid, mid],
        out_specs=pl.BlockSpec((3, width, tile), lambda i: (0, 0, i)),
        out_shape=jax.ShapeDtypeStruct((3, width, ff), BF),
        scratch_shapes=[pltpu.VMEM((width, rows), BF)] * 2,
        compiler_params=params(),
        cost_estimate=pl.CostEstimate(flops=6 * rows * width * ff, bytes_accessed=6 * rows * ff + 6 * width * ff,
                                      transcendentals=0),
        name="ffn_grad",
    )(a, dout, hidden, dg, du)


def combine_kernel(made_ref, back_ref, slot_ref, routes_ref, aux_ref, x2_ref, h2_ref, g_ref, gain_ref, wcat_ref, v_ref, w_ref,
                   mixed_ref, prev_ref, dx2_ref, da_ref, do_ref, cat_ref, sums_ref, *, experts):
    step = pl.program_id(0)
    lane = lane_iota()
    aux = aux_ref[...]
    h2 = h2_ref[...].astype(F32)
    g = g_ref[...].astype(F32)
    x2 = x2_ref[...]
    r2 = rms_scale(x2)
    slot_total = made_ref.shape[0]
    slot_ids = lane_iota(slot_total)
    hot = [jnp.where(slot_ids == slot_ref[:, k:k + 1], 1.0, 0.0).astype(BF) for k in range(2)]
    gate = [pick(aux, lane, experts + k) for k in range(2)]
    alpha = [[pick(aux, lane, experts + 2 + 2 * c + k) for k in range(2)] for c in range(2)]
    route = [routes_ref[:, k:k + 1] for k in range(2)]
    one = lambda cond: jnp.where(cond, 1.0, 0.0)
    copy = [one(route[k] == FFN_EXP + 1) for k in range(2)]
    const = [[one(route[k] == FFN_EXP + 2 + c) for c in range(2)] for k in range(2)]
    dgate = []
    x3 = x2
    for k in range(2):
        on_h2 = copy[k] + const[k][0] * alpha[0][0] + const[k][1] * alpha[1][0]
        branch = dot(hot[k], made_ref[...]) + on_h2 * h2
        for c in range(2):
            branch = branch + (const[k][c] * alpha[c][1]) * v_ref[c:c + 1, :]
        x3 = x3 + gate[k] * branch
        dgate.append(jnp.sum(g * branch, axis=1, keepdims=True))
    mixed_ref[...] = x3.astype(BF)
    mean = gate[0] * dgate[0] + gate[1] * dgate[1]
    dl = [gate[k] * (dgate[k] - mean) for k in range(2)]
    grads = jnp.where(lane == route[0], dl[0], 0.0) + jnp.where(lane == route[1], dl[1], 0.0)
    prev_ref[...] = grads[:, :experts]
    weight = [gate[0] * const[0][c] + gate[1] * const[1][c] for c in range(2)]
    g_h2 = jnp.sum(g * h2, axis=1, keepdims=True)
    sums = []
    on_g = copy[0] * gate[0] + copy[1] * gate[1]
    for c in range(2):
        da0 = weight[c] * g_h2
        da1 = weight[c] * jnp.sum(g * v_ref[c:c + 1, :], axis=1, keepdims=True)
        mid = alpha[c][0] * da0 + alpha[c][1] * da1
        grads = jnp.where(lane == experts + 2 * c, alpha[c][0] * (da0 - mid), grads)
        grads = jnp.where(lane == experts + 2 * c + 1, alpha[c][1] * (da1 - mid), grads)
        on_g = on_g + alpha[c][0] * weight[c]
        sums.append(jnp.sum((alpha[c][1] * weight[c]) * g, axis=0, keepdims=True))
    low = grads.astype(BF)
    cat = dot(low.T, h2_ref[...])
    dh2 = dot(low, wcat_ref[...], NT) + on_g * g + dot(hot[0] + hot[1], back_ref[...])
    sums.append(jnp.sum(dh2 * x2 * r2, axis=0, keepdims=True))
    u = dh2 * gain_ref[...]
    dx2 = g + r2 * (u - x2 * (r2 * r2) * jnp.mean(u * x2, axis=-1, keepdims=True))
    dx2_ref[...] = dx2
    da = dx2.astype(BF)
    da_ref[...] = da
    do_ref[...] = dot(da, w_ref[...], NT).astype(BF)
    parts = jnp.concatenate(sums + [jnp.zeros((8 - len(sums), g.shape[1]), F32)], axis=0)

    @pl.when(step == 0)
    def _():
        cat_ref[...] = cat
        sums_ref[...] = parts

    @pl.when(step > 0)
    def _():
        cat_ref[...] += cat
        sums_ref[...] += parts


def combine(made, back, slots, routes, aux, x2, h2, g, gain, wcat, const_v, w_out, experts, tile=256):
    rows, width = x2.shape
    block = pl.BlockSpec((tile, width), lambda i: (i, 0))
    thin = pl.BlockSpec((tile, 128), lambda i: (i, 0))
    two = pl.BlockSpec((tile, 2), lambda i: (i, 0))
    sds = jax.ShapeDtypeStruct
    return pl.pallas_call(
        functools.partial(combine_kernel, experts=experts),
        grid=(rows // tile,),
        in_specs=[whole(made.shape), whole(back.shape), two, two, thin, block, block, block, whole(gain.shape),
                  whole(wcat.shape), whole(const_v.shape), whole(w_out.shape)],
        out_specs=[block, pl.BlockSpec((tile, experts), lambda i: (i, 0)), block, block, block, whole((128, width)),
                   whole((8, width))],
        out_shape=[sds((rows, width), BF), sds((rows, experts), F32), sds((rows, width), F32), sds((rows, width), BF),
                   sds((rows, width), BF), sds((128, width), F32), sds((8, width), F32)],
        compiler_params=params(),
        cost_estimate=pl.CostEstimate(flops=8 * rows * width * made.shape[0], bytes_accessed=30 * rows * width,
                                      transcendentals=0),
        name="combine",
    )(made, back, slots, routes, aux, x2, h2, g, gain, wcat, const_v, w_out)


def prompt_back_kernel(dk_ref, dv_ref, wk_ref, wv_ref, x_ref, out_ref, sum_ref):
    dh = dot(dk_ref[...], wk_ref[...], NT) + dot(dv_ref[...], wv_ref[...], NT)
    out_ref[...] = dh.astype(BF)
    x = x_ref[...].astype(F32)
    part = jnp.sum(dh * (x * rms_scale(x)), axis=0, keepdims=True)
    step = pl.program_id(0)

    @pl.when(step == 0)
    def _():
        sum_ref[...] = part

    @pl.when(step > 0)
    def _():
        sum_ref[...] += part


def prompt_back(dk, dv, w_key, w_value, x, tile=256):
    rows, width = x.shape
    block = pl.BlockSpec((tile, width), lambda i: (i, 0))
    return pl.pallas_call(
        prompt_back_kernel,
        grid=(rows // tile,),
        in_specs=[block, block, whole(w_key.shape), whole(w_value.shape), block],
        out_specs=[block, whole((1, width))],
        out_shape=[jax.ShapeDtypeStruct((rows, width), BF), jax.ShapeDtypeStruct((1, width), F32)],
        compiler_params=params(),
        cost_estimate=pl.CostEstimate(flops=4 * rows * width * width, bytes_accessed=8 * rows * width, transcendentals=0),
        name="prompt_back",
    )(dk, dv, w_key, w_value, x)


def own_back_kernel(dq_ref, dk_ref, dv_ref, wq_ref, wk_ref, wv_ref, x_ref, out_ref, sum_ref):
    step = pl.program_id(0)
    x = x_ref[...].astype(F32)
    xr = x * rms_scale(x)

    @pl.when(step == 0)
    def _():
        sum_ref[...] = jnp.zeros_like(sum_ref)

    def put(dh):
        out_ref[...] = dh
        sum_ref[...] += jnp.sum(dh * xr, axis=0, keepdims=True)

    @pl.when(step < pl.num_programs(0) // 2)
    def _():
        put(dot(dq_ref[...], wq_ref[...], NT))

    @pl.when(step >= pl.num_programs(0) // 2)
    def _():
        put(dot(dq_ref[...], wq_ref[...], NT) + dot(dk_ref[...], wk_ref[...], NT) + dot(dv_ref[...], wv_ref[...], NT))


def own_back(dq, dk, dv, w_query, w_key, w_value, x, tile=256):
    rows, width = x.shape
    block = pl.BlockSpec((tile, width), lambda i: (i, 0))
    half = rows // 2 // tile
    first = (dk.shape[0] - rows // 2) // tile
    key = pl.BlockSpec((tile, width), lambda i: (first + jnp.maximum(i - half, 0), 0))
    return pl.pallas_call(
        own_back_kernel,
        grid=(rows // tile,),
        in_specs=[block, key, key] + [whole(w_key.shape)] * 3 + [block],
        out_specs=[block, whole((1, width))],
        out_shape=[jax.ShapeDtypeStruct((rows, width), F32), jax.ShapeDtypeStruct((1, width), F32)],
        compiler_params=params(),
        cost_estimate=pl.CostEstimate(flops=4 * rows * width * width, bytes_accessed=8 * rows * width, transcendentals=0),
        name="own_back",
    )(dq, dk, dv, w_query, w_key, w_value, x)


def weight_back_kernel(hp_ref, ho_ref, dq_ref, dk_ref, dv_ref, out_ref, acc_ref, *, prompt_steps, own_steps):
    step = pl.program_id(0)
    half = own_steps // 2

    @pl.when(step == 0)
    def _():
        acc_ref[...] = jnp.zeros_like(acc_ref)

    @pl.when(step < prompt_steps)
    def _():
        ht = hp_ref[...].T
        acc_ref[1] += dot(ht, dk_ref[...])
        acc_ref[2] += dot(ht, dv_ref[...])

    @pl.when(step >= prompt_steps)
    def _():
        ht = ho_ref[...].T
        acc_ref[0] += dot(ht, dq_ref[...])

        @pl.when(step >= prompt_steps + half)
        def _():
            acc_ref[1] += dot(ht, dk_ref[...])
            acc_ref[2] += dot(ht, dv_ref[...])

    @pl.when(step == pl.num_programs(0) - 1)
    def _():
        out_ref[...] = acc_ref[...].astype(BF)


def weight_back(hp, ho, dq, dk, dv, tile=256):
    rows, width = ho.shape
    ps, os_ = hp.shape[0] // tile, rows // tile
    half = os_ // 2
    prompt = pl.BlockSpec((tile, width), lambda i: (jnp.minimum(i, ps - 1), 0))
    own = pl.BlockSpec((tile, width), lambda i: (jnp.maximum(i - ps, 0), 0))
    key = pl.BlockSpec((tile, width), lambda i: (jnp.where(i < ps + half, jnp.minimum(i, ps - 1), i - half), 0))
    return pl.pallas_call(
        functools.partial(weight_back_kernel, prompt_steps=ps, own_steps=os_),
        grid=(ps + os_,),
        in_specs=[prompt, own, own, key, key],
        out_specs=whole((3, width, width)),
        out_shape=jax.ShapeDtypeStruct((3, width, width), BF),
        scratch_shapes=[pltpu.VMEM((3, width, width), F32)],
        compiler_params=params(),
        cost_estimate=pl.CostEstimate(flops=12 * rows * width * width, bytes_accessed=12 * rows * width, transcendentals=0),
        name="weight_back",
    )(hp, ho, dq, dk, dv)


def token_back_kernel(own_ref, got_ref, x_ref, dx2_ref, gain_ref, out_ref):
    x = x_ref[...].astype(F32)
    r1 = rms_scale(x)

    def put(dh):
        u = dh * gain_ref[...]
        out_ref[...] = dx2_ref[...] + r1 * (u - x * (r1 * r1) * jnp.mean(u * x, axis=-1, keepdims=True))

    step = pl.program_id(0)

    @pl.when(step < pl.num_programs(0) // 2)
    def _():
        put(own_ref[...] + jnp.sum(got_ref[...].astype(F32), axis=0))

    @pl.when(step >= pl.num_programs(0) // 2)
    def _():
        put(own_ref[...])


def token_back(own, got, x, dx2, gain, tile=256):
    rows, width = x.shape
    block = pl.BlockSpec((tile, width), lambda i: (i, 0))
    half = rows // 2 // tile
    return pl.pallas_call(
        token_back_kernel,
        grid=(rows // tile,),
        in_specs=[block, pl.BlockSpec((got.shape[0], tile, width), lambda i: (0, jnp.minimum(i, half - 1), 0)), block, block,
                  whole(gain.shape)],
        out_specs=block,
        out_shape=jax.ShapeDtypeStruct((rows, width), F32),
        compiler_params=params(),
        cost_estimate=pl.CostEstimate(flops=10 * rows * width, bytes_accessed=14 * rows * width, transcendentals=0),
        name="token_back",
    )(own, got, x, dx2, gain)


def slot_table(routes_t, priority, groups, capacity):
    ids = jnp.arange(FFN_EXP, dtype=jnp.int32)
    picked = routes_t[:, None, :] == ids[None, :, None]
    assigned = jnp.any(picked, axis=0).astype(BF)
    earlier = (priority[:, None] < priority[None, :]).astype(BF)
    rank_table = jnp.dot(assigned, earlier, preferred_element_type=F32)
    rank = jnp.sum(jnp.where(picked, rank_table[None], 0.0), axis=1).astype(jnp.int32)
    place = (routes_t % groups) * (FFN_EXP // groups) + routes_t // groups
    return jnp.where((routes_t < FFN_EXP) & (rank < capacity), place * capacity + rank, -1)


def local(
    tokens, prev_logits, routes, priority, norm_attn, w_query, w_key, w_value, w_out, norm_ffn, router, const_w, const_v,
    w_gate, w_up, w_down, cotangent,
):
    rows, width = tokens.shape
    experts = prev_logits.shape[1]
    dp = lax.axis_size("dp")
    expert_devices = lax.axis_size("expert")
    pair = w_gate.shape[0]
    capacity = 9 * rows * routes.shape[1] // (8 * experts)
    prompt_dev = PROMPT // expert_devices
    ff = w_gate.shape[2]
    e = lax.axis_index("expert").astype(jnp.int32).reshape(1)
    j = (lax.axis_index("dp") % pair).astype(jnp.int32).reshape(1)
    members = pair * expert_devices
    everyone = ("dp", "expert")
    exchange = [list(range(p * members, (p + 1) * members)) for p in range(dp // pair)]
    alike = [list(range(q, dp, pair)) for q in range(pair)]
    pairs = [list(range(p * pair, (p + 1) * pair)) for p in range(dp // pair)]

    def swap(x):
        return lax.all_to_all(x, everyone, split_axis=0, concat_axis=0, axis_index_groups=exchange, tiled=True)

    cos, sin = (jnp.asarray(t) for t in angle_tables())
    gain1, gain2 = norm_attn[None, :], norm_ffn[None, :]

    prompt_x = lax.all_gather(tokens[:prompt_dev], "expert", axis=0, tiled=True)
    slots_t = slot_table(routes.T, priority, pair, capacity)
    slots = slots_t.T
    grads_in = swap(dispatch(slots_t, cotangent, None, members, capacity)).reshape(-1, width)
    h_own, q, k_own, v_own = project(e, tokens, gain1, (w_query, w_key, w_value), cos, sin, True)
    h_prompt, k_prompt, v_prompt = project(e, prompt_x, gain1, (w_key, w_value), cos, sin, False)
    o, lse = attn_fwd(e, q, k_own, v_own, k_prompt, v_prompt)

    wcat = jnp.concatenate(
        [router, const_w.transpose(1, 0, 2).reshape(width, -1), jnp.zeros((width, 128 - experts - 4), BF)], axis=1
    )
    prev = jnp.pad(prev_logits, ((0, 0), (0, 128 - experts)))
    x2, h2, aux, ext = gates(tokens, o, w_out, gain2, wcat, prev, routes, experts)
    arrived = swap(dispatch(slots_t, h2, ext, members, capacity)).reshape(-1, width + 128)
    hidden, act, slope, made = ffn_fwd(j, arrived, w_gate, w_up, w_down)
    made = swap(made.reshape(members, capacity, width)).reshape(-1, width)
    dg, du, dout, drow = ffn_bwd(j, grads_in, arrived, act, slope, w_gate, w_up, w_down)
    drow = swap(drow.reshape(members, capacity, width)).reshape(-1, width)
    ffn_sum = ffn_grad(arrived, dout, hidden, dg, du)
    ffn_sum = lax.psum_scatter(ffn_sum, "dp", scatter_dimension=2, axis_index_groups=alike, tiled=True)

    mixed, grad_prev, dx2, da, do, cat, sums = combine(
        made, drow, slots, routes, aux, x2, h2, cotangent, gain2, wcat, const_v, w_out, experts
    )
    grad_out = jnp.dot(o.T, da, preferred_element_type=F32).astype(BF)
    dq, dk, dv = attn_bwd(e, q, do, o, lse, k_own, v_own, k_prompt, v_prompt, cos, sin)
    dh_prompt, sum_p = prompt_back(dk, dv, w_key, w_value, prompt_x)
    got = lax.all_to_all(
        dh_prompt.reshape(expert_devices, prompt_dev, width), "expert", split_axis=0, concat_axis=0, tiled=True
    )
    dh_own, sum_o = own_back(dq, dk, dv, w_query, w_key, w_value, tokens)
    grad_w = weight_back(h_prompt, h_own, dq, dk, dv)
    small = jnp.concatenate([cat[:experts + 4], sums[:3], sum_p + sum_o], axis=0).astype(BF)
    grad_w, grad_out, small = lax.psum((grad_w, grad_out, small), everyone)
    grad_w, grad_out, small = grad_w.astype(F32), grad_out.astype(F32), small.astype(F32)
    grad_tokens = token_back(dh_own, got, tokens, dx2, gain1)

    ffn_sum = ffn_sum.reshape(3, width, pair, -1).transpose(2, 0, 1, 3)
    ffn_sum = lax.all_to_all(ffn_sum, "dp", split_axis=0, concat_axis=0, axis_index_groups=pairs, tiled=True)
    ffn_sum = ffn_sum.astype(F32)
    n = experts
    return (
        mixed,
        grad_tokens,
        grad_prev,
        small[n + 7],
        grad_w[0],
        grad_w[1],
        grad_w[2],
        grad_out,
        small[n + 6],
        small[:n].T,
        small[n:n + 4].reshape(2, 2, width).transpose(0, 2, 1),
        small[n + 4:n + 6],
        ffn_sum[:, 0],
        ffn_sum[:, 1],
        ffn_sum[:, 2].transpose(0, 2, 1),
    )


def solution(mesh):
    block = P(("dp", "expert"), None)
    in_specs = (block, block, block, P(("dp", "expert"))) + (P(),) * 9 + (P("expert", None, None),) * 3 + (block,)
    out_specs = (block, block, block) + (P(),) * 9 + (
        P("expert", None, "dp"), P("expert", None, "dp"), P("expert", "dp", None),
    )
    return jax.shard_map(local, mesh=mesh, in_specs=in_specs, out_specs=out_specs, check_vma=False)
```

time: 2050 us -> 648 us (0.32)
  waiting for transfers between devices: 860 us -> 133 us
  matrix products: 728 us -> 5.13 us
  Pallas kernels: 0 us -> 303 us
  local copies, waits for them, and re-layouts: 245 us -> 28.5 us
  other arithmetic: 119 us -> 10.3 us
  blocking collectives: 41 us -> 86.8 us
  starting transfers between devices: 20 us -> 58.3 us
    reduce_scatter x5 -> x1, waiting for transfers between devices: 721 us -> 0.02 us  [local(): lax.psum_scatter(ffn_sum, 'dp', scatter_dimension=2, axis_index_groups=al...]
    dot_general x41 -> x2, matrix products: 725 us -> 5.13 us  [the longest x1 4.33 us: local(): grad_out = jnp.dot(o.T, da, preferred_element_type=F32).astype(BF)]
    pallas_call x0 -> x15, Pallas kernels: none -> 303 us  [the longest x1 63.3 us: attn_bwd(): pl.pallas_call(functools.partial(attn_bwd_kernel, tile=tile, scale=0.125)...]
    reduce_sum x13 -> x1, other arithmetic: 67.2 us -> 0.03 us  [slot_table(): jnp.sum(jnp.where(picked, rank_table[None], 0.0), axis=1).astype(jnp.int32)]
    dynamic_update_slice x4 -> x0, local copies, waits for them, and re-layouts: 63.7 us -> none  [local(): lax.map(attend_block, (query_blocks, pos_blocks, seg_blocks))]
    gather x6 -> x0, local copies, waits for them, and re-layouts: 50.9 us -> none  [the longest x2 19.4 us: local(): jnp.take(rows_back, slot_safe, axis=0)]
    psum x1, waiting for transfers between devices: 102 us -> 52.7 us  [local(): grad_w, grad_out, small = lax.psum((grad_w, grad_out, small), everyone)]
    all_to_all x4 -> x5, starting transfers between devices: 19.7 us -> 58 us  [the longest x3 32.5 us: swap(): lax.all_to_all(x, everyone, split_axis=0, concat_axis=0, axis_index_group...]
  transfers between devices with their start and end apart: 12 -> 8, of which waited for: 9 -> 5; matrix products, arithmetic and copies ran while one was open for 11% -> 5% of each run, Pallas kernels for 0% -> 27%
where the time goes in v1:
time: 648 us; the launch traced here: 639 us
  Pallas kernels  303 us (47%)
  waiting for transfers between devices  133 us (21%)
  blocking collectives  86.8 us (13%)
  starting transfers between devices  58.3 us (9%)
  local copies, waits for them, and re-layouts  28.5 us (4%)
  between operations  14.3 us (2%)
  other arithmetic  10.3 us (2%)
    pallas_call x1, Pallas kernels, attn_bwd(): pl.pallas_call(functools.partial(attn_bwd_kernel, tile=tile, scale=0.125)...  63.3 us
    psum x1, blocking collectives, local(): grad_w, grad_out, small = lax.psum((grad_w, grad_out, small), everyone)  53.2 us
    psum x1, waiting for transfers between devices, local(): grad_w, grad_out, small = lax.psum((grad_w, grad_out, small), everyone)  52.7 us
    all_to_all x3, waiting for transfers between devices, swap(): lax.all_to_all(x, everyone, split_axis=0, concat_axis=0, axis_index_group...  45.6 us
    pallas_call x1, Pallas kernels, attn_fwd(): pl.pallas_call(functools.partial(attn_fwd_kernel, chunk=chunk, tile=tile,...  44.6 us
    pallas_call x1, Pallas kernels, ffn_bwd(): pl.pallas_call(ffn_bwd_kernel, grid_spec=pltpu.PrefetchScalarGridSpec(num...  36 us
    all_to_all x1, blocking collectives, swap(): lax.all_to_all(x, everyone, split_axis=0, concat_axis=0, axis_index_group...  33.6 us
    all_to_all x3, starting transfers between devices, swap(): lax.all_to_all(x, everyone, split_axis=0, concat_axis=0, axis_index_group...  32.5 us
  transfers between devices with their start and end apart: 8, of which 5 were waited for; matrix products, arithmetic and copies ran while one was open for 5% of the time, Pallas kernels for 27%

profile of v1, /device:TPU:9, one launch (start us, length us, event | category | flops | bytes accessed | tf_op | source)
XLA Modules:
  0.0 639.1 jit_solution(15562498267709765258)
XLA Ops:
  15.9 8.8 %project_own.1 = (bf16[1024,768]{1,0:T(8,128)(2,1)}, bf16[1024,768]{1,0:T(8,128)(2,1)}, bf16[1024,768]{1,0:T(8,128)(2,1)}, bf16[1024,768]{1,0:T(8,128)(2,1)}) custom-call(s32[1]{0:T(128)} %bitcast.2.e_ref, bf16[1024,768]{1,0:T(8,128)(2,1)} %x_ref.7, f32[1,768]{1,0:T(1,128)} %broadcast_in_dim.30.gain_ref, bf16[768,768]{1,0:T(8,128)(2,1)} %wq_ref.1, ...), custom_call_target="tpu_custom_call" | custom-call | flops 3623878656 | bytes 9437184 | tf_op jit(solution)/shard_map/project_own/pallas_call | solution.py:91
  24.7 15.6 %all-gather.2.cloned.1.call-done.x_ref = bf16[2048,768]{1,0:T(8,128)(2,1)} async-done(((bf16[512,768]{1,0:T(8,128)(2,1)}), bf16[2048,768]{1,0:T(8,128)(2,1)}) %all-gather.2.cloned.1.call-update) | async-done | bytes 3145744 | tf_op jit(solution)/shard_map/all_gather | solution.py:831
  40.3 11.7 %project_prompt.1 = (bf16[2048,768]{1,0:T(8,128)(2,1)}, bf16[2048,768]{1,0:T(8,128)(2,1)}, bf16[2048,768]{1,0:T(8,128)(2,1)}) custom-call(s32[1]{0:T(128)} %bitcast.2.e_ref, bf16[2048,768]{1,0:T(8,128)(2,1)} %all-gather.2.cloned.1.call-done.x_ref, f32[1,768]{1,0:T(1,128)} %broadcast_in_dim.30.gain_ref, bf16[768,768]{1,0:T(8,128)(2,1)} %wk_ref.3, ...), custom_call_target="tpu_custom_call" | custom-call | flops 4831838208 | bytes 18874368 | tf_op jit(solution)/shard_map/project_prompt/pallas_call | solution.py:91
  52.1 44.6 %attn_fwd.1 = (bf16[1024,768]{1,0:T(8,128)(2,1)}, f32[6,2,1024]{2,1,0:T(2,128)}) custom-call(s32[1]{0:T(128)} %bitcast.2.e_ref, bf16[1024,768]{1,0:T(8,128)(2,1)} %get-tuple-element.50.q_ref, bf16[1024,768]{1,0:T(8,128)(2,1)} %get-tuple-element.51.ko_ref, bf16[1024,768]{1,0:T(8,128)(2,1)} %get-tuple-element.52.vo_ref, ...), custom_call_target="tpu_custom_call" | custom-call | flops 12884901888 | bytes 12582912 | tf_op jit(solution)/shard_map/attn_fwd/pallas_call | solution.py:188
  96.7 7.4 %gates.1 = (f32[1024,768]{1,0:T(8,128)}, bf16[1024,768]{1,0:T(8,128)(2,1)}, f32[1024,128]{1,0:T(8,128)}, bf16[1024,256]{1,0:T(8,128)(2,1)}) custom-call(bf16[1024,768]{1,0:T(8,128)(2,1)} %x_ref.7, bf16[1024,768]{1,0:T(8,128)(2,1)} %get-tuple-element.55.o_ref, bf16[768,768]{1,0:T(8,128)(2,1)} %w_ref.3, f32[1,768]{1,0:T(1,128)} %broadcast_in_dim.31.gain_ref, ...), custom_call_target="tpu_custom_call" | custom-call | flops 1207959552 | bytes 9437184 | tf_op jit(solution)/shard_map/gates/pallas_call | solution.py:379
  104.1 8.0 %dispatch_rows.1 = bf16[8,192,896]{2,1,0:T(8,128)(2,1)} custom-call(s32[2,1024]{1,0:T(2,128)} %copy.127.slot_ref, bf16[1024,768]{1,0:T(8,128)(2,1)} %get-tuple-element.56.rows_ref.h2_ref, bf16[1024,256]{1,0:T(8,128)(2,1)} %get-tuple-element.57.refs_0_), custom_call_target="tpu_custom_call" | custom-call | flops 2415919104 | bytes 3145728 | tf_op jit(solution)/shard_map/dispatch_rows/pallas_call | solution.py:407
  112.0 9.5 %all-to-all-start = ((bf16[8,192,896]{2,1,0:T(8,128)(2,1)}), bf16[8,192,896]{2,1,0:T(8,128)(2,1)S(1)}, u32[]{:S(2)}, u32[]{:S(2)}) async-start(bf16[8,192,896]{2,1,0:T(8,128)(2,1)} %dispatch_rows.1), calls=%async_computation | async-start | bytes 5505024 | tf_op jit(solution)/shard_map/all_to_all | solution.py:826
  128.3 23.4 %all-to-all-done = bf16[8,192,896]{2,1,0:T(8,128)(2,1)S(1)} async-done(((bf16[8,192,896]{2,1,0:T(8,128)(2,1)}), bf16[8,192,896]{2,1,0:T(8,128)(2,1)S(1)}, u32[]{:S(2)}, u32[]{:S(2)}) %all-to-all-start) | async-done | bytes 2752544 | tf_op jit(solution)/shard_map/all_to_all | solution.py:826
  153.2 7.7 %all-to-all-start.2 = ((bf16[8,192,768]{2,1,0:T(8,128)(2,1)}), bf16[8,192,768]{2,1,0:T(8,128)(2,1)}, u32[]{:S(2)}, u32[]{:S(2)}) async-start(bf16[8,192,768]{2,1,0:T(8,128)(2,1)} %dispatch_grads.1), calls=%async_computation.2 | async-start | bytes 4718592 | tf_op jit(solution)/shard_map/all_to_all | solution.py:826
  161.2 26.9 %ffn_fwd.1 = (bf16[1536,2048]{1,0:T(8,128)(2,1)}, bf16[1536,2048]{1,0:T(8,128)(2,1)}, bf16[1536,2048]{1,0:T(8,128)(2,1)}, bf16[1536,768]{1,0:T(8,128)(2,1)}) custom-call(s32[1]{0:T(128)} %bitcast.j_ref, bf16[1536,896]{1,0:T(8,128)(2,1)} %bitcast.51, bf16[2,768,2048]{2,1,0:T(8,128)(2,1)} %wg_ref.3, bf16[2,768,2048]{2,1,0:T(8,128)(2,1)} %wu_ref.3, ...), custom_call_target="tpu_custom_call" | custom-call | flops 14495514624 | bytes 28311552 | tf_op jit(solution)/shard_map/ffn_fwd/pallas_call | solution.py:452
  188.2 36.0 %ffn_bwd.1 = (bf16[1536,2048]{1,0:T(8,128)(2,1)}, bf16[1536,2048]{1,0:T(8,128)(2,1)}, bf16[1536,768]{1,0:T(8,128)(2,1)}, bf16[1536,768]{1,0:T(8,128)(2,1)}) custom-call(s32[1]{0:T(128)} %bitcast.j_ref, bf16[1536,768]{1,0:T(8,128)(2,1)} %bitcast.7.g_ref, bf16[1536,896]{1,0:T(8,128)(2,1)} %bitcast.52, bf16[1536,2048]{1,0:T(8,128)(2,1)} %get-tuple-element.59.act_ref, ...), custom_call_target="tpu_custom_call" | custom-call | flops 14495514624 | bytes 34603008 | tf_op jit(solution)/shard_map/ffn_bwd/pallas_call | solution.py:503
  224.2 22.1 %ffn_grad.1 = bf16[3,768,2048]{2,1,0:T(8,128)(2,1)} custom-call(bf16[1536,896]{1,0:T(8,128)(2,1)} %bitcast.53, bf16[1536,768]{1,0:T(8,128)(2,1)} %get-tuple-element.81.dout_ref, bf16[1536,2048]{1,0:T(8,128)(2,1)} %get-tuple-element.82.hid_ref, bf16[1536,2048]{1,0:T(8,128)(2,1)} %get-tuple-element.83.dg_ref, bf16[1536,2048]{1,0:T(8,128)(2,1)} %get-tuple-element.84.du_ref), custom_call_target="tpu_custom_call" | custom-call | flops 14495514624 | bytes 28311552 | tf_op jit(solution)/shard_map/ffn_grad/pallas_call | solution.py:535
  248.0 33.6 %all_to_all.30 = bf16[8,192,768]{2,1,0:T(8,128)(2,1)} all-to-all(bf16[8,192,768]{2,1,0:T(8,128)(2,1)S(1)} %bitcast.57), channel_id=1, replica_groups={{0,1,2,3,4,5,6,7},{8,9,10,11,12,13,14,15},{16,17,18,19,20,21,22,23},{24..., dimensions={0} | all-to-all | bytes 4718592 | tf_op jit(solution)/shard_map/all_to_all | solution.py:826
  281.6 15.3 %all-to-all-start.3 = ((bf16[8,192,768]{2,1,0:T(8,128)(2,1)}), bf16[8,192,768]{2,1,0:T(8,128)(2,1)S(1)}, u32[]{:S(2)}, u32[]{:S(2)}) async-start(bf16[8,192,768]{2,1,0:T(8,128)(2,1)} %bitcast.8), calls=%async_computation.3 | async-start | bytes 4718592 | tf_op jit(solution)/shard_map/all_to_all | solution.py:826
  300.5 22.2 %all-to-all-done.3 = bf16[8,192,768]{2,1,0:T(8,128)(2,1)S(1)} async-done(((bf16[8,192,768]{2,1,0:T(8,128)(2,1)}), bf16[8,192,768]{2,1,0:T(8,128)(2,1)S(1)}, u32[]{:S(2)}, u32[]{:S(2)}) %all-to-all-start.3) | async-done | bytes 2359328 | tf_op jit(solution)/shard_map/all_to_all | solution.py:826
  324.0 23.1 %combine.1 = (bf16[1024,768]{1,0:T(8,128)(2,1)}, f32[1024,12]{1,0:T(8,128)}, f32[1024,768]{1,0:T(8,128)}, bf16[1024,768]{1,0:T(8,128)(2,1)}, bf16[1024,768]{1,0:...) custom-call(bf16[1536,768]{1,0:T(8,128)(2,1)} %bitcast.55, bf16[1536,768]{1,0:T(8,128)(2,1)} %bitcast.56, ...), custom_call_target="tpu_custom_call" | custom-call | flops 9663676416 | bytes 23592960 | tf_op jit(solution)/shard_map/combine/pallas_call | solution.py:622
  347.2 63.3 %attn_bwd.1 = (bf16[1024,768]{1,0:T(8,128)(2,1)}, bf16[2560,768]{1,0:T(8,128)(2,1)}, bf16[2560,768]{1,0:T(8,128)(2,1)}) custom-call(s32[1]{0:T(128)} %bitcast.2.e_ref, bf16[1024,768]{1,0:T(8,128)(2,1)} %get-tuple-element.50.q_ref, bf16[1024,768]{1,0:T(8,128)(2,1)} %get-tuple-element.65.do_ref, bf16[1024,768]{1,0:T(8,128)(2,1)} %get-tuple-element.55.o_ref, ...), custom_call_target="tpu_custom_call" | custom-call | flops 32212254720 | bytes 25165824 | tf_op jit(solution)/shard_map/attn_bwd/pallas_call | solution.py:319
  410.5 11.5 %prompt_back.1 = (bf16[2048,768]{1,0:T(8,128)(2,1)}, f32[1,768]{1,0:T(1,128)}) custom-call(bf16[2560,768]{1,0:T(8,128)(2,1)} %get-tuple-element.68.dk_ref, bf16[2560,768]{1,0:T(8,128)(2,1)} %get-tuple-element.69.dv_ref, bf16[768,768]{1,0:T(8,128)(2,1)} %wk_ref.3, bf16[768,768]{1,0:T(8,128)(2,1)} %wv_ref.3, bf16[2048,768]{1,0:T(8,128)(2,1)} %all-gather.2.cloned.1.call-done.x_ref), custom_call_target="tpu_custom_call" | custom-call | flops 4831838208 | bytes 12582912 | tf_op jit(solution)/shard_map/prompt_back/pallas_call | solution.py:657
  422.0 20.7 %all-to-all-start.4 = ((bf16[4,512,768]{2,1,0:T(8,128)(2,1)}), bf16[4,512,768]{2,1,0:T(8,128)(2,1)S(1)}, u32[]{:S(2)}, u32[]{:S(2)}) async-start(bf16[4,512,768]{2,1,0:T(8,128)(2,1)} %bitcast.50), calls=%async_computation.4 | async-start | bytes 6291456 | tf_op jit(solution)/shard_map/all_to_all | solution.py:858
  447.0 17.1 %weight_back.1 = bf16[3,768,768]{2,1,0:T(8,128)(2,1)} custom-call(bf16[2048,768]{1,0:T(8,128)(2,1)} %get-tuple-element.78.hp_ref, bf16[1024,768]{1,0:T(8,128)(2,1)} %get-tuple-element.79.ho_ref, bf16[1024,768]{1,0:T(8,128)(2,1)} %get-tuple-element.67.dq_ref, bf16[2560,768]{1,0:T(8,128)(2,1)} %get-tuple-element.68.dk_ref, ...), custom_call_target="tpu_custom_call" | custom-call | flops 7247757312 | bytes 9437184 | tf_op jit(solution)/shard_map/weight_back/pallas_call | solution.py:745
  467.4 18.9 %all-to-all-done.4.got_ref = bf16[4,512,768]{2,1,0:T(8,128)(2,1)S(1)} async-done(((bf16[4,512,768]{2,1,0:T(8,128)(2,1)}), bf16[4,512,768]{2,1,0:T(8,128)(2,1)S(1)}, u32[]{:S(2)}, u32[]{:S(2)}) %all-to-all-start.4) | async-done | bytes 3145760 | tf_op jit(solution)/shard_map/all_to_all | solution.py:858
  492.9 8.4 %own_back.1 = (f32[1024,768]{1,0:T(8,128)}, f32[1,768]{1,0:T(1,128)}) custom-call(bf16[1024,768]{1,0:T(8,128)(2,1)} %get-tuple-element.67.dq_ref, bf16[2560,768]{1,0:T(8,128)(2,1)} %get-tuple-element.68.dk_ref, bf16[2560,768]{1,0:T(8,128)(2,1)} %get-tuple-element.69.dv_ref, bf16[768,768]{1,0:T(8,128)(2,1)} %wq_ref.1, bf16[768,768]{1,0:T(8,128)(2,1)} %wk_ref.3, ...), custom_call_target="tpu_custom_call" | custom-call | flops 2415919104 | bytes 6291456 | tf_op jit(solution)/shard_map/own_back/pallas_call | solution.py:697
  503.6 53.2 %psum.21 = bf16[20,768]{1,0:T(8,128)(2,1)S(1)} all-reduce(bf16[20,768]{1,0:T(8,128)(2,1)S(1)} %pad_maximum_fusion), channel_id=1, replica_groups=mesh['dp'=8,'expert'=4] {'dp','expert'}, use_global_device_ids=true, to_apply=%region_2.3 | all-reduce | flops 15360 | bytes 61440 | tf_op jit(solution)/shard_map/psum | solution.py:864
  560.0 52.7 %all-reduce.4.cloned.1.call-done = (bf16[3,768,768]{2,1,0:T(8,128)(2,1)}, bf16[768,768]{1,0:T(8,128)(2,1)}) async-done(((bf16[3,768,768]{2,1,0:T(8,128)(2,1)}, bf16[768,768]{1,0:T(8,128)(2,1)}), (bf16[3,768,768]{2,1,0:T(8,128)(2,1)}, bf16[768,768]{1,0:T(8,128)(2,1)})) %all-reduce.4.cloned.1.call-update) | async-done | bytes 4718608 | tf_op jit(solution)/shard_map/psum | solution.py:864
  (86 shorter events, 63.0 us)
Async XLA Ops:
  7.2 2.2 copy-start.12
  7.2 2.8 copy-start.13
  7.2 3.4 copy-start.11
  7.2 3.6 copy-start.10
  7.2 3.7 copy-start.9
  7.2 4.2 copy-start.15
  7.2 33.1 %all-gather.2.cloned.1.call-start = ((), (), s32[]{:S(2)}) async-start(), calls=%async_computation.7 | async-start | bytes 3932160 | tf_op jit(solution)/shard_map/all_gather | solution.py:831
  11.0 2.9 copy-start.8
  11.2 2.9 copy-start
  112.0 39.7 %all-to-all-start = ((bf16[8,192,896]{2,1,0:T(8,128)(2,1)}), bf16[8,192,896]{2,1,0:T(8,128)(2,1)S(1)}, u32[]{:S(2)}, u32[]{:S(2)}) async-start(bf16[8,192,896]{2,1,0:T(8,128)(2,1)} %dispatch_rows.1), calls=%async_computation | async-start | bytes 5505024 | tf_op jit(solution)/shard_map/all_to_all | solution.py:826
  151.7 1.5 copy-start.4
  153.2 34.9 %all-to-all-start.2 = ((bf16[8,192,768]{2,1,0:T(8,128)(2,1)}), bf16[8,192,768]{2,1,0:T(8,128)(2,1)}, u32[]{:S(2)}, u32[]{:S(2)}) async-start(bf16[8,192,768]{2,1,0:T(8,128)(2,1)} %dispatch_grads.1), calls=%async_computation.2 | async-start | bytes 4718592 | tf_op jit(solution)/shard_map/all_to_all | solution.py:826
  161.0 303.2 %reduce-scatter.2.cloned.1.call-start = ((), (), s32[]{:S(2)}) async-start(), calls=%async_computation.8 | async-start | bytes 11796480 | tf_op jit(solution)/shard_map/reduce_scatter | solution.py:850
  246.3 1.7 copy-start.6
  281.6 16.5 %copy-start.1 = (s32[1024,2]{1,0:T(8,128)S(1)}, s32[1024,2]{1,0:T(8,128)}, u32[]{:S(2)}) copy-start(s32[1024,2]{1,0:T(8,128)} %copy-done) | copy-start | bytes 24580
  281.6 41.0 %all-to-all-start.3 = ((bf16[8,192,768]{2,1,0:T(8,128)(2,1)}), bf16[8,192,768]{2,1,0:T(8,128)(2,1)S(1)}, u32[]{:S(2)}, u32[]{:S(2)}) async-start(bf16[8,192,768]{2,1,0:T(8,128)(2,1)} %bitcast.8), calls=%async_computation.3 | async-start | bytes 4718592 | tf_op jit(solution)/shard_map/all_to_all | solution.py:826
  322.6 1.4 copy-start.5
  422.0 64.3 %all-to-all-start.4 = ((bf16[4,512,768]{2,1,0:T(8,128)(2,1)}), bf16[4,512,768]{2,1,0:T(8,128)(2,1)S(1)}, u32[]{:S(2)}, u32[]{:S(2)}) async-start(bf16[4,512,768]{2,1,0:T(8,128)(2,1)} %bitcast.50), calls=%async_computation.4 | async-start | bytes 6291456 | tf_op jit(solution)/shard_map/all_to_all | solution.py:858
  442.7 170.0 %all-reduce.4.cloned.1.call-start = ((), (), s32[]{:S(2)}) async-start(), calls=%async_computation.9 | async-start | bytes 9437184 | tf_op jit(solution)/shard_map/psum | solution.py:864
  486.4 1.6 copy-start.2
  488.0 138.5 %all-to-all-start.5 = ((bf16[2,3,768,256]{3,2,1,0:T(8,128)(2,1)}), bf16[2,3,768,256]{3,2,1,0:T(8,128)(2,1)}, u32[]{:S(2)}, u32[]{:S(2)}) async-start(bf16[2,3,768,256]{3,2,1,0:T(8,128)(2,1)} %bitcast.49), calls=%async_computation.6 | async-start | bytes 4718592 | tf_op jit(solution)/shard_map/all_to_all | solution.py:869
  492.9 10.0 %copy-start.14 = (f32[1,768]{1,0:T(1,128)S(1)}, f32[1,768]{1,0:T(1,128)}, u32[]{:S(2)}) copy-start(f32[1,768]{1,0:T(1,128)} %get-tuple-element.76) | copy-start | bytes 9220
  492.9 65.1 %copy-start.7 = (f32[1024,12]{1,0:T(8,128)S(1)}, f32[1024,12]{1,0:T(8,128)}, u32[]{:S(2)}) copy-start(f32[1024,12]{1,0:T(8,128)} %get-tuple-element.147) | copy-start | bytes 147460
  612.7 3.0 copy-start.3
Sparse Core Ops, SparseCore 0:
  10.2 30.0 all-gather.1
  246.5 161.9 reduce-scatter.1
  464.3 148.4 all-reduce.3

commit v2 on v1

--- a/solution.py
+++ b/solution.py
@@ -706,7 +706,7 @@
     )(dq, dk, dv, w_query, w_key, w_value, x)
 
 
-def weight_back_kernel(hp_ref, ho_ref, dq_ref, dk_ref, dv_ref, out_ref, acc_ref, *, prompt_steps, own_steps):
+def weight_back_kernel(hp_ref, ho_ref, o_ref, da_ref, dq_ref, dk_ref, dv_ref, out_ref, acc_ref, *, prompt_steps, own_steps):
     step = pl.program_id(0)
     half = own_steps // 2
 
@@ -724,6 +724,7 @@
     def _():
         ht = ho_ref[...].T
         acc_ref[0] += dot(ht, dq_ref[...])
+        acc_ref[3] += dot(o_ref[...].T, da_ref[...])
 
         @pl.when(step >= prompt_steps + half)
         def _():
@@ -732,10 +733,14 @@
 
     @pl.when(step == pl.num_programs(0) - 1)
     def _():
-        out_ref[...] = acc_ref[...].astype(BF)
-
-
-def weight_back(hp, ho, dq, dk, dv, tile=256):
+        width = acc_ref.shape[1]
+        for n in range(4):
+            out_ref[n * width:(n + 1) * width, :] = acc_ref[n].astype(BF)
+        if out_ref.shape[0] > 4 * width:
+            out_ref[4 * width:, :] = jnp.zeros((out_ref.shape[0] - 4 * width, width), BF)
+
+
+def weight_back(hp, ho, o, da, dq, dk, dv, out_rows, tile=256):
     rows, width = ho.shape
     ps, os_ = hp.shape[0] // tile, rows // tile
     half = os_ // 2
@@ -745,14 +750,14 @@
     return pl.pallas_call(
         functools.partial(weight_back_kernel, prompt_steps=ps, own_steps=os_),
         grid=(ps + os_,),
-        in_specs=[prompt, own, own, key, key],
-        out_specs=whole((3, width, width)),
-        out_shape=jax.ShapeDtypeStruct((3, width, width), BF),
-        scratch_shapes=[pltpu.VMEM((3, width, width), F32)],
-        compiler_params=params(),
-        cost_estimate=pl.CostEstimate(flops=12 * rows * width * width, bytes_accessed=12 * rows * width, transcendentals=0),
+        in_specs=[prompt, own, own, own, own, key, key],
+        out_specs=whole((out_rows, width)),
+        out_shape=jax.ShapeDtypeStruct((out_rows, width), BF),
+        scratch_shapes=[pltpu.VMEM((4, width, width), F32)],
+        compiler_params=params(),
+        cost_estimate=pl.CostEstimate(flops=16 * rows * width * width, bytes_accessed=14 * rows * width, transcendentals=0),
         name="weight_back",
-    )(hp, ho, dq, dk, dv)
+    )(hp, ho, o, da, dq, dk, dv)
 
 
 def token_back_kernel(own_ref, got_ref, x_ref, dx2_ref, gain_ref, out_ref):
@@ -767,7 +772,7 @@
 
     @pl.when(step < pl.num_programs(0) // 2)
     def _():
-        put(own_ref[...] + jnp.sum(got_ref[...].astype(F32), axis=0))
+        put(own_ref[...] + got_ref[...])
 
     @pl.when(step >= pl.num_programs(0) // 2)
     def _():
@@ -781,7 +786,7 @@
     return pl.pallas_call(
         token_back_kernel,
         grid=(rows // tile,),
-        in_specs=[block, pl.BlockSpec((got.shape[0], tile, width), lambda i: (0, jnp.minimum(i, half - 1), 0)), block, block,
+        in_specs=[block, pl.BlockSpec((tile, width), lambda i: (jnp.minimum(i, half - 1), 0)), block, block,
                   whole(gain.shape)],
         out_specs=block,
         out_shape=jax.ShapeDtypeStruct((rows, width), F32),
@@ -789,6 +794,189 @@
         cost_estimate=pl.CostEstimate(flops=10 * rows * width, bytes_accessed=14 * rows * width, transcendentals=0),
         name="token_back",
     )(own, got, x, dx2, gain)
+
+
+MESH = pl.DeviceIdType.MESH
+
+
+def padded_rows(rows, rest):
+    unit = 8 * rest * 16
+    return -(-rows // unit) * unit
+
+
+def sum_kernel(g_ref, small_ref, dh_ref, out_ref, small_out_ref, got_ref, half_ref, r0_ref, t1_ref, r1_ref, t2_ref, r2_ref,
+               r3_ref, sm_ref, rs_ref, rd0_ref, td_ref, rd1_ref, send_sem, recv_sem, *, rest, chunks):
+    dp, ex = lax.axis_index("dp"), lax.axis_index("expert")
+    c, x, y, z = ex % 2, ex // 2, dp % 2, dp // 2
+    mate = (dp, x * 2 + 1 - c)
+    across = (dp, (1 - x) * 2 + c)
+    beside = (z * 2 + 1 - y, ex)
+    ahead = [((z + d) % rest * 2 + y, ex) for d in range(1, rest)]
+
+    barrier = pltpu.get_barrier_semaphore()
+    for peer in [mate, across, beside] + ahead:
+        pl.semaphore_signal(barrier, inc=1, device_id=peer, device_id_type=MESH)
+    pl.semaphore_wait(barrier, 2 + rest)
+
+    started = []
+
+    def send(src, dst, peer):
+        n = len(started)
+        copy = pltpu.make_async_remote_copy(src_ref=src, dst_ref=dst, send_sem=send_sem.at[n], recv_sem=recv_sem.at[n],
+                                            device_id=peer, device_id_type=MESH)
+        copy.start()
+        started.append(copy)
+        return copy
+
+    rows, width = g_ref.shape
+    half = rows // 2
+    size = half // chunks
+    lanes = width // 2
+    q1, q2, q3 = size // 2, size // 4, size // 4 // rest
+    part = [pl.ds(0, lanes), pl.ds(lanes, lanes)]
+    first, second = [across, beside], [beside, across]
+    bit1, bit2 = [x, y], [y, x]
+
+    def ds(at, n):
+        return pl.ds(pl.multiple_of(at, 16), n)
+
+    def at1(k, p, bit):
+        return k * size + bit * q1
+
+    def spot2(k, p, bit):
+        return k * size + bit1[p] * q1 + bit * q2
+
+    def stage0(k):
+        return [send(g_ref.at[ds((1 - c) * half + k * size, size)], r0_ref.at[ds(k * size, size)], mate)]
+
+    def stage1(k):
+        sl = pl.ds(k * size, size)
+        half_ref[sl] = (g_ref[ds(c * half + k * size, size)].astype(F32) + r0_ref[sl].astype(F32)).astype(BF)
+        return [send(half_ref.at[ds(at1(k, p, 1 - bit1[p]), q1), part[p]], r1_ref.at[p, pl.ds(k * q1, q1)], first[p])
+                for p in range(2)]
+
+    def stage2(k):
+        out = []
+        for p in range(2):
+            sl = pl.ds(k * q1, q1)
+            t1_ref[p, sl] = (half_ref[ds(at1(k, p, bit1[p]), q1), part[p]].astype(F32) + r1_ref[p, sl].astype(F32)).astype(BF)
+            out.append(send(t1_ref.at[p, ds(k * q1 + (1 - bit2[p]) * q2, q2)], r2_ref.at[p, pl.ds(k * q2, q2)], second[p]))
+        return out
+
+    def stage3(k):
+        out = []
+        for p in range(2):
+            sl = pl.ds(k * q2, q2)
+            t2_ref[p, sl] = (t1_ref[p, ds(k * q1 + bit2[p] * q2, q2)].astype(F32) + r2_ref[p, sl].astype(F32)).astype(BF)
+            for d in range(1, rest):
+                to = (z + d) % rest
+                out.append(send(t2_ref.at[p, ds(k * q2 + to * q3, q3)], r3_ref.at[p, d - 1, pl.ds(k * q3, q3)], ahead[d - 1]))
+        return out
+
+    def stage4(k):
+        out = []
+        for p in range(2):
+            total = t2_ref[p, ds(k * q2 + z * q3, q3)].astype(F32)
+            for d in range(1, rest):
+                total = total + r3_ref[p, d - 1, pl.ds(k * q3, q3)].astype(F32)
+            mine = ds(c * half + spot2(k, p, bit2[p]) + z * q3, q3)
+            out_ref[mine, part[p]] = total.astype(BF)
+            for d in range(1, rest):
+                out.append(send(out_ref.at[mine, part[p]], out_ref.at[mine, part[p]], ahead[d - 1]))
+        return out
+
+    def stage5(k):
+        out = []
+        for p in range(2):
+            mine = ds(c * half + spot2(k, p, bit2[p]), q2)
+            out.append(send(out_ref.at[mine, part[p]], out_ref.at[mine, part[p]], second[p]))
+        return out
+
+    def stage6(k):
+        out = []
+        for p in range(2):
+            mine = ds(c * half + at1(k, p, bit1[p]), q1)
+            out.append(send(out_ref.at[mine, part[p]], out_ref.at[mine, part[p]], first[p]))
+        return out
+
+    def stage7(k):
+        mine = ds(c * half + k * size, size)
+        return [send(out_ref.at[mine], out_ref.at[mine], mate)]
+
+    block = got_ref.shape[0]
+
+    def dh_rows(xx, cc):
+        return ds((xx * 2 + cc) * block, block)
+
+    def dh0():
+        return [send(dh_ref.at[dh_rows(w, 1 - c)], rd0_ref.at[w], mate) for w in range(2)]
+
+    def dh1():
+        td_ref[...] = (dh_ref[dh_rows(1 - x, c)].astype(F32) + rd0_ref[1 - x].astype(F32)).astype(BF)
+        return [send(td_ref, rd1_ref, across)]
+
+    def dh2():
+        got_ref[...] = dh_ref[dh_rows(x, c)].astype(F32) + rd0_ref[x].astype(F32) + rd1_ref[...].astype(F32)
+        return []
+
+    def small_pair(n, peer):
+        def run():
+            if n:
+                sm_ref[n] = sm_ref[n - 1] + rs_ref[n - 1]
+            else:
+                sm_ref[0] = small_ref[...]
+            return [send(sm_ref.at[n], rs_ref.at[n], peer)]
+        return run
+
+    def small_rest():
+        sm_ref[3] = sm_ref[2] + rs_ref[2]
+        return [send(sm_ref.at[3], rs_ref.at[2 + d], ahead[d - 1]) for d in range(1, rest)]
+
+    def small_end():
+        total = sm_ref[3]
+        for d in range(1, rest):
+            total = total + rs_ref[2 + d]
+        small_out_ref[...] = total
+        return []
+
+    lines = [[functools.partial(f, k) for f in (stage0, stage1, stage2, stage3, stage4, stage5, stage6, stage7)]
+             for k in range(chunks)]
+    lines.insert(1, [dh0, dh1, dh2])
+    lines.append([small_pair(0, mate), small_pair(1, across), small_pair(2, beside), small_rest, small_end])
+    waiting = [[] for _ in lines]
+    for t in range(max(n + len(line) for n, line in enumerate(lines)) + 1):
+        for n, line in enumerate(lines):
+            s = t - n
+            if 0 <= s <= len(line):
+                for copy in waiting[n]:
+                    copy.wait_recv()
+                waiting[n] = line[s]() if s < len(line) else []
+    for copy in started:
+        copy.wait_send()
+
+
+def device_sums(g, small, dh, rest, block, chunks):
+    rows, width = g.shape
+    half, lanes = rows // 2, width // 2
+    copies = chunks * (1 + 2 + 2 + 2 * (rest - 1) * 2 + 2 + 2 + 1) + 3 + 3 + rest - 1
+    vm = pltpu.VMEM
+    vmem = pl.BlockSpec(memory_space=pltpu.VMEM)
+    return pl.pallas_call(
+        functools.partial(sum_kernel, rest=rest, chunks=chunks),
+        in_specs=[vmem] * 3,
+        out_specs=[vmem] * 3,
+        out_shape=[jax.ShapeDtypeStruct(g.shape, BF), jax.ShapeDtypeStruct(small.shape, F32),
+                   jax.ShapeDtypeStruct((block, width), F32)],
+        scratch_shapes=[
+            vm((half, width), BF), vm((half, width), BF), vm((2, half // 2, lanes), BF), vm((2, half // 2, lanes), BF),
+            vm((2, half // 4, lanes), BF), vm((2, half // 4, lanes), BF), vm((2, rest - 1, half // 4 // rest, lanes), BF),
+            vm((4,) + small.shape, F32), vm((2 + rest,) + small.shape, F32), vm((2, block, width), BF), vm((block, width), BF),
+            vm((block, width), BF), pltpu.SemaphoreType.DMA((copies,)), pltpu.SemaphoreType.DMA((copies,)),
+        ],
+        compiler_params=params(collective_id=0, has_side_effects=True),
+        cost_estimate=pl.CostEstimate(flops=4 * rows * width, bytes_accessed=8 * rows * width, transcendentals=0),
+        name="device_sums",
+    )(g, small, dh)
 
 
 def slot_table(routes_t, priority, groups, capacity):
@@ -852,32 +1040,31 @@
     mixed, grad_prev, dx2, da, do, cat, sums = combine(
         made, drow, slots, routes, aux, x2, h2, cotangent, gain2, wcat, const_v, w_out, experts
     )
-    grad_out = jnp.dot(o.T, da, preferred_element_type=F32).astype(BF)
     dq, dk, dv = attn_bwd(e, q, do, o, lse, k_own, v_own, k_prompt, v_prompt, cos, sin)
     dh_prompt, sum_p = prompt_back(dk, dv, w_key, w_value, prompt_x)
-    got = lax.all_to_all(
-        dh_prompt.reshape(expert_devices, prompt_dev, width), "expert", split_axis=0, concat_axis=0, tiled=True
-    )
     dh_own, sum_o = own_back(dq, dk, dv, w_query, w_key, w_value, tokens)
-    grad_w = weight_back(h_prompt, h_own, dq, dk, dv)
-    small = jnp.concatenate([cat[:experts + 4], sums[:3], sum_p + sum_o], axis=0).astype(BF)
-    grad_w, grad_out, small = lax.psum((grad_w, grad_out, small), everyone)
-    grad_w, grad_out, small = grad_w.astype(F32), grad_out.astype(F32), small.astype(F32)
+    rest = dp // 2
+    out_rows = padded_rows(4 * width, rest)
+    chunks = max(n for n in (1, 2, 3) if out_rows // 2 % (n * 4 * rest * 16) == 0)
+    grad_w = weight_back(h_prompt, h_own, o, da, dq, dk, dv, out_rows)
+    n = experts
+    small = jnp.concatenate([cat[:n + 4], sums[:3], sum_p + sum_o, jnp.zeros((4, width), F32)], axis=0)
+    grad_w, small, got = device_sums(grad_w, small, dh_prompt, rest, prompt_dev, chunks)
+    grad_w = grad_w.astype(F32)
     grad_tokens = token_back(dh_own, got, tokens, dx2, gain1)
 
     ffn_sum = ffn_sum.reshape(3, width, pair, -1).transpose(2, 0, 1, 3)
     ffn_sum = lax.all_to_all(ffn_sum, "dp", split_axis=0, concat_axis=0, axis_index_groups=pairs, tiled=True)
     ffn_sum = ffn_sum.astype(F32)
-    n = experts
     return (
         mixed,
         grad_tokens,
         grad_prev,
         small[n + 7],
-        grad_w[0],
-        grad_w[1],
-        grad_w[2],
-        grad_out,
+        grad_w[:width],
+        grad_w[width:2 * width],
+        grad_w[2 * width:3 * width],
+        grad_w[3 * width:4 * width],
         small[n + 6],
         small[:n].T,
         small[n:n + 4].reshape(2, 2, width).transpose(0, 2, 1),

time: 648 us -> 595 us (0.918)
  Pallas kernels: 303 us -> 418 us
  waiting for transfers between devices: 133 us -> 61.4 us
  blocking collectives: 86.8 us -> 33.6 us
  starting transfers between devices: 58.3 us -> 26 us
    pallas_call x0 -> x1, Pallas kernels: none -> 105 us  [device_sums(): pl.pallas_call(functools.partial(sum_kernel, rest=rest, chunks=chunks), i...]
    psum x1 -> x0, blocking collectives: 53.2 us -> none  [local(): grad_w, grad_out, small = lax.psum((grad_w, grad_out, small), everyone)]
    psum x1 -> x0, waiting for transfers between devices: 52.7 us -> none  [local(): grad_w, grad_out, small = lax.psum((grad_w, grad_out, small), everyone)]
    all_to_all x1 -> x0, starting transfers between devices: 20.7 us -> none  [local(): lax.all_to_all(dh_prompt.reshape(expert_devices, prompt_dev, width), 'exp...]
    all_to_all x1 -> x0, waiting for transfers between devices: 18.9 us -> none  [local(): lax.all_to_all(dh_prompt.reshape(expert_devices, prompt_dev, width), 'exp...]
    all_to_all x3, starting transfers between devices: 32.5 us -> 21.9 us  [swap(): lax.all_to_all(x, everyone, split_axis=0, concat_axis=0, axis_index_group...]
    pallas_call x1, Pallas kernels: 63.3 us -> 71.8 us  [attn_bwd(): pl.pallas_call(functools.partial(attn_bwd_kernel, tile=tile, scale=0.125)...]
  transfers between devices with their start and end apart: 8 -> 6, of which waited for: 5 -> 3; matrix products, arithmetic and copies ran while one was open for 5% -> 4% of each run, Pallas kernels for 27% -> 49%
where the time goes in v2:
time: 595 us; the launch traced here: 589 us
  Pallas kernels  418 us (70%)
  waiting for transfers between devices  61.4 us (10%)
  blocking collectives  33.6 us (6%)
  local copies, waits for them, and re-layouts  29 us (5%)
  starting transfers between devices  26 us (4%)
  between operations  14.6 us (2%)
    pallas_call x1, Pallas kernels, device_sums(): pl.pallas_call(functools.partial(sum_kernel, rest=rest, chunks=chunks), i...  105 us
    pallas_call x1, Pallas kernels, attn_bwd(): pl.pallas_call(functools.partial(attn_bwd_kernel, tile=tile, scale=0.125)...  71.8 us
    all_to_all x3, waiting for transfers between devices, swap(): lax.all_to_all(x, everyone, split_axis=0, concat_axis=0, axis_index_group...  45.7 us
    pallas_call x1, Pallas kernels, attn_fwd(): pl.pallas_call(functools.partial(attn_fwd_kernel, chunk=chunk, tile=tile,...  44.6 us
    pallas_call x1, Pallas kernels, ffn_bwd(): pl.pallas_call(ffn_bwd_kernel, grid_spec=pltpu.PrefetchScalarGridSpec(num...  36 us
    all_to_all x1, blocking collectives, swap(): lax.all_to_all(x, everyone, split_axis=0, concat_axis=0, axis_index_group...  33.6 us
    pallas_call x1, Pallas kernels, ffn_fwd(): pl.pallas_call(ffn_fwd_kernel, grid_spec=pltpu.PrefetchScalarGridSpec(num...  26.9 us
    pallas_call x1, Pallas kernels, combine(): pl.pallas_call(functools.partial(combine_kernel, experts=experts), grid=(...  22.8 us
  transfers between devices with their start and end apart: 6, of which 3 were waited for; matrix products, arithmetic and copies ran while one was open for 4% of the time, Pallas kernels for 49%

profile of v2, /device:TPU:9, one launch (start us, length us, event | category | flops | bytes accessed | tf_op | source)
XLA Modules:
  0.0 589.4 jit_solution(5236878065003039329)
XLA Ops:
  15.9 8.8 %project_own.1 = (bf16[1024,768]{1,0:T(8,128)(2,1)}, bf16[1024,768]{1,0:T(8,128)(2,1)}, bf16[1024,768]{1,0:T(8,128)(2,1)}, bf16[1024,768]{1,0:T(8,128)(2,1)}) custom-call(s32[1]{0:T(128)} %bitcast.2.e_ref, bf16[1024,768]{1,0:T(8,128)(2,1)} %x_ref.7, f32[1,768]{1,0:T(1,128)} %broadcast_in_dim.33.gain_ref, bf16[768,768]{1,0:T(8,128)(2,1)} %wq_ref.1, ...), custom_call_target="tpu_custom_call" | custom-call | flops 3623878656 | bytes 9437184 | tf_op jit(solution)/shard_map/project_own/pallas_call | solution.py:91
  24.7 15.7 %all-gather.2.cloned.1.call-done.x_ref = bf16[2048,768]{1,0:T(8,128)(2,1)} async-done(((bf16[512,768]{1,0:T(8,128)(2,1)}), bf16[2048,768]{1,0:T(8,128)(2,1)}) %all-gather.2.cloned.1.call-update) | async-done | bytes 3145744 | tf_op jit(solution)/shard_map/all_gather | solution.py:1019
  40.4 11.7 %project_prompt.1 = (bf16[2048,768]{1,0:T(8,128)(2,1)}, bf16[2048,768]{1,0:T(8,128)(2,1)}, bf16[2048,768]{1,0:T(8,128)(2,1)}) custom-call(s32[1]{0:T(128)} %bitcast.2.e_ref, bf16[2048,768]{1,0:T(8,128)(2,1)} %all-gather.2.cloned.1.call-done.x_ref, f32[1,768]{1,0:T(1,128)} %broadcast_in_dim.33.gain_ref, bf16[768,768]{1,0:T(8,128)(2,1)} %wk_ref.3, ...), custom_call_target="tpu_custom_call" | custom-call | flops 4831838208 | bytes 18874368 | tf_op jit(solution)/shard_map/project_prompt/pallas_call | solution.py:91
  52.0 44.6 %attn_fwd.1 = (bf16[1024,768]{1,0:T(8,128)(2,1)}, f32[6,2,1024]{2,1,0:T(2,128)}) custom-call(s32[1]{0:T(128)} %bitcast.2.e_ref, bf16[1024,768]{1,0:T(8,128)(2,1)} %get-tuple-element.53.q_ref, bf16[1024,768]{1,0:T(8,128)(2,1)} %get-tuple-element.54.ko_ref, bf16[1024,768]{1,0:T(8,128)(2,1)} %get-tuple-element.55.vo_ref, ...), custom_call_target="tpu_custom_call" | custom-call | flops 12884901888 | bytes 12582912 | tf_op jit(solution)/shard_map/attn_fwd/pallas_call | solution.py:188
  96.7 7.4 %gates.1 = (f32[1024,768]{1,0:T(8,128)}, bf16[1024,768]{1,0:T(8,128)(2,1)}, f32[1024,128]{1,0:T(8,128)}, bf16[1024,256]{1,0:T(8,128)(2,1)}) custom-call(bf16[1024,768]{1,0:T(8,128)(2,1)} %x_ref.7, bf16[1024,768]{1,0:T(8,128)(2,1)} %get-tuple-element.58.o_ref, bf16[768,768]{1,0:T(8,128)(2,1)} %w_ref.3, f32[1,768]{1,0:T(1,128)} %broadcast_in_dim.34.gain_ref, ...), custom_call_target="tpu_custom_call" | custom-call | flops 1207959552 | bytes 9437184 | tf_op jit(solution)/shard_map/gates/pallas_call | solution.py:379
  104.1 8.0 %dispatch_rows.1 = bf16[8,192,896]{2,1,0:T(8,128)(2,1)} custom-call(s32[2,1024]{1,0:T(2,128)} %copy.127.slot_ref, bf16[1024,768]{1,0:T(8,128)(2,1)} %get-tuple-element.59.rows_ref.h2_ref, bf16[1024,256]{1,0:T(8,128)(2,1)} %get-tuple-element.60.refs_0_), custom_call_target="tpu_custom_call" | custom-call | flops 2415919104 | bytes 3145728 | tf_op jit(solution)/shard_map/dispatch_rows/pallas_call | solution.py:407
  112.1 9.5 %all-to-all-start = ((bf16[8,192,896]{2,1,0:T(8,128)(2,1)}), bf16[8,192,896]{2,1,0:T(8,128)(2,1)}, u32[]{:S(2)}, u32[]{:S(2)}) async-start(bf16[8,192,896]{2,1,0:T(8,128)(2,1)} %dispatch_rows.1), calls=%async_computation | async-start | bytes 5505024 | tf_op jit(solution)/shard_map/all_to_all | solution.py:1014
  121.6 6.8 %dispatch_grads.1 = bf16[8,192,768]{2,1,0:T(8,128)(2,1)} custom-call(s32[2,1024]{1,0:T(2,128)} %copy.127.slot_ref, bf16[1024,768]{1,0:T(8,128)(2,1)} %g_ref.1), custom_call_target="tpu_custom_call" | custom-call | flops 2415919104 | bytes 3145728 | tf_op jit(solution)/shard_map/dispatch_grads/pallas_call | solution.py:407
  128.3 23.4 %all-to-all-done = bf16[8,192,896]{2,1,0:T(8,128)(2,1)} async-done(((bf16[8,192,896]{2,1,0:T(8,128)(2,1)}), bf16[8,192,896]{2,1,0:T(8,128)(2,1)}, u32[]{:S(2)}, u32[]{:S(2)}) %all-to-all-start) | async-done | bytes 2752544 | tf_op jit(solution)/shard_map/all_to_all | solution.py:1014
  151.8 7.4 %all-to-all-start.2 = ((bf16[8,192,768]{2,1,0:T(8,128)(2,1)}), bf16[8,192,768]{2,1,0:T(8,128)(2,1)S(1)}, u32[]{:S(2)}, u32[]{:S(2)}) async-start(bf16[8,192,768]{2,1,0:T(8,128)(2,1)} %dispatch_grads.1), calls=%async_computation.2 | async-start | bytes 4718592 | tf_op jit(solution)/shard_map/all_to_all | solution.py:1014
  159.5 26.9 %ffn_fwd.1 = (bf16[1536,2048]{1,0:T(8,128)(2,1)}, bf16[1536,2048]{1,0:T(8,128)(2,1)}, bf16[1536,2048]{1,0:T(8,128)(2,1)}, bf16[1536,768]{1,0:T(8,128)(2,1)}) custom-call(s32[1]{0:T(128)} %bitcast.j_ref, bf16[1536,896]{1,0:T(8,128)(2,1)} %bitcast.4.a_ref, bf16[2,768,2048]{2,1,0:T(8,128)(2,1)} %wg_ref.3, bf16[2,768,2048]{2,1,0:T(8,128)(2,1)} %wu_ref.3, ...), custom_call_target="tpu_custom_call" | custom-call | flops 14495514624 | bytes 28311552 | tf_op jit(solution)/shard_map/ffn_fwd/pallas_call | solution.py:452
  187.8 36.0 %ffn_bwd.1 = (bf16[1536,2048]{1,0:T(8,128)(2,1)}, bf16[1536,2048]{1,0:T(8,128)(2,1)}, bf16[1536,768]{1,0:T(8,128)(2,1)}, bf16[1536,768]{1,0:T(8,128)(2,1)}) custom-call(s32[1]{0:T(128)} %bitcast.j_ref, bf16[1536,768]{1,0:T(8,128)(2,1)} %bitcast.44, bf16[1536,896]{1,0:T(8,128)(2,1)} %bitcast.4.a_ref, bf16[1536,2048]{1,0:T(8,128)(2,1)} %get-tuple-element.62.act_ref, ...), custom_call_target="tpu_custom_call" | custom-call | flops 14495514624 | bytes 34603008 | tf_op jit(solution)/shard_map/ffn_bwd/pallas_call | solution.py:503
  223.8 22.1 %ffn_grad.1 = bf16[3,768,2048]{2,1,0:T(8,128)(2,1)} custom-call(bf16[1536,896]{1,0:T(8,128)(2,1)} %bitcast.4.a_ref, bf16[1536,768]{1,0:T(8,128)(2,1)} %get-tuple-element.87.dout_ref, bf16[1536,2048]{1,0:T(8,128)(2,1)} %get-tuple-element.88.hid_ref, bf16[1536,2048]{1,0:T(8,128)(2,1)} %get-tuple-element.89.dg_ref, bf16[1536,2048]{1,0:T(8,128)(2,1)} %get-tuple-element.90.du_ref), custom_call_target="tpu_custom_call" | custom-call | flops 14495514624 | bytes 28311552 | tf_op jit(solution)/shard_map/ffn_grad/pallas_call | solution.py:535
  247.6 33.6 %all_to_all.25 = bf16[8,192,768]{2,1,0:T(8,128)(2,1)} all-to-all(bf16[8,192,768]{2,1,0:T(8,128)(2,1)S(1)} %bitcast.47), channel_id=1, replica_groups={{0,1,2,3,4,5,6,7},{8,9,10,11,12,13,14,15},{16,17,18,19,20,21,22,23},{24..., dimensions={0} | all-to-all | bytes 4718592 | tf_op jit(solution)/shard_map/all_to_all | solution.py:1014
  281.2 5.0 all-to-all-start.1
  289.8 22.3 %all-to-all-done.1 = bf16[8,192,768]{2,1,0:T(8,128)(2,1)S(1)} async-done(((bf16[8,192,768]{2,1,0:T(8,128)(2,1)}), bf16[8,192,768]{2,1,0:T(8,128)(2,1)S(1)}, u32[]{:S(2)}, u32[]{:S(2)}) %all-to-all-start.1) | async-done | bytes 2359328 | tf_op jit(solution)/shard_map/all_to_all | solution.py:1014
  313.5 22.8 %combine.1 = (bf16[1024,768]{1,0:T(8,128)(2,1)}, f32[1024,12]{1,0:T(8,128)}, f32[1024,768]{1,0:T(8,128)}, bf16[1024,768]{1,0:T(8,128)(2,1)}, bf16[1024,768]{1,0:...) custom-call(bf16[1536,768]{1,0:T(8,128)(2,1)} %bitcast.46, bf16[1536,768]{1,0:T(8,128)(2,1)} %bitcast.45, ...), custom_call_target="tpu_custom_call" | custom-call | flops 9663676416 | bytes 23592960 | tf_op jit(solution)/shard_map/combine/pallas_call | solution.py:622
  337.9 71.8 %attn_bwd.1 = (bf16[1024,768]{1,0:T(8,128)(2,1)}, bf16[2560,768]{1,0:T(8,128)(2,1)}, bf16[2560,768]{1,0:T(8,128)(2,1)}) custom-call(s32[1]{0:T(128)} %bitcast.2.e_ref, bf16[1024,768]{1,0:T(8,128)(2,1)} %get-tuple-element.53.q_ref, bf16[1024,768]{1,0:T(8,128)(2,1)} %get-tuple-element.68.do_ref, bf16[1024,768]{1,0:T(8,128)(2,1)} %get-tuple-element.58.o_ref, ...), custom_call_target="tpu_custom_call" | custom-call | flops 32212254720 | bytes 25165824 | tf_op jit(solution)/shard_map/attn_bwd/pallas_call | solution.py:319
  409.7 11.5 %prompt_back.1 = (bf16[2048,768]{1,0:T(8,128)(2,1)}, f32[1,768]{1,0:T(1,128)}) custom-call(bf16[2560,768]{1,0:T(8,128)(2,1)} %get-tuple-element.71.dk_ref, bf16[2560,768]{1,0:T(8,128)(2,1)} %get-tuple-element.72.dv_ref, bf16[768,768]{1,0:T(8,128)(2,1)} %wk_ref.3, bf16[768,768]{1,0:T(8,128)(2,1)} %wv_ref.3, bf16[2048,768]{1,0:T(8,128)(2,1)} %all-gather.2.cloned.1.call-done.x_ref), custom_call_target="tpu_custom_call" | custom-call | flops 4831838208 | bytes 12582912 | tf_op jit(solution)/shard_map/prompt_back/pallas_call | solution.py:657
  421.2 19.0 %weight_back.1.g_ref = bf16[3072,768]{1,0:T(8,128)(2,1)} custom-call(bf16[2048,768]{1,0:T(8,128)(2,1)} %get-tuple-element.74.hp_ref, bf16[1024,768]{1,0:T(8,128)(2,1)} %get-tuple-element.75.ho_ref, bf16[1024,768]{1,0:T(8,128)(2,1)} %get-tuple-element.58.o_ref, bf16[1024,768]{1,0:T(8,128)(2,1)} %get-tuple-element.76.da_ref, ...), custom_call_target="tpu_custom_call" | custom-call | flops 9663676416 | bytes 11010048 | tf_op jit(solution)/shard_map/weight_back/pallas_call | solution.py:750
  447.2 8.4 %own_back.1 = (f32[1024,768]{1,0:T(8,128)}, f32[1,768]{1,0:T(1,128)}) custom-call(bf16[1024,768]{1,0:T(8,128)(2,1)} %get-tuple-element.70.dq_ref, bf16[2560,768]{1,0:T(8,128)(2,1)} %get-tuple-element.71.dk_ref, bf16[2560,768]{1,0:T(8,128)(2,1)} %get-tuple-element.72.dv_ref, bf16[768,768]{1,0:T(8,128)(2,1)} %wq_ref.1, bf16[768,768]{1,0:T(8,128)(2,1)} %wk_ref.3, ...), custom_call_target="tpu_custom_call" | custom-call | flops 2415919104 | bytes 6291456 | tf_op jit(solution)/shard_map/own_back/pallas_call | solution.py:697
  457.0 105.5 %device_sums.1 = (bf16[3072,768]{1,0:T(8,128)(2,1)}, f32[24,768]{1,0:T(8,128)}, f32[512,768]{1,0:T(8,128)}) custom-call(bf16[3072,768]{1,0:T(8,128)(2,1)} %weight_back.1.g_ref, f32[24,768]{1,0:T(8,128)} %maximum_maximum_fusion.1.small_ref, bf16[2048,768]{1,0:T(8,128)(2,1)} %get-tuple-element.81.dh_ref), custom_call_target="tpu_custom_call" | custom-call | flops 9437184 | bytes 18874368 | tf_op jit(solution)/shard_map/device_sums/pallas_call | solution.py:964
  566.0 7.0 %token_back.1 = f32[1024,768]{1,0:T(8,128)} custom-call(f32[1024,768]{1,0:T(8,128)} %get-tuple-element.73.own_ref, f32[512,768]{1,0:T(8,128)} %get-tuple-element.82.got_ref, bf16[1024,768]{1,0:T(8,128)(2,1)} %x_ref.7, f32[1024,768]{1,0:T(8,128)} %get-tuple-element.83.dx2_ref, f32[1,768]{1,0:T(1,128)} %broadcast_in_dim.33.gain_ref), custom_call_target="tpu_custom_call" | custom-call | flops 7864320 | bytes 11010048 | tf_op jit(solution)/shard_map/token_back/pallas_call | solution.py:786
  574.3 3.8 fusion.25
  (82 shorter events, 35.8 us)
Async XLA Ops:
  7.2 2.2 copy-start.11
  7.2 2.8 copy-start.8
  7.2 3.0 copy-start.10
  7.2 3.2 copy-start.9
  7.2 3.4 copy-start.12
  7.2 4.0 copy-start.7
  7.2 4.4 copy-start.14
  7.3 33.1 %all-gather.2.cloned.1.call-start = ((), (), s32[]{:S(2)}) async-start(), calls=%async_computation.6 | async-start | bytes 3932160 | tf_op jit(solution)/shard_map/all_gather | solution.py:1019
  10.2 3.1 copy-start
  112.1 39.7 %all-to-all-start = ((bf16[8,192,896]{2,1,0:T(8,128)(2,1)}), bf16[8,192,896]{2,1,0:T(8,128)(2,1)}, u32[]{:S(2)}, u32[]{:S(2)}) async-start(bf16[8,192,896]{2,1,0:T(8,128)(2,1)} %dispatch_rows.1), calls=%async_computation | async-start | bytes 5505024 | tf_op jit(solution)/shard_map/all_to_all | solution.py:1014
  151.8 34.6 %all-to-all-start.2 = ((bf16[8,192,768]{2,1,0:T(8,128)(2,1)}), bf16[8,192,768]{2,1,0:T(8,128)(2,1)S(1)}, u32[]{:S(2)}, u32[]{:S(2)}) async-start(bf16[8,192,768]{2,1,0:T(8,128)(2,1)} %dispatch_grads.1), calls=%async_computation.2 | async-start | bytes 4718592 | tf_op jit(solution)/shard_map/all_to_all | solution.py:1014
  159.2 281.0 %reduce-scatter.2.cloned.1.call-start = ((), (), s32[]{:S(2)}) async-start(), calls=%async_computation.7 | async-start | bytes 11796480 | tf_op jit(solution)/shard_map/reduce_scatter | solution.py:1038
  186.4 1.4 copy-start.2
  245.9 1.7 copy-start.4
  281.2 6.3 %copy-start.1 = (s32[1024,2]{1,0:T(8,128)S(1)}, s32[1024,2]{1,0:T(8,128)}, u32[]{:S(2)}) copy-start(s32[1024,2]{1,0:T(8,128)} %copy-done) | copy-start | bytes 24580
  281.2 30.9 %all-to-all-start.1 = ((bf16[8,192,768]{2,1,0:T(8,128)(2,1)}), bf16[8,192,768]{2,1,0:T(8,128)(2,1)S(1)}, u32[]{:S(2)}, u32[]{:S(2)}) async-start(bf16[8,192,768]{2,1,0:T(8,128)(2,1)} %bitcast.5), calls=%async_computation.1 | async-start | bytes 4718592 | tf_op jit(solution)/shard_map/all_to_all | solution.py:1014
  312.1 1.4 copy-start.3
  443.4 134.7 %all-to-all-start.4 = ((bf16[2,3,768,256]{3,2,1,0:T(8,128)(2,1)}), bf16[2,3,768,256]{3,2,1,0:T(8,128)(2,1)S(1)}, u32[]{:S(2)}, u32[]{:S(2)}) async-start(bf16[2,3,768,256]{3,2,1,0:T(8,128)(2,1)} %bitcast.42), calls=%async_computation.5 | async-start | bytes 4718592 | tf_op jit(solution)/shard_map/all_to_all | solution.py:1057
  447.2 8.4 %copy-start.13 = (f32[1,768]{1,0:T(1,128)S(1)}, f32[1,768]{1,0:T(1,128)}, u32[]{:S(2)}) copy-start(f32[1,768]{1,0:T(1,128)} %get-tuple-element.79) | copy-start | bytes 9220
  457.0 108.2 %copy-start.5 = (f32[1024,12]{1,0:T(8,128)S(1)}, f32[1024,12]{1,0:T(8,128)}, u32[]{:S(2)}) copy-start(f32[1024,12]{1,0:T(8,128)} %get-tuple-element.153) | copy-start | bytes 147460
  566.0 8.3 %slice-start = ((s8[4718592]{0:T(1024)(128)(4,1)}), s8[4194304]{0:T(1024)(128)(4,1)S(1)}, s32[]{:S(2)}) async-start(s8[4718592]{0:T(1024)(128)(4,1)} %bitcast.39), calls=%async_computation.8 | async-start | bytes 8388608
  566.0 7.0 %copy-start.6 = (f32[24,768]{1,0:T(8,128)S(1)}, f32[24,768]{1,0:T(8,128)}, u32[]{:S(2)}) copy-start(f32[24,768]{1,0:T(8,128)} %get-tuple-element.85) | copy-start | bytes 221188
  566.0 8.3 %slice-start.1 = ((s8[4718592]{0:T(1024)(128)(4,1)}), s8[524288]{0:T(1024)(128)(4,1)S(1)}, s32[]{:S(2)}) async-start(s8[4718592]{0:T(1024)(128)(4,1)} %bitcast.39), calls=%async_computation.9 | async-start | bytes 1048576
Sparse Core Ops, SparseCore 0:
  10.2 30.0 all-gather.1
  246.1 161.9 reduce-scatter.1

commit v3 on v2

--- a/solution.py
+++ b/solution.py
@@ -334,6 +334,9 @@
     )(e, q, do, o, lse, ko, vo, kp, vp, cos, sin)
 
 
+MESH = pl.DeviceIdType.MESH
+
+
 def pick(values, lane, index):
     return jnp.sum(jnp.where(lane == index, values, 0.0), axis=1, keepdims=True)
 
@@ -390,160 +393,179 @@
     )(x, o, w_out, gain, wcat, prev, routes)
 
 
-def dispatch_kernel(slot_ref, rows_ref, *refs, capacity):
-    out_ref = refs[-1]
-    width = rows_ref.shape[1]
+def dispatch_kernel(slot_ref, rows_ref, out_ref, *, capacity):
     ids = pl.program_id(0) * capacity + lax.broadcasted_iota(jnp.int32, (capacity, 1), 0)
     hot = [jnp.where(ids == slot_ref[k:k + 1, :], 1.0, 0.0).astype(BF) for k in range(2)]
-    out_ref[0, :, :width] = dot(hot[0] + hot[1], rows_ref[...]).astype(BF)
-    if len(refs) > 1:
-        out_ref[0, :, width:] = (dot(hot[0], refs[0][:, :128]) + dot(hot[1], refs[0][:, 128:])).astype(BF)
-
-
-def dispatch(slots, rows, ext, destinations, capacity):
+    out_ref[0] = dot(hot[0] + hot[1], rows_ref[...]).astype(BF)
+
+
+def dispatch(slots, rows, destinations, capacity):
     count, width = rows.shape
-    extra = () if ext is None else (ext,)
-    out_width = width + (128 if extra else 0)
     return pl.pallas_call(
         functools.partial(dispatch_kernel, capacity=capacity),
         grid=(destinations,),
-        in_specs=[whole(slots.shape), whole(rows.shape)] + [whole(a.shape) for a in extra],
-        out_specs=pl.BlockSpec((1, capacity, out_width), lambda i: (i, 0, 0)),
-        out_shape=jax.ShapeDtypeStruct((destinations, capacity, out_width), BF),
+        in_specs=[whole(slots.shape), whole(rows.shape)],
+        out_specs=pl.BlockSpec((1, capacity, width), lambda i: (i, 0, 0)),
+        out_shape=jax.ShapeDtypeStruct((destinations, capacity, width), BF),
         compiler_params=params(),
         cost_estimate=pl.CostEstimate(flops=2 * destinations * capacity * count * width, bytes_accessed=4 * count * width,
                                       transcendentals=0),
-        name="dispatch_rows" if extra else "dispatch_grads",
-    )(slots, rows, *extra)
-
-
-def ffn_fwd_kernel(j_ref, a_ref, wg_ref, wu_ref, wd_ref, hid_ref, act_ref, slope_ref, out_ref, acc_ref):
-    width = wg_ref.shape[1]
-    a = a_ref[:, :width]
-    gate, up = dot(a, wg_ref[0]), dot(a, wu_ref[0])
-    sig = jax.nn.sigmoid(gate)
-    act = gate * sig
-    hidden = (act * up).astype(BF)
-    hid_ref[...] = hidden
-    act_ref[...] = act.astype(BF)
-    slope_ref[...] = (up * sig * (1.0 + gate * (1.0 - sig))).astype(BF)
-    made = dot(hidden, wd_ref[0])
-    step = pl.program_id(0)
-
-    @pl.when(step == 0)
-    def _():
-        acc_ref[...] = made
-
-    @pl.when(step > 0)
-    def _():
-        acc_ref[...] += made
-
-    @pl.when(step == pl.num_programs(0) - 1)
-    def _():
-        out_ref[...] = acc_ref[...].astype(BF)
-
-
-def ffn_fwd(j, a, w_gate, w_up, w_down, tile=256):
-    rows = a.shape[0]
-    _, width, ff = w_gate.shape
-    col = pl.BlockSpec((1, width, tile), lambda i, j: (j[0], 0, i))
-    row = pl.BlockSpec((1, tile, width), lambda i, j: (j[0], i, 0))
-    mid = pl.BlockSpec((rows, tile), lambda i, j: (0, i))
+        name="dispatch_grads",
+    )(slots, rows)
+
+
+def expert_kernel(slot_ref, h2_ref, ext_ref, g_ref, wg_hbm, wu_hbm, wd_hbm, made_hbm, back_hbm, grad_hbm,
+                  wg_ref, wu_ref, wd_ref, a_ref, s_ref, b_ref, d_ref, at_ref, dt_ref, hid_ref, dg_ref, du_ref, macc_ref,
+                  bacc_ref, out_ref, send_sem, recv_sem, local_sem, out_sem, *, capacity, tile, grad_tile):
+    dp, ex = lax.axis_index("dp"), lax.axis_index("expert")
+    j, c, x = dp % 2, ex % 2, ex // 2
+    width = h2_ref.shape[1]
+    ff = wg_ref.shape[1]
+    loads = [pltpu.make_async_copy(src.at[j], dst, local_sem.at[n])
+             for n, (src, dst) in enumerate(((wg_hbm, wg_ref), (wu_hbm, wu_ref), (wd_hbm, wd_ref)))]
+    for copy in loads:
+        copy.start()
+
+    def flip(bit, by):
+        return bit + by * (1 - 2 * bit)
+
+    def peer(r):
+        return dp + (r // 2 % 2) * (1 - 2 * j), flip(x, r // 4) * 2 + flip(c, r % 2)
+
+    def place(r):
+        return flip(j, r // 2 % 2) * 4 + flip(x, r // 4) * 2 + flip(c, r % 2)
+
+    barrier = pltpu.get_barrier_semaphore()
+    for r in range(1, 8):
+        pl.semaphore_signal(barrier, inc=1, device_id=peer(r), device_id_type=MESH)
+    pl.semaphore_wait(barrier, 7)
+
+    def send(src, dst, kind, r):
+        n = kind * 8 + r
+        copy = pltpu.make_async_remote_copy(src_ref=src, dst_ref=dst, send_sem=send_sem.at[n], recv_sem=recv_sem.at[n],
+                                            device_id=peer(r), device_id_type=MESH)
+        copy.start()
+        return copy
+
+    rows = {}
+    for r in (4, 5, 6, 7, 2, 3, 1, 0):
+        ids = place(r) * capacity + lax.broadcasted_iota(jnp.int32, (capacity, 1), 0)
+        hot = [jnp.where(ids == slot_ref[k:k + 1, :], 1.0, 0.0).astype(BF) for k in range(2)]
+        into = s_ref if r else a_ref
+        into[r, :, :width] = dot(hot[0] + hot[1], h2_ref[...]).astype(BF)
+        into[r, :, width:] = (dot(hot[0], ext_ref[:, :128]) + dot(hot[1], ext_ref[:, 128:])).astype(BF)
+        if r:
+            rows[r] = send(s_ref.at[r], a_ref.at[r], 0, r)
+
+    for copy in loads:
+        copy.wait()
+    returned, kept = [], []
+    mine = pl.ds(pl.multiple_of(place(0) * capacity, 16), capacity)
+    two = 2 * capacity
+    for n, first in enumerate((0, 4, 6, 2)):
+        for r in (first, first + 1):
+            if r:
+                rows[r].wait_recv()
+            got = a_ref[r]
+            half = pl.ds((r - first) * capacity, capacity)
+            gate = jnp.sum(got[:, width:].astype(F32), axis=1, keepdims=True)
+            g = g_ref[pl.ds(pl.multiple_of(place(r) * capacity, 16), capacity), :].astype(F32)
+            d_ref[half, :] = (g * gate).astype(BF)
+        span = pl.ds(n * two, two)
+        a = a_ref[first:first + 2, :, :width].reshape(two, width)
+        at_ref[:, span] = a.T
+        dt_ref[:, span] = d_ref[...].T
+        macc_ref[...] = jnp.zeros_like(macc_ref)
+        bacc_ref[...] = jnp.zeros_like(bacc_ref)
+
+        @pl.loop(0, ff // tile)
+        def _(i):
+            cols = pl.ds(pl.multiple_of(i * tile, tile), tile)
+            a = a_ref[first:first + 2, :, :width].reshape(two, width)
+            gate, up = dot(a, wg_ref[:, cols]), dot(a, wu_ref[:, cols])
+            dh = dot(d_ref[...], wd_ref[cols, :], NT)
+            sig = jax.nn.sigmoid(gate)
+            act = gate * sig
+            hidden = (act * up).astype(BF)
+            du = (dh * act).astype(BF)
+            dg = (dh * up * sig * (1.0 + gate * (1.0 - sig))).astype(BF)
+            hid_ref[span, cols] = hidden
+            du_ref[span, cols] = du
+            dg_ref[span, cols] = dg
+            macc_ref[...] += dot(hidden, wd_ref[cols, :])
+            bacc_ref[...] += dot(dg, wg_ref[:, cols], NT) + dot(du, wu_ref[:, cols], NT)
+
+        for r in (first, first + 1):
+            half = pl.ds((r - first) * capacity, capacity)
+            if r:
+                rows[r].wait_send()
+            s_ref[r, :, :width] = macc_ref[half, :].astype(BF)
+            b_ref[r] = bacc_ref[half, :].astype(BF)
+            made = s_ref.at[r, :, pl.ds(0, width)]
+            if r:
+                returned.append(send(made, made_hbm.at[mine], 1, r))
+                returned.append(send(b_ref.at[r], back_hbm.at[mine], 2, r))
+            else:
+                kept += [pltpu.make_async_copy(made, made_hbm.at[mine], local_sem.at[3]),
+                         pltpu.make_async_copy(b_ref.at[r], back_hbm.at[mine], local_sem.at[4])]
+                for copy in kept:
+                    copy.start()
+
+    steps = ff // grad_tile
+
+    def put(i, slot):
+        cols = pl.ds(pl.multiple_of(i * grad_tile, grad_tile), grad_tile)
+        return pltpu.make_async_copy(out_ref.at[slot], grad_hbm.at[:, :, cols], out_sem.at[slot])
+
+    @pl.loop(0, steps)
+    def _(i):
+        slot = i % 2
+
+        @pl.when(i >= 2)
+        def _():
+            put(i - 2, slot).wait()
+
+        cols = pl.ds(pl.multiple_of(i * grad_tile, grad_tile), grad_tile)
+        out_ref[slot, 0] = dot(at_ref[...], dg_ref[:, cols]).astype(BF)
+        out_ref[slot, 1] = dot(at_ref[...], du_ref[:, cols]).astype(BF)
+        out_ref[slot, 2] = dot(dt_ref[...], hid_ref[:, cols]).astype(BF)
+        put(i, slot).start()
+
+    for i in range(max(steps - 2, 0), steps):
+        put(i, i % 2).wait()
+    for copy in kept:
+        copy.wait()
+    for copy in returned:
+        copy.wait_recv()
+        copy.wait_send()
+
+
+def experts_on_rows(slots, h2, ext, g, w_gate, w_up, w_down, capacity, tile=512, grad_tile=256):
+    width = h2.shape[1]
+    ff = w_gate.shape[2]
+    total = 8 * capacity
+    vm = pltpu.VMEM
+    vmem, hbm = pl.BlockSpec(memory_space=pltpu.VMEM), pl.BlockSpec(memory_space=pl.ANY)
     return pl.pallas_call(
-        ffn_fwd_kernel,
-        grid_spec=pltpu.PrefetchScalarGridSpec(
-            num_scalar_prefetch=1, grid=(ff // tile,),
-            in_specs=[whole(a.shape), col, col, row],
-            out_specs=[mid, mid, mid, whole((rows, width))],
-            scratch_shapes=[pltpu.VMEM((rows, width), F32)]),
-        out_shape=[jax.ShapeDtypeStruct((rows, ff), BF)] * 3 + [jax.ShapeDtypeStruct((rows, width), BF)],
-        compiler_params=params(),
-        cost_estimate=pl.CostEstimate(flops=6 * rows * width * ff, bytes_accessed=6 * rows * ff + 6 * width * ff,
-                                      transcendentals=rows * ff),
-        name="ffn_fwd",
-    )(j, a, w_gate, w_up, w_down)
-
-
-def ffn_bwd_kernel(j_ref, g_ref, a_ref, act_ref, slope_ref, wg_ref, wu_ref, wd_ref, dg_ref, du_ref, dout_ref, drow_ref, acc_ref):
-    width = g_ref.shape[1]
-    step = pl.program_id(0)
-
-    @pl.when(step == 0)
-    def _():
-        gate = jnp.sum(a_ref[...].astype(F32), axis=1, keepdims=True)
-        dout_ref[...] = (g_ref[...].astype(F32) * gate).astype(BF)
-
-    dh = dot(dout_ref[...], wd_ref[0], NT)
-    du = (dh * act_ref[...].astype(F32)).astype(BF)
-    dg = (dh * slope_ref[...].astype(F32)).astype(BF)
-    du_ref[...] = du
-    dg_ref[...] = dg
-    back = dot(dg, wg_ref[0], NT) + dot(du, wu_ref[0], NT)
-
-    @pl.when(step == 0)
-    def _():
-        acc_ref[...] = back
-
-    @pl.when(step > 0)
-    def _():
-        acc_ref[...] += back
-
-    @pl.when(step == pl.num_programs(0) - 1)
-    def _():
-        drow_ref[...] = acc_ref[...].astype(BF)
-
-
-def ffn_bwd(j, g, a, act, slope, w_gate, w_up, w_down, tile=256):
-    rows, width = g.shape
-    ff = w_gate.shape[2]
-    col = pl.BlockSpec((1, width, tile), lambda i, j: (j[0], 0, i))
-    row = pl.BlockSpec((1, tile, width), lambda i, j: (j[0], i, 0))
-    mid = pl.BlockSpec((rows, tile), lambda i, j: (0, i))
-    gate = pl.BlockSpec((rows, 128), lambda i, j: (0, width // 128))
-    return pl.pallas_call(
-        ffn_bwd_kernel,
-        grid_spec=pltpu.PrefetchScalarGridSpec(
-            num_scalar_prefetch=1, grid=(ff // tile,),
-            in_specs=[whole(g.shape), gate, mid, mid, col, col, row],
-            out_specs=[mid, mid, whole((rows, width)), whole((rows, width))],
-            scratch_shapes=[pltpu.VMEM((rows, width), F32)]),
-        out_shape=[jax.ShapeDtypeStruct((rows, ff), BF)] * 2 + [jax.ShapeDtypeStruct((rows, width), BF)] * 2,
-        compiler_params=params(),
-        cost_estimate=pl.CostEstimate(flops=6 * rows * width * ff, bytes_accessed=8 * rows * ff + 6 * width * ff,
-                                      transcendentals=0),
-        name="ffn_bwd",
-    )(j, g, a, act, slope, w_gate, w_up, w_down)
-
-
-def ffn_grad_kernel(a_ref, dout_ref, hid_ref, dg_ref, du_ref, out_ref, at_ref, dt_ref):
-    width = dout_ref.shape[1]
-
-    @pl.when(pl.program_id(0) == 0)
-    def _():
-        at_ref[...] = a_ref[:, :width].T
-        dt_ref[...] = dout_ref[...].T
-
-    out_ref[0] = dot(at_ref[...], dg_ref[...]).astype(BF)
-    out_ref[1] = dot(at_ref[...], du_ref[...]).astype(BF)
-    out_ref[2] = dot(dt_ref[...], hid_ref[...]).astype(BF)
-
-
-def ffn_grad(a, dout, hidden, dg, du, tile=256):
-    rows, width = dout.shape
-    ff = dg.shape[1]
-    mid = pl.BlockSpec((rows, tile), lambda i: (0, i))
-    return pl.pallas_call(
-        ffn_grad_kernel,
-        grid=(ff // tile,),
-        in_specs=[whole(a.shape), whole(dout.shape), mid, mid, mid],
-        out_specs=pl.BlockSpec((3, width, tile), lambda i: (0, 0, i)),
-        out_shape=jax.ShapeDtypeStruct((3, width, ff), BF),
-        scratch_shapes=[pltpu.VMEM((width, rows), BF)] * 2,
-        compiler_params=params(),
-        cost_estimate=pl.CostEstimate(flops=6 * rows * width * ff, bytes_accessed=6 * rows * ff + 6 * width * ff,
-                                      transcendentals=0),
-        name="ffn_grad",
-    )(a, dout, hidden, dg, du)
+        functools.partial(expert_kernel, capacity=capacity, tile=tile, grad_tile=grad_tile),
+        in_specs=[vmem] * 4 + [hbm] * 3,
+        out_specs=[hbm] * 3,
+        out_shape=[jax.ShapeDtypeStruct((total, width), BF), jax.ShapeDtypeStruct((total, width), BF),
+                   jax.ShapeDtypeStruct((3, width, ff), BF)],
+        scratch_shapes=[
+            vm((width, ff), BF), vm((width, ff), BF), vm((ff, width), BF),
+            vm((8, capacity, width + 128), BF), vm((8, capacity, width + 128), BF), vm((8, capacity, width), BF),
+            vm((2 * capacity, width), BF), vm((width, total), BF), vm((width, total), BF),
+            vm((total, ff), BF), vm((total, ff), BF), vm((total, ff), BF),
+            vm((2 * capacity, width), F32), vm((2 * capacity, width), F32), vm((2, 3, width, grad_tile), BF),
+            pltpu.SemaphoreType.DMA((24,)), pltpu.SemaphoreType.DMA((24,)), pltpu.SemaphoreType.DMA((5,)),
+            pltpu.SemaphoreType.DMA((2,)),
+        ],
+        compiler_params=pltpu.CompilerParams(vmem_limit_bytes=62 << 20, collective_id=1, has_side_effects=True),
+        cost_estimate=pl.CostEstimate(flops=18 * total * width * ff, bytes_accessed=12 * width * ff + 8 * total * width,
+                                      transcendentals=total * ff),
+        name="experts_on_rows",
+    )(slots, h2, ext, g, w_gate, w_up, w_down)
 
 
 def combine_kernel(made_ref, back_ref, slot_ref, routes_ref, aux_ref, x2_ref, h2_ref, g_ref, gain_ref, wcat_ref, v_ref, w_ref,
@@ -796,9 +818,6 @@
     )(own, got, x, dx2, gain)
 
 
-MESH = pl.DeviceIdType.MESH
-
-
 def padded_rows(rows, rest):
     unit = 8 * rest * 16
     return -(-rows // unit) * unit
@@ -1019,7 +1038,9 @@
     prompt_x = lax.all_gather(tokens[:prompt_dev], "expert", axis=0, tiled=True)
     slots_t = slot_table(routes.T, priority, pair, capacity)
     slots = slots_t.T
-    grads_in = swap(dispatch(slots_t, cotangent, None, members, capacity)).reshape(-1, width)
+    grads_out = dispatch(slots_t, cotangent, members, capacity)
+    tokens, grads_out = lax.optimization_barrier((tokens, grads_out))
+    grads_in = swap(grads_out).reshape(-1, width)
     h_own, q, k_own, v_own = project(e, tokens, gain1, (w_query, w_key, w_value), cos, sin, True)
     h_prompt, k_prompt, v_prompt = project(e, prompt_x, gain1, (w_key, w_value), cos, sin, False)
     o, lse = attn_fwd(e, q, k_own, v_own, k_prompt, v_prompt)
@@ -1029,12 +1050,7 @@
     )
     prev = jnp.pad(prev_logits, ((0, 0), (0, 128 - experts)))
     x2, h2, aux, ext = gates(tokens, o, w_out, gain2, wcat, prev, routes, experts)
-    arrived = swap(dispatch(slots_t, h2, ext, members, capacity)).reshape(-1, width + 128)
-    hidden, act, slope, made = ffn_fwd(j, arrived, w_gate, w_up, w_down)
-    made = swap(made.reshape(members, capacity, width)).reshape(-1, width)
-    dg, du, dout, drow = ffn_bwd(j, grads_in, arrived, act, slope, w_gate, w_up, w_down)
-    drow = swap(drow.reshape(members, capacity, width)).reshape(-1, width)
-    ffn_sum = ffn_grad(arrived, dout, hidden, dg, du)
+    made, drow, ffn_sum = experts_on_rows(slots_t, h2, ext, grads_in, w_gate, w_up, w_down, capacity)
     ffn_sum = lax.psum_scatter(ffn_sum, "dp", scatter_dimension=2, axis_index_groups=alike, tiled=True)
 
     mixed, grad_prev, dx2, da, do, cat, sums = combine(

time: 595 us -> 538 us (0.904)
  blocking collectives: 33.6 us -> 0 us
  starting transfers between devices: 26 us -> 8.92 us
    all_to_all x3 -> x1, waiting for transfers between devices: 45.7 us -> 0.01 us  [swap(): lax.all_to_all(x, everyone, split_axis=0, concat_axis=0, axis_index_group...]
    reduce_scatter x1, waiting for transfers between devices: 0.01 us -> 40.2 us  [local(): lax.psum_scatter(ffn_sum, 'dp', scatter_dimension=2, axis_index_groups=al...]
    all_to_all x1 -> x0, blocking collectives: 33.6 us -> none  [swap(): lax.all_to_all(x, everyone, split_axis=0, concat_axis=0, axis_index_group...]
    pallas_call x3 -> x1, Pallas kernels: 85 us -> 114 us  [experts_on_rows(): pl.pallas_call(functools.partial(expert_kernel, capacity=capacity, tile=t...]
    all_to_all x3 -> x1, starting transfers between devices: 21.9 us -> 5.07 us  [swap(): lax.all_to_all(x, everyone, split_axis=0, concat_axis=0, axis_index_group...]
    pallas_call x1, Pallas kernels: 105 us -> 92.5 us  [device_sums(): pl.pallas_call(functools.partial(sum_kernel, rest=rest, chunks=chunks), i...]
    pallas_call x1, Pallas kernels: 71.8 us -> 63.7 us  [attn_bwd(): pl.pallas_call(functools.partial(attn_bwd_kernel, tile=tile, scale=0.125)...]
    pallas_call x2 -> x1, Pallas kernels: 14.8 us -> 6.79 us  [dispatch(): pl.pallas_call(functools.partial(dispatch_kernel, capacity=capacity), gri...]
  transfers between devices with their start and end apart: 6 -> 4, of which waited for: 3 -> 2; matrix products, arithmetic and copies ran while one was open for 4% -> 4% of each run, Pallas kernels for 49% -> 58%
where the time goes in v3:
time: 538 us; the launch traced here: 528 us
  Pallas kernels  418 us (78%)
  waiting for transfers between devices  55.8 us (10%)
  local copies, waits for them, and re-layouts  24.4 us (5%)
  between operations  14.7 us (3%)
  starting transfers between devices  8.92 us (2%)
    pallas_call x1, Pallas kernels, experts_on_rows(): pl.pallas_call(functools.partial(expert_kernel, capacity=capacity, tile=t...  114 us
    pallas_call x1, Pallas kernels, device_sums(): pl.pallas_call(functools.partial(sum_kernel, rest=rest, chunks=chunks), i...  92.5 us
    pallas_call x1, Pallas kernels, attn_bwd(): pl.pallas_call(functools.partial(attn_bwd_kernel, tile=tile, scale=0.125)...  63.7 us
    pallas_call x1, Pallas kernels, attn_fwd(): pl.pallas_call(functools.partial(attn_fwd_kernel, chunk=chunk, tile=tile,...  44.6 us
    reduce_scatter x1, waiting for transfers between devices, local(): lax.psum_scatter(ffn_sum, 'dp', scatter_dimension=2, axis_index_groups=al...  40.2 us
    pallas_call x1, Pallas kernels, combine(): pl.pallas_call(functools.partial(combine_kernel, experts=experts), grid=(...  22.8 us
    pallas_call x2, Pallas kernels, project(): pl.pallas_call(functools.partial(project_kernel, count=len(weights)), gri...  20.4 us
    pallas_call x1, Pallas kernels, weight_back(): pl.pallas_call(functools.partial(weight_back_kernel, prompt_steps=ps, own...  19 us
  transfers between devices with their start and end apart: 4, of which 2 were waited for; matrix products, arithmetic and copies ran while one was open for 4% of the time, Pallas kernels for 58%

profile of v3, /device:TPU:9, one launch (start us, length us, event | category | flops | bytes accessed | tf_op | source)
XLA Modules:
  0.0 527.9 jit_solution(7534169606423201342)
XLA Ops:
  7.2 2.1 slice.45
  12.3 6.8 %dispatch_grads.1 = bf16[8,192,768]{2,1,0:T(8,128)(2,1)} custom-call(s32[2,1024]{1,0:T(2,128)} %copy.128.slot_ref, bf16[1024,768]{1,0:T(8,128)(2,1)} %g_ref.1), custom_call_target="tpu_custom_call" | custom-call | flops 2415919104 | bytes 3145728 | tf_op jit(solution)/shard_map/dispatch_grads/pallas_call | solution.py:404
  19.1 5.1 all-to-all-start
  27.7 8.7 %project_own.1 = (bf16[1024,768]{1,0:T(8,128)(2,1)}, bf16[1024,768]{1,0:T(8,128)(2,1)}, bf16[1024,768]{1,0:T(8,128)(2,1)}, bf16[1024,768]{1,0:T(8,128)(2,1)}) custom-call(s32[1]{0:T(128)} %bitcast.1.e_ref, bf16[1024,768]{1,0:T(8,128)(2,1)} %x_ref.3, f32[1,768]{1,0:T(1,128)} %broadcast_in_dim.33.gain_ref, bf16[768,768]{1,0:T(8,128)(2,1)} %wq_ref.1, ...), custom_call_target="tpu_custom_call" | custom-call | flops 3623878656 | bytes 9437184 | tf_op jit(solution)/shard_map/project_own/pallas_call | solution.py:91
  36.4 15.6 %all-gather.2.cloned.1.call-done.x_ref = bf16[2048,768]{1,0:T(8,128)(2,1)} async-done(((bf16[512,768]{1,0:T(8,128)(2,1)}), bf16[2048,768]{1,0:T(8,128)(2,1)}) %all-gather.2.cloned.1.call-update) | async-done | bytes 3145744 | tf_op jit(solution)/shard_map/all_gather | solution.py:1038
  52.0 11.7 %project_prompt.1 = (bf16[2048,768]{1,0:T(8,128)(2,1)}, bf16[2048,768]{1,0:T(8,128)(2,1)}, bf16[2048,768]{1,0:T(8,128)(2,1)}) custom-call(s32[1]{0:T(128)} %bitcast.1.e_ref, bf16[2048,768]{1,0:T(8,128)(2,1)} %all-gather.2.cloned.1.call-done.x_ref, f32[1,768]{1,0:T(1,128)} %broadcast_in_dim.33.gain_ref, bf16[768,768]{1,0:T(8,128)(2,1)} %wk_ref.3, ...), custom_call_target="tpu_custom_call" | custom-call | flops 4831838208 | bytes 18874368 | tf_op jit(solution)/shard_map/project_prompt/pallas_call | solution.py:91
  63.8 44.6 %attn_fwd.1 = (bf16[1024,768]{1,0:T(8,128)(2,1)}, f32[6,2,1024]{2,1,0:T(2,128)}) custom-call(s32[1]{0:T(128)} %bitcast.1.e_ref, bf16[1024,768]{1,0:T(8,128)(2,1)} %get-tuple-element.51.q_ref, bf16[1024,768]{1,0:T(8,128)(2,1)} %get-tuple-element.52.ko_ref, bf16[1024,768]{1,0:T(8,128)(2,1)} %get-tuple-element.53.vo_ref, ...), custom_call_target="tpu_custom_call" | custom-call | flops 12884901888 | bytes 12582912 | tf_op jit(solution)/shard_map/attn_fwd/pallas_call | solution.py:188
  108.3 7.9 %gates.1 = (f32[1024,768]{1,0:T(8,128)}, bf16[1024,768]{1,0:T(8,128)(2,1)}, f32[1024,128]{1,0:T(8,128)}, bf16[1024,256]{1,0:T(8,128)(2,1)}) custom-call(bf16[1024,768]{1,0:T(8,128)(2,1)} %x_ref.3, bf16[1024,768]{1,0:T(8,128)(2,1)} %get-tuple-element.56.o_ref, bf16[768,768]{1,0:T(8,128)(2,1)} %w_ref.3, f32[1,768]{1,0:T(1,128)} %broadcast_in_dim.34.gain_ref, ...), custom_call_target="tpu_custom_call" | custom-call | flops 1207959552 | bytes 9437184 | tf_op jit(solution)/shard_map/gates/pallas_call | solution.py:382
  116.2 113.8 %experts_on_rows.1 = (bf16[1536,768]{1,0:T(8,128)(2,1)}, bf16[1536,768]{1,0:T(8,128)(2,1)}, bf16[3,768,2048]{2,1,0:T(8,128)(2,1)}) custom-call(s32[2,1024]{1,0:T(2,128)} %copy.128.slot_ref, bf16[1024,768]{1,0:T(8,128)(2,1)} %get-tuple-element.57.h2_ref, bf16[1024,256]{1,0:T(8,128)(2,1)} %get-tuple-element.58.ext_ref, bf16[1536,768]{1,0:T(8,128)(2,1)} %bitcast.3.g_ref, ...), custom_call_target="tpu_custom_call" | custom-call | flops 43486543872 | bytes 28311552 | tf_op jit(solution)/shard_map/experts_on_rows/pallas_call | solution.py:549
  231.1 1.5 fusion.13.slot_ref
  232.5 22.8 %combine.1 = (bf16[1024,768]{1,0:T(8,128)(2,1)}, f32[1024,12]{1,0:T(8,128)}, f32[1024,768]{1,0:T(8,128)}, bf16[1024,768]{1,0:T(8,128)(2,1)}, bf16[1024,768]{1,0:...) custom-call(bf16[1536,768]{1,0:T(8,128)(2,1)} %get-tuple-element.60.made_ref, ...), custom_call_target="tpu_custom_call" | custom-call | flops 9663676416 | bytes 23592960 | tf_op jit(solution)/shard_map/combine/pallas_call | solution.py:644
  256.9 63.7 %attn_bwd.1 = (bf16[1024,768]{1,0:T(8,128)(2,1)}, bf16[2560,768]{1,0:T(8,128)(2,1)}, bf16[2560,768]{1,0:T(8,128)(2,1)}) custom-call(s32[1]{0:T(128)} %bitcast.1.e_ref, bf16[1024,768]{1,0:T(8,128)(2,1)} %get-tuple-element.51.q_ref, bf16[1024,768]{1,0:T(8,128)(2,1)} %get-tuple-element.65.do_ref, bf16[1024,768]{1,0:T(8,128)(2,1)} %get-tuple-element.56.o_ref, ...), custom_call_target="tpu_custom_call" | custom-call | flops 32212254720 | bytes 25165824 | tf_op jit(solution)/shard_map/attn_bwd/pallas_call | solution.py:319
  320.6 11.6 %prompt_back.1 = (bf16[2048,768]{1,0:T(8,128)(2,1)}, f32[1,768]{1,0:T(1,128)}) custom-call(bf16[2560,768]{1,0:T(8,128)(2,1)} %get-tuple-element.68.dk_ref, bf16[2560,768]{1,0:T(8,128)(2,1)} %get-tuple-element.69.dv_ref, bf16[768,768]{1,0:T(8,128)(2,1)} %wk_ref.3, bf16[768,768]{1,0:T(8,128)(2,1)} %wv_ref.3, bf16[2048,768]{1,0:T(8,128)(2,1)} %all-gather.2.cloned.1.call-done.x_ref), custom_call_target="tpu_custom_call" | custom-call | flops 4831838208 | bytes 12582912 | tf_op jit(solution)/shard_map/prompt_back/pallas_call | solution.py:679
  332.2 19.0 %weight_back.1.g_ref = bf16[3072,768]{1,0:T(8,128)(2,1)} custom-call(bf16[2048,768]{1,0:T(8,128)(2,1)} %get-tuple-element.71.hp_ref, bf16[1024,768]{1,0:T(8,128)(2,1)} %get-tuple-element.72.ho_ref, bf16[1024,768]{1,0:T(8,128)(2,1)} %get-tuple-element.56.o_ref, bf16[1024,768]{1,0:T(8,128)(2,1)} %get-tuple-element.73.da_ref, ...), custom_call_target="tpu_custom_call" | custom-call | flops 9663676416 | bytes 11010048 | tf_op jit(solution)/shard_map/weight_back/pallas_call | solution.py:772
  351.1 40.2 %reduce-scatter.2.cloned.1.call-done = bf16[3,768,512]{2,1,0:T(8,128)(2,1)} async-done(((bf16[3,768,2048]{2,1,0:T(8,128)(2,1)}), bf16[3,768,512]{2,1,0:T(8,128)(2,1)}) %reduce-scatter.2.cloned.1.call-update) | async-done | bytes 2359312 | tf_op jit(solution)/shard_map/reduce_scatter | solution.py:1054
  391.3 3.3 copy.145
  394.6 3.8 all-to-all-start.1
  398.5 8.4 %own_back.1 = (f32[1024,768]{1,0:T(8,128)}, f32[1,768]{1,0:T(1,128)}) custom-call(bf16[1024,768]{1,0:T(8,128)(2,1)} %get-tuple-element.67.dq_ref, bf16[2560,768]{1,0:T(8,128)(2,1)} %get-tuple-element.68.dk_ref, bf16[2560,768]{1,0:T(8,128)(2,1)} %get-tuple-element.69.dv_ref, bf16[768,768]{1,0:T(8,128)(2,1)} %wq_ref.1, bf16[768,768]{1,0:T(8,128)(2,1)} %wk_ref.3, ...), custom_call_target="tpu_custom_call" | custom-call | flops 2415919104 | bytes 6291456 | tf_op jit(solution)/shard_map/own_back/pallas_call | solution.py:719
  408.3 92.5 %device_sums.1 = (bf16[3072,768]{1,0:T(8,128)(2,1)}, f32[24,768]{1,0:T(8,128)}, f32[512,768]{1,0:T(8,128)}) custom-call(bf16[3072,768]{1,0:T(8,128)(2,1)} %weight_back.1.g_ref, f32[24,768]{1,0:T(8,128)} %maximum_maximum_fusion.1.small_ref, bf16[2048,768]{1,0:T(8,128)(2,1)} %get-tuple-element.78.dh_ref), custom_call_target="tpu_custom_call" | custom-call | flops 9437184 | bytes 18874368 | tf_op jit(solution)/shard_map/device_sums/pallas_call | solution.py:983
  501.6 1.3 slice.56
  504.3 7.0 %token_back.1 = f32[1024,768]{1,0:T(8,128)} custom-call(f32[1024,768]{1,0:T(8,128)} %get-tuple-element.70.own_ref, f32[512,768]{1,0:T(8,128)} %get-tuple-element.79.got_ref, bf16[1024,768]{1,0:T(8,128)(2,1)} %x_ref.3, f32[1024,768]{1,0:T(8,128)} %get-tuple-element.80.dx2_ref, f32[1,768]{1,0:T(1,128)} %broadcast_in_dim.33.gain_ref), custom_call_target="tpu_custom_call" | custom-call | flops 7864320 | bytes 11010048 | tf_op jit(solution)/shard_map/token_back/pallas_call | solution.py:808
  512.6 3.8 fusion.25
  516.9 2.2 slice_bitcast_fusion
  519.0 1.6 copy.141
  (68 shorter events, 14.3 us)
Async XLA Ops:
  7.2 2.2 copy-start.5
  7.2 2.6 copy-start.11
  7.2 44.8 %all-gather.2.cloned.1.call-start = ((), (), s32[]{:S(2)}) async-start(), calls=%async_computation.3 | async-start | bytes 3932160 | tf_op jit(solution)/shard_map/all_gather | solution.py:1038
  9.6 9.5 %copy-start = (s32[1024,2]{1,0:T(8,128)}, s32[1024,2]{1,0:T(8,128)S(1)}, u32[]{:S(2)}) copy-start(s32[1024,2]{1,0:T(8,128)S(1)} %copy.120.routes_ref) | copy-start | bytes 24580
  19.1 5.1 copy-start.8
  19.1 5.7 %copy-start.7 = (bf16[2,768,2]{1,2,0:T(2,128)(2,1)S(1)}, bf16[2,768,2]{1,2,0:T(2,128)(2,1)}, u32[]{:S(2)}) copy-start(bf16[2,768,2]{1,2,0:T(2,128)(2,1)} %param.30) | copy-start | bytes 18436
  19.1 5.9 %copy-start.6 = (bf16[768,12]{0,1:T(8,128)(2,1)S(1)}, bf16[768,12]{0,1:T(8,128)(2,1)}, u32[]{:S(2)}) copy-start(bf16[768,12]{0,1:T(8,128)(2,1)} %param.29) | copy-start | bytes 55300
  19.1 6.1 %copy-start.9 = (f32[768]{0:T(1024)S(1)}, f32[768]{0:T(1024)}, u32[]{:S(2)}) copy-start(f32[768]{0:T(1024)} %param.28) | copy-start | bytes 9220
  19.1 6.7 %copy-start.4 = (f32[1024,12]{0,1:T(8,128)S(1)}, f32[1024,12]{0,1:T(8,128)}, u32[]{:S(2)}) copy-start(f32[1024,12]{0,1:T(8,128)} %param.20) | copy-start | bytes 147460
  19.1 97.1 %all-to-all-start = ((bf16[8,192,768]{2,1,0:T(8,128)(2,1)}), bf16[8,192,768]{2,1,0:T(8,128)(2,1)}, u32[]{:S(2)}, u32[]{:S(2)}) async-start(bf16[8,192,768]{2,1,0:T(8,128)(2,1)} %dispatch_grads.1), calls=%async_computation | async-start | bytes 4718592 | tf_op jit(solution)/shard_map/all_to_all | solution.py:1033
  24.2 367.2 %reduce-scatter.2.cloned.1.call-start = ((), (), s32[]{:S(2)}) async-start(), calls=%async_computation.4 | async-start | bytes 11796480 | tf_op jit(solution)/shard_map/reduce_scatter | solution.py:1054
  230.0 1.0 copy-start.1
  394.6 121.8 %all-to-all-start.1 = ((bf16[2,3,768,256]{3,2,1,0:T(8,128)(2,1)}), bf16[2,3,768,256]{3,2,1,0:T(8,128)(2,1)S(1)}, u32[]{:S(2)}, u32[]{:S(2)}) async-start(bf16[2,3,768,256]{3,2,1,0:T(8,128)(2,1)} %bitcast.36), calls=%async_computation.2 | async-start | bytes 4718592 | tf_op jit(solution)/shard_map/all_to_all | solution.py:1073
  398.4 8.4 %copy-start.10 = (f32[1,768]{1,0:T(1,128)S(1)}, f32[1,768]{1,0:T(1,128)}, u32[]{:S(2)}) copy-start(f32[1,768]{1,0:T(1,128)} %get-tuple-element.76) | copy-start | bytes 9220
  408.3 95.2 %copy-start.2 = (f32[1024,12]{1,0:T(8,128)S(1)}, f32[1024,12]{1,0:T(8,128)}, u32[]{:S(2)}) copy-start(f32[1024,12]{1,0:T(8,128)} %get-tuple-element.147) | copy-start | bytes 147460
  504.3 8.3 %slice-start = ((s8[4718592]{0:T(1024)(128)(4,1)}), s8[4194304]{0:T(1024)(128)(4,1)S(1)}, s32[]{:S(2)}) async-start(s8[4718592]{0:T(1024)(128)(4,1)} %bitcast.33), calls=%async_computation.5 | async-start | bytes 8388608
  504.3 7.0 %copy-start.3 = (f32[24,768]{1,0:T(8,128)S(1)}, f32[24,768]{1,0:T(8,128)}, u32[]{:S(2)}) copy-start(f32[24,768]{1,0:T(8,128)} %get-tuple-element.82) | copy-start | bytes 221188
  504.3 8.3 %slice-start.1 = ((s8[4718592]{0:T(1024)(128)(4,1)}), s8[524288]{0:T(1024)(128)(4,1)S(1)}, s32[]{:S(2)}) async-start(s8[4718592]{0:T(1024)(128)(4,1)} %bitcast.33), calls=%async_computation.6 | async-start | bytes 1048576
Sparse Core Ops, SparseCore 0:
  10.2 41.8 all-gather.1
  230.2 161.1 reduce-scatter.1

commit v4 on v3

--- a/solution.py
+++ b/solution.py
@@ -348,6 +348,16 @@
     return ea / total, eb / total
 
 
+def spread(column):
+    lane = lane_iota()
+    parts, left = jnp.zeros((1, 128), F32), column
+    for n in range(3):
+        part = left.astype(BF).astype(F32)
+        parts = jnp.where(lane == n, part, parts)
+        left = left - part
+    return parts.astype(BF)
+
+
 def gate_kernel(x_ref, o_ref, w_ref, gain_ref, wcat_ref, prev_ref, routes_ref, x2_ref, h2_ref, aux_ref, ext_ref, *, experts):
     x2 = x_ref[...].astype(F32) + dot(o_ref[...], w_ref[...])
     x2_ref[...] = x2
@@ -366,13 +376,7 @@
             aux = jnp.where(lane == at + 2 * c + k, alpha[k], aux)
     aux_ref[...] = aux
     for k in range(2):
-        parts, left = [], gates[k]
-        for _ in range(3):
-            part = left.astype(BF)
-            parts.append(part.astype(F32))
-            left = left - parts[-1]
-        spread = jnp.where(lane == 0, parts[0], jnp.where(lane == 1, parts[1], jnp.where(lane == 2, parts[2], 0.0)))
-        ext_ref[:, k * 128:(k + 1) * 128] = spread.astype(BF)
+        ext_ref[:, k * 128:(k + 1) * 128] = spread(gates[k])
 
 
 def gates(x, o, w_out, gain, wcat, prev, routes, experts, tile=256):
@@ -414,8 +418,8 @@
     )(slots, rows)
 
 
-def expert_kernel(slot_ref, h2_ref, ext_ref, g_ref, wg_hbm, wu_hbm, wd_hbm, made_hbm, back_hbm, grad_hbm,
-                  wg_ref, wu_ref, wd_ref, a_ref, s_ref, b_ref, d_ref, at_ref, dt_ref, hid_ref, dg_ref, du_ref, macc_ref,
+def expert_kernel(slot_ref, h2_ref, ext_ref, g_ref, wg_hbm, wu_hbm, wd_hbm, made_ref, back_hbm, grad_hbm,
+                  wg_ref, wu_ref, wd_ref, a_ref, s_ref, d_ref, at_ref, dt_ref, hid_ref, dg_ref, du_ref, macc_ref,
                   bacc_ref, out_ref, send_sem, recv_sem, local_sem, out_sem, *, capacity, tile, grad_tile):
     dp, ex = lax.axis_index("dp"), lax.axis_index("expert")
     j, c, x = dp % 2, ex % 2, ex // 2
@@ -459,7 +463,7 @@
 
     for copy in loads:
         copy.wait()
-    returned, kept = [], []
+    returned = []
     mine = pl.ds(pl.multiple_of(place(0) * capacity, 16), capacity)
     two = 2 * capacity
     for n, first in enumerate((0, 4, 6, 2)):
@@ -499,17 +503,16 @@
             half = pl.ds((r - first) * capacity, capacity)
             if r:
                 rows[r].wait_send()
-            s_ref[r, :, :width] = macc_ref[half, :].astype(BF)
-            b_ref[r] = bacc_ref[half, :].astype(BF)
-            made = s_ref.at[r, :, pl.ds(0, width)]
+            theirs = pl.ds(pl.multiple_of(place(r) * capacity, 16), capacity)
+            made = macc_ref[half, :].astype(BF)
+            made_ref[theirs, :] = made
+            s_ref[r, :, :width] = bacc_ref[half, :].astype(BF)
+            s_ref[r, :, width:] = spread(jnp.sum(g_ref[theirs, :].astype(F32) * made.astype(F32), axis=1, keepdims=True))
             if r:
-                returned.append(send(made, made_hbm.at[mine], 1, r))
-                returned.append(send(b_ref.at[r], back_hbm.at[mine], 2, r))
+                returned.append(send(s_ref.at[r], back_hbm.at[mine], 1, r))
             else:
-                kept += [pltpu.make_async_copy(made, made_hbm.at[mine], local_sem.at[3]),
-                         pltpu.make_async_copy(b_ref.at[r], back_hbm.at[mine], local_sem.at[4])]
-                for copy in kept:
-                    copy.start()
+                kept = pltpu.make_async_copy(s_ref.at[0], back_hbm.at[mine], local_sem.at[3])
+                kept.start()
 
     steps = ff // grad_tile
 
@@ -533,8 +536,7 @@
 
     for i in range(max(steps - 2, 0), steps):
         put(i, i % 2).wait()
-    for copy in kept:
-        copy.wait()
+    kept.wait()
     for copy in returned:
         copy.wait_recv()
         copy.wait_send()
@@ -549,16 +551,16 @@
     return pl.pallas_call(
         functools.partial(expert_kernel, capacity=capacity, tile=tile, grad_tile=grad_tile),
         in_specs=[vmem] * 4 + [hbm] * 3,
-        out_specs=[hbm] * 3,
-        out_shape=[jax.ShapeDtypeStruct((total, width), BF), jax.ShapeDtypeStruct((total, width), BF),
+        out_specs=[vmem, hbm, hbm],
+        out_shape=[jax.ShapeDtypeStruct((total, width), BF), jax.ShapeDtypeStruct((total, width + 128), BF),
                    jax.ShapeDtypeStruct((3, width, ff), BF)],
         scratch_shapes=[
             vm((width, ff), BF), vm((width, ff), BF), vm((ff, width), BF),
-            vm((8, capacity, width + 128), BF), vm((8, capacity, width + 128), BF), vm((8, capacity, width), BF),
+            vm((8, capacity, width + 128), BF), vm((8, capacity, width + 128), BF),
             vm((2 * capacity, width), BF), vm((width, total), BF), vm((width, total), BF),
             vm((total, ff), BF), vm((total, ff), BF), vm((total, ff), BF),
             vm((2 * capacity, width), F32), vm((2 * capacity, width), F32), vm((2, 3, width, grad_tile), BF),
-            pltpu.SemaphoreType.DMA((24,)), pltpu.SemaphoreType.DMA((24,)), pltpu.SemaphoreType.DMA((5,)),
+            pltpu.SemaphoreType.DMA((16,)), pltpu.SemaphoreType.DMA((16,)), pltpu.SemaphoreType.DMA((4,)),
             pltpu.SemaphoreType.DMA((2,)),
         ],
         compiler_params=pltpu.CompilerParams(vmem_limit_bytes=62 << 20, collective_id=1, has_side_effects=True),
@@ -568,45 +570,52 @@
     )(slots, h2, ext, g, w_gate, w_up, w_down)
 
 
-def combine_kernel(made_ref, back_ref, slot_ref, routes_ref, aux_ref, x2_ref, h2_ref, g_ref, gain_ref, wcat_ref, v_ref, w_ref,
-                   mixed_ref, prev_ref, dx2_ref, da_ref, do_ref, cat_ref, sums_ref, *, experts):
+def one(cond):
+    return jnp.where(cond, 1.0, 0.0)
+
+
+def pick_parts(aux, routes, experts):
+    lane = lane_iota()
+    gate = [pick(aux, lane, experts + k) for k in range(2)]
+    alpha = [[pick(aux, lane, experts + 2 + 2 * c + k) for k in range(2)] for c in range(2)]
+    copy = [one(routes[k] == FFN_EXP + 1) for k in range(2)]
+    const = [[one(routes[k] == FFN_EXP + 2 + c) for c in range(2)] for k in range(2)]
+    on_h2 = [copy[k] + const[k][0] * alpha[0][0] + const[k][1] * alpha[1][0] for k in range(2)]
+    return gate, alpha, copy, const, on_h2
+
+
+def one_hot(slots, total):
+    return jnp.where(lane_iota(total) == slots, 1.0, 0.0).astype(BF)
+
+
+def combine_kernel(back_ref, slot_ref, routes_ref, aux_ref, x2_ref, h2_ref, g_ref, gain_ref, wcat_ref, v_ref, w_ref,
+                   prev_ref, dx2_ref, da_ref, do_ref, cat_ref, sums_ref, *, experts):
     step = pl.program_id(0)
     lane = lane_iota()
-    aux = aux_ref[...]
     h2 = h2_ref[...].astype(F32)
     g = g_ref[...].astype(F32)
     x2 = x2_ref[...]
+    width = x2.shape[1]
     r2 = rms_scale(x2)
-    slot_total = made_ref.shape[0]
-    slot_ids = lane_iota(slot_total)
-    hot = [jnp.where(slot_ids == slot_ref[:, k:k + 1], 1.0, 0.0).astype(BF) for k in range(2)]
-    gate = [pick(aux, lane, experts + k) for k in range(2)]
-    alpha = [[pick(aux, lane, experts + 2 + 2 * c + k) for k in range(2)] for c in range(2)]
     route = [routes_ref[:, k:k + 1] for k in range(2)]
-    one = lambda cond: jnp.where(cond, 1.0, 0.0)
-    copy = [one(route[k] == FFN_EXP + 1) for k in range(2)]
-    const = [[one(route[k] == FFN_EXP + 2 + c) for c in range(2)] for k in range(2)]
+    gate, alpha, copy, const, on_h2 = pick_parts(aux_ref[...], route, experts)
+    hot = [one_hot(slot_ref[:, k:k + 1], back_ref.shape[0]) for k in range(2)]
+    g_h2 = jnp.sum(g * h2, axis=1, keepdims=True)
+    g_v = [jnp.sum(g * v_ref[c:c + 1, :], axis=1, keepdims=True) for c in range(2)]
     dgate = []
-    x3 = x2
     for k in range(2):
-        on_h2 = copy[k] + const[k][0] * alpha[0][0] + const[k][1] * alpha[1][0]
-        branch = dot(hot[k], made_ref[...]) + on_h2 * h2
-        for c in range(2):
-            branch = branch + (const[k][c] * alpha[c][1]) * v_ref[c:c + 1, :]
-        x3 = x3 + gate[k] * branch
-        dgate.append(jnp.sum(g * branch, axis=1, keepdims=True))
-    mixed_ref[...] = x3.astype(BF)
+        at_expert = jnp.sum(dot(hot[k], back_ref[:, width:]), axis=1, keepdims=True)
+        dgate.append(at_expert + on_h2[k] * g_h2 + const[k][0] * alpha[0][1] * g_v[0] + const[k][1] * alpha[1][1] * g_v[1])
     mean = gate[0] * dgate[0] + gate[1] * dgate[1]
     dl = [gate[k] * (dgate[k] - mean) for k in range(2)]
     grads = jnp.where(lane == route[0], dl[0], 0.0) + jnp.where(lane == route[1], dl[1], 0.0)
     prev_ref[...] = grads[:, :experts]
     weight = [gate[0] * const[0][c] + gate[1] * const[1][c] for c in range(2)]
-    g_h2 = jnp.sum(g * h2, axis=1, keepdims=True)
     sums = []
     on_g = copy[0] * gate[0] + copy[1] * gate[1]
     for c in range(2):
         da0 = weight[c] * g_h2
-        da1 = weight[c] * jnp.sum(g * v_ref[c:c + 1, :], axis=1, keepdims=True)
+        da1 = weight[c] * g_v[c]
         mid = alpha[c][0] * da0 + alpha[c][1] * da1
         grads = jnp.where(lane == experts + 2 * c, alpha[c][0] * (da0 - mid), grads)
         grads = jnp.where(lane == experts + 2 * c + 1, alpha[c][1] * (da1 - mid), grads)
@@ -614,7 +623,7 @@
         sums.append(jnp.sum((alpha[c][1] * weight[c]) * g, axis=0, keepdims=True))
     low = grads.astype(BF)
     cat = dot(low.T, h2_ref[...])
-    dh2 = dot(low, wcat_ref[...], NT) + on_g * g + dot(hot[0] + hot[1], back_ref[...])
+    dh2 = dot(low, wcat_ref[...], NT) + on_g * g + dot(hot[0] + hot[1], back_ref[:, :width])
     sums.append(jnp.sum(dh2 * x2 * r2, axis=0, keepdims=True))
     u = dh2 * gain_ref[...]
     dx2 = g + r2 * (u - x2 * (r2 * r2) * jnp.mean(u * x2, axis=-1, keepdims=True))
@@ -622,7 +631,7 @@
     da = dx2.astype(BF)
     da_ref[...] = da
     do_ref[...] = dot(da, w_ref[...], NT).astype(BF)
-    parts = jnp.concatenate(sums + [jnp.zeros((8 - len(sums), g.shape[1]), F32)], axis=0)
+    parts = jnp.concatenate(sums + [jnp.zeros((8 - len(sums), width), F32)], axis=0)
 
     @pl.when(step == 0)
     def _():
@@ -635,7 +644,7 @@
         sums_ref[...] += parts
 
 
-def combine(made, back, slots, routes, aux, x2, h2, g, gain, wcat, const_v, w_out, experts, tile=256):
+def combine(back, slots, routes, aux, x2, h2, g, gain, wcat, const_v, w_out, experts, tile=256):
     rows, width = x2.shape
     block = pl.BlockSpec((tile, width), lambda i: (i, 0))
     thin = pl.BlockSpec((tile, 128), lambda i: (i, 0))
@@ -644,17 +653,45 @@
     return pl.pallas_call(
         functools.partial(combine_kernel, experts=experts),
         grid=(rows // tile,),
-        in_specs=[whole(made.shape), whole(back.shape), two, two, thin, block, block, block, whole(gain.shape),
-                  whole(wcat.shape), whole(const_v.shape), whole(w_out.shape)],
-        out_specs=[block, pl.BlockSpec((tile, experts), lambda i: (i, 0)), block, block, block, whole((128, width)),
+        in_specs=[whole(back.shape), two, two, thin, block, block, block, whole(gain.shape), whole(wcat.shape),
+                  whole(const_v.shape), whole(w_out.shape)],
+        out_specs=[pl.BlockSpec((tile, experts), lambda i: (i, 0)), block, block, block, whole((128, width)),
                    whole((8, width))],
-        out_shape=[sds((rows, width), BF), sds((rows, experts), F32), sds((rows, width), F32), sds((rows, width), BF),
+        out_shape=[sds((rows, experts), F32), sds((rows, width), F32), sds((rows, width), BF),
                    sds((rows, width), BF), sds((128, width), F32), sds((8, width), F32)],
         compiler_params=params(),
-        cost_estimate=pl.CostEstimate(flops=8 * rows * width * made.shape[0], bytes_accessed=30 * rows * width,
+        cost_estimate=pl.CostEstimate(flops=4 * rows * width * back.shape[0], bytes_accessed=26 * rows * width,
                                       transcendentals=0),
         name="combine",
-    )(made, back, slots, routes, aux, x2, h2, g, gain, wcat, const_v, w_out)
+    )(back, slots, routes, aux, x2, h2, g, gain, wcat, const_v, w_out)
+
+
+def mix_kernel(made_ref, slot_ref, routes_ref, aux_ref, x2_ref, h2_ref, v_ref, out_ref, *, experts):
+    route = [routes_ref[:, k:k + 1] for k in range(2)]
+    gate, alpha, _, const, on_h2 = pick_parts(aux_ref[...], route, experts)
+    out = x2_ref[...] + (gate[0] * on_h2[0] + gate[1] * on_h2[1]) * h2_ref[...].astype(F32)
+    for c in range(2):
+        out = out + ((gate[0] * const[0][c] + gate[1] * const[1][c]) * alpha[c][1]) * v_ref[c:c + 1, :]
+    for k in range(2):
+        out = out + gate[k] * dot(one_hot(slot_ref[:, k:k + 1], made_ref.shape[0]), made_ref[...])
+    out_ref[...] = out.astype(BF)
+
+
+def mix(made, slots, routes, aux, x2, h2, const_v, experts, tile=256):
+    rows, width = x2.shape
+    block = pl.BlockSpec((tile, width), lambda i: (i, 0))
+    two = pl.BlockSpec((tile, 2), lambda i: (i, 0))
+    return pl.pallas_call(
+        functools.partial(mix_kernel, experts=experts),
+        grid=(rows // tile,),
+        in_specs=[whole(made.shape), two, two, pl.BlockSpec((tile, 128), lambda i: (i, 0)), block, block, whole(const_v.shape)],
+        out_specs=block,
+        out_shape=jax.ShapeDtypeStruct((rows, width), BF),
+        compiler_params=params(),
+        cost_estimate=pl.CostEstimate(flops=4 * rows * width * made.shape[0], bytes_accessed=12 * rows * width,
+                                      transcendentals=0),
+        name="mix",
+    )(made, slots, routes, aux, x2, h2, const_v)
 
 
 def prompt_back_kernel(dk_ref, dv_ref, wk_ref, wv_ref, x_ref, out_ref, sum_ref):
@@ -1050,11 +1087,11 @@
     )
     prev = jnp.pad(prev_logits, ((0, 0), (0, 128 - experts)))
     x2, h2, aux, ext = gates(tokens, o, w_out, gain2, wcat, prev, routes, experts)
-    made, drow, ffn_sum = experts_on_rows(slots_t, h2, ext, grads_in, w_gate, w_up, w_down, capacity)
+    made, back, ffn_sum = experts_on_rows(slots_t, h2, ext, grads_in, w_gate, w_up, w_down, capacity)
     ffn_sum = lax.psum_scatter(ffn_sum, "dp", scatter_dimension=2, axis_index_groups=alike, tiled=True)
-
-    mixed, grad_prev, dx2, da, do, cat, sums = combine(
-        made, drow, slots, routes, aux, x2, h2, cotangent, gain2, wcat, const_v, w_out, experts
+    made = swap(made.reshape(members, capacity, width)).reshape(-1, width)
+    grad_prev, dx2, da, do, cat, sums = combine(
+        back, slots, routes, aux, x2, h2, cotangent, gain2, wcat, const_v, w_out, experts
     )
     dq, dk, dv = attn_bwd(e, q, do, o, lse, k_own, v_own, k_prompt, v_prompt, cos, sin)
     dh_prompt, sum_p = prompt_back(dk, dv, w_key, w_value, prompt_x)
@@ -1069,6 +1106,7 @@
     grad_w = grad_w.astype(F32)
     grad_tokens = token_back(dh_own, got, tokens, dx2, gain1)
 
+    mixed = mix(made, slots, routes, aux, x2, h2, const_v, experts)
     ffn_sum = ffn_sum.reshape(3, width, pair, -1).transpose(2, 0, 1, 3)
     ffn_sum = lax.all_to_all(ffn_sum, "dp", split_axis=0, concat_axis=0, axis_index_groups=pairs, tiled=True)
     ffn_sum = ffn_sum.astype(F32)

time: 538 us -> 493 us (0.916)
  waiting for transfers between devices: 55.8 us -> 20.1 us
  Pallas kernels: 418 us -> 406 us
    reduce_scatter x1, waiting for transfers between devices: 40.2 us -> 0.02 us  [local(): lax.psum_scatter(ffn_sum, 'dp', scatter_dimension=2, axis_index_groups=al...]
    pallas_call x1, Pallas kernels: 114 us -> 88.3 us  [experts_on_rows(): pl.pallas_call(functools.partial(expert_kernel, capacity=capacity, tile=t...]
    pallas_call x0 -> x1, Pallas kernels: none -> 9.26 us  [mix(): pl.pallas_call(functools.partial(mix_kernel, experts=experts), grid=(rows...]
    pallas_call x1, Pallas kernels: 92.5 us -> 98.4 us  [device_sums(): pl.pallas_call(functools.partial(sum_kernel, rest=rest, chunks=chunks), i...]
  transfers between devices with their start and end apart: 4 -> 5, of which waited for: 2 -> 2; matrix products, arithmetic and copies ran while one was open for 4% -> 4% of each run, Pallas kernels for 58% -> 66%
where the time goes in v4:
time: 493 us; the launch traced here: 483 us
  Pallas kernels  406 us (82%)
  local copies, waits for them, and re-layouts  23.5 us (5%)
  waiting for transfers between devices  20.1 us (4%)
  between operations  14.8 us (3%)
  starting transfers between devices  13.1 us (3%)
    pallas_call x1, Pallas kernels, device_sums(): pl.pallas_call(functools.partial(sum_kernel, rest=rest, chunks=chunks), i...  98.4 us
    pallas_call x1, Pallas kernels, experts_on_rows(): pl.pallas_call(functools.partial(expert_kernel, capacity=capacity, tile=t...  88.3 us
    pallas_call x1, Pallas kernels, attn_bwd(): pl.pallas_call(functools.partial(attn_bwd_kernel, tile=tile, scale=0.125)...  63.5 us
    pallas_call x1, Pallas kernels, attn_fwd(): pl.pallas_call(functools.partial(attn_fwd_kernel, chunk=chunk, tile=tile,...  44.6 us
    pallas_call x1, Pallas kernels, combine(): pl.pallas_call(functools.partial(combine_kernel, experts=experts), grid=(...  21.1 us
    pallas_call x2, Pallas kernels, project(): pl.pallas_call(functools.partial(project_kernel, count=len(weights)), gri...  20.4 us
    pallas_call x1, Pallas kernels, weight_back(): pl.pallas_call(functools.partial(weight_back_kernel, prompt_steps=ps, own...  18.9 us
    all_gather x1, waiting for transfers between devices, local(): prompt_x = lax.all_gather(tokens[:prompt_dev], 'expert', axis=0, tiled=True)  15.6 us
  transfers between devices with their start and end apart: 5, of which 2 were waited for; matrix products, arithmetic and copies ran while one was open for 4% of the time, Pallas kernels for 66%

profile of v4, /device:TPU:9, one launch (start us, length us, event | category | flops | bytes accessed | tf_op | source)
XLA Modules:
  0.0 483.0 jit_solution(16336133559235389774)
XLA Ops:
  7.2 2.1 slice.45
  12.3 6.8 %dispatch_grads.1 = bf16[8,192,768]{2,1,0:T(8,128)(2,1)} custom-call(s32[2,1024]{1,0:T(2,128)} %copy.132.slot_ref, bf16[1024,768]{1,0:T(8,128)(2,1)} %g_ref.1), custom_call_target="tpu_custom_call" | custom-call | flops 2415919104 | bytes 3145728 | tf_op jit(solution)/shard_map/dispatch_grads/pallas_call | solution.py:408
  19.1 5.1 %all-to-all-start = ((bf16[8,192,768]{2,1,0:T(8,128)(2,1)}), bf16[8,192,768]{2,1,0:T(8,128)(2,1)}, u32[]{:S(2)}, u32[]{:S(2)}) async-start(bf16[8,192,768]{2,1,0:T(8,128)(2,1)} %dispatch_grads.1), calls=%async_computation | async-start | bytes 4718592 | tf_op jit(solution)/shard_map/all_to_all | solution.py:1070
  27.7 8.7 %project_own.1 = (bf16[1024,768]{1,0:T(8,128)(2,1)}, bf16[1024,768]{1,0:T(8,128)(2,1)}, bf16[1024,768]{1,0:T(8,128)(2,1)}, bf16[1024,768]{1,0:T(8,128)(2,1)}) custom-call(s32[1]{0:T(128)} %bitcast.1.e_ref, bf16[1024,768]{1,0:T(8,128)(2,1)} %x_ref.3, f32[1,768]{1,0:T(1,128)} %broadcast_in_dim.33.gain_ref, bf16[768,768]{1,0:T(8,128)(2,1)} %wq_ref.1, ...), custom_call_target="tpu_custom_call" | custom-call | flops 3623878656 | bytes 9437184 | tf_op jit(solution)/shard_map/project_own/pallas_call | solution.py:91
  36.4 15.6 %all-gather.2.cloned.1.call-done.x_ref = bf16[2048,768]{1,0:T(8,128)(2,1)} async-done(((bf16[512,768]{1,0:T(8,128)(2,1)}), bf16[2048,768]{1,0:T(8,128)(2,1)}) %all-gather.2.cloned.1.call-update) | async-done | bytes 3145744 | tf_op jit(solution)/shard_map/all_gather | solution.py:1075
  52.0 11.7 %project_prompt.1 = (bf16[2048,768]{1,0:T(8,128)(2,1)}, bf16[2048,768]{1,0:T(8,128)(2,1)}, bf16[2048,768]{1,0:T(8,128)(2,1)}) custom-call(s32[1]{0:T(128)} %bitcast.1.e_ref, bf16[2048,768]{1,0:T(8,128)(2,1)} %all-gather.2.cloned.1.call-done.x_ref, f32[1,768]{1,0:T(1,128)} %broadcast_in_dim.33.gain_ref, bf16[768,768]{1,0:T(8,128)(2,1)} %wk_ref.3, ...), custom_call_target="tpu_custom_call" | custom-call | flops 4831838208 | bytes 18874368 | tf_op jit(solution)/shard_map/project_prompt/pallas_call | solution.py:91
  63.7 44.6 %attn_fwd.1 = (bf16[1024,768]{1,0:T(8,128)(2,1)}, f32[6,2,1024]{2,1,0:T(2,128)}) custom-call(s32[1]{0:T(128)} %bitcast.1.e_ref, bf16[1024,768]{1,0:T(8,128)(2,1)} %get-tuple-element.50.q_ref, bf16[1024,768]{1,0:T(8,128)(2,1)} %get-tuple-element.51.ko_ref, bf16[1024,768]{1,0:T(8,128)(2,1)} %get-tuple-element.52.vo_ref, ...), custom_call_target="tpu_custom_call" | custom-call | flops 12884901888 | bytes 12582912 | tf_op jit(solution)/shard_map/attn_fwd/pallas_call | solution.py:188
  108.3 7.9 %gates.1 = (f32[1024,768]{1,0:T(8,128)}, bf16[1024,768]{1,0:T(8,128)(2,1)}, f32[1024,128]{1,0:T(8,128)}, bf16[1024,256]{1,0:T(8,128)(2,1)}) custom-call(bf16[1024,768]{1,0:T(8,128)(2,1)} %x_ref.3, bf16[1024,768]{1,0:T(8,128)(2,1)} %get-tuple-element.55.o_ref, bf16[768,768]{1,0:T(8,128)(2,1)} %w_ref.3, f32[1,768]{1,0:T(1,128)} %broadcast_in_dim.34.gain_ref, ...), custom_call_target="tpu_custom_call" | custom-call | flops 1207959552 | bytes 9437184 | tf_op jit(solution)/shard_map/gates/pallas_call | solution.py:386
  116.2 88.3 %experts_on_rows.1 = (bf16[1536,768]{1,0:T(8,128)(2,1)}, bf16[1536,896]{1,0:T(8,128)(2,1)}, bf16[3,768,2048]{2,1,0:T(8,128)(2,1)}) custom-call(s32[2,1024]{1,0:T(2,128)} %copy.132.slot_ref, bf16[1024,768]{1,0:T(8,128)(2,1)} %get-tuple-element.56.h2_ref, bf16[1024,256]{1,0:T(8,128)(2,1)} %get-tuple-element.57.ext_ref, bf16[1536,768]{1,0:T(8,128)(2,1)} %bitcast.3.g_ref, ...), custom_call_target="tpu_custom_call" | custom-call | flops 43486543872 | bytes 28311552 | tf_op jit(solution)/shard_map/experts_on_rows/pallas_call | solution.py:551
  207.1 4.2 all-to-all-start.1
  211.3 21.1 %combine.1 = (f32[1024,12]{1,0:T(8,128)}, f32[1024,768]{1,0:T(8,128)}, bf16[1024,768]{1,0:T(8,128)(2,1)}, bf16[1024,768]{1,0:T(8,128)(2,1)}, f32[128,768]{1,0:T(8,128)}, /*index=5*/f32[8,768]{1,0:T(8,128)}) custom-call(bf16[1536,896]{1,0:T(8,128)(2,1)} %get-tuple-element.62.back_ref, s32[1024,2]{1,0:T(8,128)} %fusion.13.slot_ref, s32[1024,2]{1,0:T(8,128)} %copy-done, ...), custom_call_target="tpu_custom_call" | custom-call | flops 4831838208 | bytes 20447232 | tf_op jit(solution)/shard_map/combine/pallas_call | solution.py:653
  232.4 63.5 %attn_bwd.1 = (bf16[1024,768]{1,0:T(8,128)(2,1)}, bf16[2560,768]{1,0:T(8,128)(2,1)}, bf16[2560,768]{1,0:T(8,128)(2,1)}) custom-call(s32[1]{0:T(128)} %bitcast.1.e_ref, bf16[1024,768]{1,0:T(8,128)(2,1)} %get-tuple-element.50.q_ref, bf16[1024,768]{1,0:T(8,128)(2,1)} %get-tuple-element.63.do_ref, bf16[1024,768]{1,0:T(8,128)(2,1)} %get-tuple-element.55.o_ref, ...), custom_call_target="tpu_custom_call" | custom-call | flops 32212254720 | bytes 25165824 | tf_op jit(solution)/shard_map/attn_bwd/pallas_call | solution.py:319
  296.7 8.4 %own_back.1 = (f32[1024,768]{1,0:T(8,128)}, f32[1,768]{1,0:T(1,128)}) custom-call(bf16[1024,768]{1,0:T(8,128)(2,1)} %get-tuple-element.65.dq_ref, bf16[2560,768]{1,0:T(8,128)(2,1)} %get-tuple-element.66.dk_ref, bf16[2560,768]{1,0:T(8,128)(2,1)} %get-tuple-element.67.dv_ref, bf16[768,768]{1,0:T(8,128)(2,1)} %wq_ref.1, bf16[768,768]{1,0:T(8,128)(2,1)} %wk_ref.3, ...), custom_call_target="tpu_custom_call" | custom-call | flops 2415919104 | bytes 6291456 | tf_op jit(solution)/shard_map/own_back/pallas_call | solution.py:756
  305.1 11.5 %prompt_back.1 = (bf16[2048,768]{1,0:T(8,128)(2,1)}, f32[1,768]{1,0:T(1,128)}) custom-call(bf16[2560,768]{1,0:T(8,128)(2,1)} %get-tuple-element.66.dk_ref, bf16[2560,768]{1,0:T(8,128)(2,1)} %get-tuple-element.67.dv_ref, bf16[768,768]{1,0:T(8,128)(2,1)} %wk_ref.3, bf16[768,768]{1,0:T(8,128)(2,1)} %wv_ref.3, bf16[2048,768]{1,0:T(8,128)(2,1)} %all-gather.2.cloned.1.call-done.x_ref), custom_call_target="tpu_custom_call" | custom-call | flops 4831838208 | bytes 12582912 | tf_op jit(solution)/shard_map/prompt_back/pallas_call | solution.py:716
  318.0 18.9 %weight_back.1.g_ref = bf16[3072,768]{1,0:T(8,128)(2,1)} custom-call(bf16[2048,768]{1,0:T(8,128)(2,1)} %get-tuple-element.69.hp_ref, bf16[1024,768]{1,0:T(8,128)(2,1)} %get-tuple-element.70.ho_ref, bf16[1024,768]{1,0:T(8,128)(2,1)} %get-tuple-element.55.o_ref, bf16[1024,768]{1,0:T(8,128)(2,1)} %get-tuple-element.71.da_ref, ...), custom_call_target="tpu_custom_call" | custom-call | flops 9663676416 | bytes 11010048 | tf_op jit(solution)/shard_map/weight_back/pallas_call | solution.py:809
  336.9 98.4 %device_sums.1 = (bf16[3072,768]{1,0:T(8,128)(2,1)}, f32[24,768]{1,0:T(8,128)}, f32[512,768]{1,0:T(8,128)}) custom-call(bf16[3072,768]{1,0:T(8,128)(2,1)} %weight_back.1.g_ref, f32[24,768]{1,0:T(8,128)} %maximum_maximum_fusion.1.small_ref, bf16[2048,768]{1,0:T(8,128)(2,1)} %get-tuple-element.76.dh_ref), custom_call_target="tpu_custom_call" | custom-call | flops 9437184 | bytes 18874368 | tf_op jit(solution)/shard_map/device_sums/pallas_call | solution.py:1020
  435.3 3.2 copy.150
  439.9 3.8 all-to-all-start.2
  446.3 7.0 %token_back.1 = f32[1024,768]{1,0:T(8,128)} custom-call(f32[1024,768]{1,0:T(8,128)} %get-tuple-element.68.own_ref, f32[512,768]{1,0:T(8,128)} %get-tuple-element.77.got_ref, bf16[1024,768]{1,0:T(8,128)(2,1)} %x_ref.3, f32[1024,768]{1,0:T(8,128)} %get-tuple-element.78.dx2_ref, f32[1,768]{1,0:T(1,128)} %broadcast_in_dim.33.gain_ref), custom_call_target="tpu_custom_call" | custom-call | flops 7864320 | bytes 11010048 | tf_op jit(solution)/shard_map/token_back/pallas_call | solution.py:845
  454.0 3.8 fusion.25
  457.8 9.3 %mix.1 = bf16[1024,768]{1,0:T(8,128)(2,1)} custom-call(bf16[1536,768]{1,0:T(8,128)(2,1)} %bitcast.39, s32[1024,2]{1,0:T(8,128)} %fusion.13.slot_ref, s32[1024,2]{1,0:T(8,128)} %copy-done, f32[1024,128]{1,0:T(8,128)} %get-tuple-element.60.aux_ref, f32[1024,768]{1,0:T(8,128)} %get-tuple-element.61.x2_ref, bf16[1024,768]{1,0:T(8,128)(2,1)} %get-tuple-element.56.h2_ref, ...), custom_call_target="tpu_custom_call" | custom-call | flops 4831838208 | bytes 9437184 | tf_op jit(solution)/shard_map/mix/pallas_call | solution.py:684
  467.1 4.4 all-to-all-done.2
  471.9 2.2 slice_bitcast_fusion
  474.0 1.6 copy.146
  (75 shorter events, 16.3 us)
Async XLA Ops:
  7.2 2.2 copy-start.6
  7.2 2.6 copy-start.13
  7.2 44.8 %all-gather.2.cloned.1.call-start = ((), (), s32[]{:S(2)}) async-start(), calls=%async_computation.4 | async-start | bytes 3932160 | tf_op jit(solution)/shard_map/all_gather | solution.py:1075
  9.6 9.5 %copy-start = (s32[1024,2]{1,0:T(8,128)}, s32[1024,2]{1,0:T(8,128)S(1)}, u32[]{:S(2)}) copy-start(s32[1024,2]{1,0:T(8,128)S(1)} %copy.124.routes_ref) | copy-start | bytes 24580
  19.1 5.1 %copy-start.10 = (f32[768]{0:T(1024)S(1)}, f32[768]{0:T(1024)}, u32[]{:S(2)}) copy-start(f32[768]{0:T(1024)} %param.23) | copy-start | bytes 9220
  19.1 5.7 %copy-start.11 = (f32[768]{0:T(1024)S(1)}, f32[768]{0:T(1024)}, u32[]{:S(2)}) copy-start(f32[768]{0:T(1024)} %param.28) | copy-start | bytes 9220
  19.1 6.3 %copy-start.9 = (bf16[2,768,2]{1,2,0:T(2,128)(2,1)S(1)}, bf16[2,768,2]{1,2,0:T(2,128)(2,1)}, u32[]{:S(2)}) copy-start(bf16[2,768,2]{1,2,0:T(2,128)(2,1)} %param.30) | copy-start | bytes 18436
  19.1 6.5 %copy-start.7 = (bf16[768,12]{0,1:T(8,128)(2,1)S(1)}, bf16[768,12]{0,1:T(8,128)(2,1)}, u32[]{:S(2)}) copy-start(bf16[768,12]{0,1:T(8,128)(2,1)} %param.29) | copy-start | bytes 55300
  19.1 6.7 %copy-start.5 = (f32[1024,12]{0,1:T(8,128)S(1)}, f32[1024,12]{0,1:T(8,128)}, u32[]{:S(2)}) copy-start(f32[1024,12]{0,1:T(8,128)} %param.20) | copy-start | bytes 147460
  19.1 97.1 %all-to-all-start = ((bf16[8,192,768]{2,1,0:T(8,128)(2,1)}), bf16[8,192,768]{2,1,0:T(8,128)(2,1)}, u32[]{:S(2)}, u32[]{:S(2)}) async-start(bf16[8,192,768]{2,1,0:T(8,128)(2,1)} %dispatch_grads.1), calls=%async_computation | async-start | bytes 4718592 | tf_op jit(solution)/shard_map/all_to_all | solution.py:1070
  24.2 411.1 %reduce-scatter.2.cloned.1.call-start = ((), (), s32[]{:S(2)}) async-start(), calls=%async_computation.5 | async-start | bytes 11796480 | tf_op jit(solution)/shard_map/reduce_scatter | solution.py:1091
  204.5 1.0 copy-start.1
  207.1 231.4 %all-to-all-start.1 = ((bf16[8,192,768]{2,1,0:T(8,128)(2,1)}), bf16[8,192,768]{2,1,0:T(8,128)(2,1)S(1)}, u32[]{:S(2)}, u32[]{:S(2)}) async-start(bf16[8,192,768]{2,1,0:T(8,128)(2,1)} %bitcast.40), calls=%async_computation.1 | async-start | bytes 4718592 | tf_op jit(solution)/shard_map/all_to_all | solution.py:1070
  232.4 63.5 %copy-start.8 = (f32[8,768]{1,0:T(8,128)S(1)}, f32[8,768]{1,0:T(8,128)}, u32[]{:S(2)}) copy-start(f32[8,768]{1,0:T(8,128)} %get-tuple-element.73) | copy-start | bytes 73732
  305.1 11.5 %copy-start.12 = (f32[1,768]{1,0:T(1,128)S(1)}, f32[1,768]{1,0:T(1,128)}, u32[]{:S(2)}) copy-start(f32[1,768]{1,0:T(1,128)} %get-tuple-element.75) | copy-start | bytes 9220
  438.5 1.4 copy-start.2
  438.5 5.2 %copy-start.4 = (f32[24,768]{1,0:T(8,128)S(1)}, f32[24,768]{1,0:T(8,128)}, u32[]{:S(2)}) copy-start(f32[24,768]{1,0:T(8,128)} %get-tuple-element.80) | copy-start | bytes 221188
  438.5 7.0 %copy-start.3 = (f32[1024,12]{1,0:T(8,128)S(1)}, f32[1024,12]{1,0:T(8,128)}, u32[]{:S(2)}) copy-start(f32[1024,12]{1,0:T(8,128)} %get-tuple-element.145) | copy-start | bytes 147460
  439.9 31.6 %all-to-all-start.2 = ((bf16[2,3,768,256]{3,2,1,0:T(8,128)(2,1)}), bf16[2,3,768,256]{3,2,1,0:T(8,128)(2,1)S(1)}, u32[]{:S(2)}, u32[]{:S(2)}) async-start(bf16[2,3,768,256]{3,2,1,0:T(8,128)(2,1)} %bitcast.38), calls=%async_computation.3 | async-start | bytes 4718592 | tf_op jit(solution)/shard_map/all_to_all | solution.py:1111
  446.3 7.6 %slice-start = ((s8[4718592]{0:T(1024)(128)(4,1)}), s8[4194304]{0:T(1024)(128)(4,1)S(1)}, s32[]{:S(2)}) async-start(s8[4718592]{0:T(1024)(128)(4,1)} %bitcast.35), calls=%async_computation.6 | async-start | bytes 8388608
  446.3 7.6 %slice-start.1 = ((s8[4718592]{0:T(1024)(128)(4,1)}), s8[524288]{0:T(1024)(128)(4,1)S(1)}, s32[]{:S(2)}) async-start(s8[4718592]{0:T(1024)(128)(4,1)} %bitcast.35), calls=%async_computation.7 | async-start | bytes 1048576
Sparse Core Ops, SparseCore 0:
  10.2 41.8 all-gather.1
  204.7 161.1 reduce-scatter.1

commit v5 on v4

--- a/solution.py
+++ b/solution.py
@@ -694,181 +694,30 @@
     )(made, slots, routes, aux, x2, h2, const_v)
 
 
-def prompt_back_kernel(dk_ref, dv_ref, wk_ref, wv_ref, x_ref, out_ref, sum_ref):
-    dh = dot(dk_ref[...], wk_ref[...], NT) + dot(dv_ref[...], wv_ref[...], NT)
-    out_ref[...] = dh.astype(BF)
-    x = x_ref[...].astype(F32)
-    part = jnp.sum(dh * (x * rms_scale(x)), axis=0, keepdims=True)
-    step = pl.program_id(0)
-
-    @pl.when(step == 0)
-    def _():
-        sum_ref[...] = part
-
-    @pl.when(step > 0)
-    def _():
-        sum_ref[...] += part
-
-
-def prompt_back(dk, dv, w_key, w_value, x, tile=256):
-    rows, width = x.shape
-    block = pl.BlockSpec((tile, width), lambda i: (i, 0))
-    return pl.pallas_call(
-        prompt_back_kernel,
-        grid=(rows // tile,),
-        in_specs=[block, block, whole(w_key.shape), whole(w_value.shape), block],
-        out_specs=[block, whole((1, width))],
-        out_shape=[jax.ShapeDtypeStruct((rows, width), BF), jax.ShapeDtypeStruct((1, width), F32)],
-        compiler_params=params(),
-        cost_estimate=pl.CostEstimate(flops=4 * rows * width * width, bytes_accessed=8 * rows * width, transcendentals=0),
-        name="prompt_back",
-    )(dk, dv, w_key, w_value, x)
-
-
-def own_back_kernel(dq_ref, dk_ref, dv_ref, wq_ref, wk_ref, wv_ref, x_ref, out_ref, sum_ref):
-    step = pl.program_id(0)
-    x = x_ref[...].astype(F32)
-    xr = x * rms_scale(x)
-
-    @pl.when(step == 0)
-    def _():
-        sum_ref[...] = jnp.zeros_like(sum_ref)
-
-    def put(dh):
-        out_ref[...] = dh
-        sum_ref[...] += jnp.sum(dh * xr, axis=0, keepdims=True)
-
-    @pl.when(step < pl.num_programs(0) // 2)
-    def _():
-        put(dot(dq_ref[...], wq_ref[...], NT))
-
-    @pl.when(step >= pl.num_programs(0) // 2)
-    def _():
-        put(dot(dq_ref[...], wq_ref[...], NT) + dot(dk_ref[...], wk_ref[...], NT) + dot(dv_ref[...], wv_ref[...], NT))
-
-
-def own_back(dq, dk, dv, w_query, w_key, w_value, x, tile=256):
-    rows, width = x.shape
-    block = pl.BlockSpec((tile, width), lambda i: (i, 0))
-    half = rows // 2 // tile
-    first = (dk.shape[0] - rows // 2) // tile
-    key = pl.BlockSpec((tile, width), lambda i: (first + jnp.maximum(i - half, 0), 0))
-    return pl.pallas_call(
-        own_back_kernel,
-        grid=(rows // tile,),
-        in_specs=[block, key, key] + [whole(w_key.shape)] * 3 + [block],
-        out_specs=[block, whole((1, width))],
-        out_shape=[jax.ShapeDtypeStruct((rows, width), F32), jax.ShapeDtypeStruct((1, width), F32)],
-        compiler_params=params(),
-        cost_estimate=pl.CostEstimate(flops=4 * rows * width * width, bytes_accessed=8 * rows * width, transcendentals=0),
-        name="own_back",
-    )(dq, dk, dv, w_query, w_key, w_value, x)
-
-
-def weight_back_kernel(hp_ref, ho_ref, o_ref, da_ref, dq_ref, dk_ref, dv_ref, out_ref, acc_ref, *, prompt_steps, own_steps):
-    step = pl.program_id(0)
-    half = own_steps // 2
-
-    @pl.when(step == 0)
-    def _():
-        acc_ref[...] = jnp.zeros_like(acc_ref)
-
-    @pl.when(step < prompt_steps)
-    def _():
-        ht = hp_ref[...].T
-        acc_ref[1] += dot(ht, dk_ref[...])
-        acc_ref[2] += dot(ht, dv_ref[...])
-
-    @pl.when(step >= prompt_steps)
-    def _():
-        ht = ho_ref[...].T
-        acc_ref[0] += dot(ht, dq_ref[...])
-        acc_ref[3] += dot(o_ref[...].T, da_ref[...])
-
-        @pl.when(step >= prompt_steps + half)
-        def _():
-            acc_ref[1] += dot(ht, dk_ref[...])
-            acc_ref[2] += dot(ht, dv_ref[...])
-
-    @pl.when(step == pl.num_programs(0) - 1)
-    def _():
-        width = acc_ref.shape[1]
-        for n in range(4):
-            out_ref[n * width:(n + 1) * width, :] = acc_ref[n].astype(BF)
-        if out_ref.shape[0] > 4 * width:
-            out_ref[4 * width:, :] = jnp.zeros((out_ref.shape[0] - 4 * width, width), BF)
-
-
-def weight_back(hp, ho, o, da, dq, dk, dv, out_rows, tile=256):
-    rows, width = ho.shape
-    ps, os_ = hp.shape[0] // tile, rows // tile
-    half = os_ // 2
-    prompt = pl.BlockSpec((tile, width), lambda i: (jnp.minimum(i, ps - 1), 0))
-    own = pl.BlockSpec((tile, width), lambda i: (jnp.maximum(i - ps, 0), 0))
-    key = pl.BlockSpec((tile, width), lambda i: (jnp.where(i < ps + half, jnp.minimum(i, ps - 1), i - half), 0))
-    return pl.pallas_call(
-        functools.partial(weight_back_kernel, prompt_steps=ps, own_steps=os_),
-        grid=(ps + os_,),
-        in_specs=[prompt, own, own, own, own, key, key],
-        out_specs=whole((out_rows, width)),
-        out_shape=jax.ShapeDtypeStruct((out_rows, width), BF),
-        scratch_shapes=[pltpu.VMEM((4, width, width), F32)],
-        compiler_params=params(),
-        cost_estimate=pl.CostEstimate(flops=16 * rows * width * width, bytes_accessed=14 * rows * width, transcendentals=0),
-        name="weight_back",
-    )(hp, ho, o, da, dq, dk, dv)
-
-
-def token_back_kernel(own_ref, got_ref, x_ref, dx2_ref, gain_ref, out_ref):
-    x = x_ref[...].astype(F32)
-    r1 = rms_scale(x)
-
-    def put(dh):
-        u = dh * gain_ref[...]
-        out_ref[...] = dx2_ref[...] + r1 * (u - x * (r1 * r1) * jnp.mean(u * x, axis=-1, keepdims=True))
-
-    step = pl.program_id(0)
-
-    @pl.when(step < pl.num_programs(0) // 2)
-    def _():
-        put(own_ref[...] + got_ref[...])
-
-    @pl.when(step >= pl.num_programs(0) // 2)
-    def _():
-        put(own_ref[...])
-
-
-def token_back(own, got, x, dx2, gain, tile=256):
-    rows, width = x.shape
-    block = pl.BlockSpec((tile, width), lambda i: (i, 0))
-    half = rows // 2 // tile
-    return pl.pallas_call(
-        token_back_kernel,
-        grid=(rows // tile,),
-        in_specs=[block, pl.BlockSpec((tile, width), lambda i: (jnp.minimum(i, half - 1), 0)), block, block,
-                  whole(gain.shape)],
-        out_specs=block,
-        out_shape=jax.ShapeDtypeStruct((rows, width), F32),
-        compiler_params=params(),
-        cost_estimate=pl.CostEstimate(flops=10 * rows * width, bytes_accessed=14 * rows * width, transcendentals=0),
-        name="token_back",
-    )(own, got, x, dx2, gain)
-
-
 def padded_rows(rows, rest):
     unit = 8 * rest * 16
     return -(-rows // unit) * unit
 
 
-def sum_kernel(g_ref, small_ref, dh_ref, out_ref, small_out_ref, got_ref, half_ref, r0_ref, t1_ref, r1_ref, t2_ref, r2_ref,
-               r3_ref, sm_ref, rs_ref, rd0_ref, td_ref, rd1_ref, send_sem, recv_sem, *, rest, chunks):
+def finale_kernel(small_ref, gain_ref, *refs, rest, chunks, norm_row, tile):
+    hbm, refs = refs[:12], refs[12:]
+    out_ref, small_out_ref, token_hbm = refs[:3]
+    local, refs = refs[3:15], refs[15:]
+    (turned_ref, g_ref, norm_ref, dh_ref, r0_ref, sm_ref, rs_ref, rd0_ref, td_ref, rd1_ref, tok_ref,
+     load_sem, tok_sem, send_sem, recv_sem) = refs[:15]
+    r1_ref, r2_ref, r3_ref = (refs[15 + 2 * n:17 + 2 * n] for n in range(3))
+    ho_ref, dq_ref, o_ref, da_ref, wq_ref, dk_ref, wk_ref, dv_ref, wv_ref, hp_ref, x_ref, dx2_ref = local[:12]
+
+    loads = [pltpu.make_async_copy(src, dst, load_sem.at[n]) for n, (src, dst) in enumerate(zip(hbm, local))]
+    for copy in loads:
+        copy.start()
+
     dp, ex = lax.axis_index("dp"), lax.axis_index("expert")
     c, x, y, z = ex % 2, ex // 2, dp % 2, dp // 2
     mate = (dp, x * 2 + 1 - c)
     across = (dp, (1 - x) * 2 + c)
     beside = (z * 2 + 1 - y, ex)
     ahead = [((z + d) % rest * 2 + y, ex) for d in range(1, rest)]
-
     barrier = pltpu.get_barrier_semaphore()
     for peer in [mate, across, beside] + ahead:
         pl.semaphore_signal(barrier, inc=1, device_id=peer, device_id_type=MESH)
@@ -885,11 +734,13 @@
         return copy
 
     rows, width = g_ref.shape
+    own = ho_ref.shape[0]
+    prompt = hp_ref.shape[0]
     half = rows // 2
     size = half // chunks
-    lanes = width // 2
     q1, q2, q3 = size // 2, size // 4, size // 4 // rest
-    part = [pl.ds(0, lanes), pl.ds(lanes, lanes)]
+    cut = width // 3
+    part = [pl.ds(0, cut), pl.ds(cut, width - cut)]
     first, second = [across, beside], [beside, across]
     bit1, bit2 = [x, y], [y, x]
 
@@ -907,34 +758,34 @@
 
     def stage1(k):
         sl = pl.ds(k * size, size)
-        half_ref[sl] = (g_ref[ds(c * half + k * size, size)].astype(F32) + r0_ref[sl].astype(F32)).astype(BF)
-        return [send(half_ref.at[ds(at1(k, p, 1 - bit1[p]), q1), part[p]], r1_ref.at[p, pl.ds(k * q1, q1)], first[p])
+        r0_ref[sl] = (g_ref[ds(c * half + k * size, size)].astype(F32) + r0_ref[sl].astype(F32)).astype(BF)
+        return [send(r0_ref.at[ds(at1(k, p, 1 - bit1[p]), q1), part[p]], r1_ref[p].at[pl.ds(k * q1, q1)], first[p])
                 for p in range(2)]
 
     def stage2(k):
         out = []
         for p in range(2):
             sl = pl.ds(k * q1, q1)
-            t1_ref[p, sl] = (half_ref[ds(at1(k, p, bit1[p]), q1), part[p]].astype(F32) + r1_ref[p, sl].astype(F32)).astype(BF)
-            out.append(send(t1_ref.at[p, ds(k * q1 + (1 - bit2[p]) * q2, q2)], r2_ref.at[p, pl.ds(k * q2, q2)], second[p]))
+            r1_ref[p][sl] = (r0_ref[ds(at1(k, p, bit1[p]), q1), part[p]].astype(F32) + r1_ref[p][sl].astype(F32)).astype(BF)
+            out.append(send(r1_ref[p].at[ds(k * q1 + (1 - bit2[p]) * q2, q2)], r2_ref[p].at[pl.ds(k * q2, q2)], second[p]))
         return out
 
     def stage3(k):
         out = []
         for p in range(2):
             sl = pl.ds(k * q2, q2)
-            t2_ref[p, sl] = (t1_ref[p, ds(k * q1 + bit2[p] * q2, q2)].astype(F32) + r2_ref[p, sl].astype(F32)).astype(BF)
+            r2_ref[p][sl] = (r1_ref[p][ds(k * q1 + bit2[p] * q2, q2)].astype(F32) + r2_ref[p][sl].astype(F32)).astype(BF)
             for d in range(1, rest):
                 to = (z + d) % rest
-                out.append(send(t2_ref.at[p, ds(k * q2 + to * q3, q3)], r3_ref.at[p, d - 1, pl.ds(k * q3, q3)], ahead[d - 1]))
+                out.append(send(r2_ref[p].at[ds(k * q2 + to * q3, q3)], r3_ref[p].at[d - 1, pl.ds(k * q3, q3)], ahead[d - 1]))
         return out
 
     def stage4(k):
         out = []
         for p in range(2):
-            total = t2_ref[p, ds(k * q2 + z * q3, q3)].astype(F32)
+            total = r2_ref[p][ds(k * q2 + z * q3, q3)].astype(F32)
             for d in range(1, rest):
-                total = total + r3_ref[p, d - 1, pl.ds(k * q3, q3)].astype(F32)
+                total = total + r3_ref[p][d - 1, pl.ds(k * q3, q3)].astype(F32)
             mine = ds(c * half + spot2(k, p, bit2[p]) + z * q3, q3)
             out_ref[mine, part[p]] = total.astype(BF)
             for d in range(1, rest):
@@ -959,80 +810,199 @@
         mine = ds(c * half + k * size, size)
         return [send(out_ref.at[mine], out_ref.at[mine], mate)]
 
-    block = got_ref.shape[0]
+    stages = (stage0, stage1, stage2, stage3, stage4, stage5, stage6, stage7)
+    waiting = {}
+
+    def wait(line):
+        for copy in waiting.pop(line, []):
+            copy.wait_recv()
+
+    def step(k, s):
+        wait(k)
+        waiting[k] = stages[s](k) if s < len(stages) else []
+
+    block = own // 2
 
     def dh_rows(xx, cc):
         return ds((xx * 2 + cc) * block, block)
 
-    def dh0():
-        return [send(dh_ref.at[dh_rows(w, 1 - c)], rd0_ref.at[w], mate) for w in range(2)]
-
-    def dh1():
+    def prompt_rows(cc):
+        @pl.loop(0, 2 * (block // tile))
+        def _(i):
+            at = ds((i // (block // tile) * 2 + cc) * block + i % (block // tile) * tile, tile)
+            dh_ref[at] = (dot(dk_ref[at], wk_ref[...], NT) + dot(dv_ref[at], wv_ref[...], NT)).astype(BF)
+
+    small_peers = [mate, across, beside]
+
+    def small_step(n):
+        wait("small")
+        if n < 4:
+            sm_ref[n] = small_ref[...] if n == 0 else sm_ref[n - 1] + rs_ref[n - 1]
+            if n == 0:
+                at = lax.broadcasted_iota(jnp.int32, (small_ref.shape[0], 1), 0)
+                norm = jnp.sum(norm_ref[...].T, axis=0, keepdims=True) / gain_ref[...]
+                sm_ref[0] = jnp.where(at == norm_row, norm, small_ref[...])
+        if n < 3:
+            waiting["small"] = [send(sm_ref.at[n], rs_ref.at[n], small_peers[n])]
+        elif n == 3:
+            waiting["small"] = [send(sm_ref.at[3], rs_ref.at[2 + d], ahead[d - 1]) for d in range(1, rest)]
+        else:
+            total = sm_ref[3]
+            for d in range(1, rest):
+                total = total + rs_ref[2 + d]
+            small_out_ref[...] = total
+
+    strip = width // 3
+
+    def gradient(b, terms, first_row, w_ref):
+        mine = slice(b * strip, (b + 1) * strip)
+        got = sum(dot(turned_ref[mine, at:at + count], rhs_ref[...]) for at, count, rhs_ref in terms)
+        g_ref[first_row + b * strip:first_row + (b + 1) * strip, :] = got.astype(BF)
+        if w_ref is not None:
+            share = got * w_ref[mine, :].astype(F32)
+            norm_ref[mine, :] += sum(share[:, n:n + 128] for n in range(0, width, 128))
+
+    def put_tokens(i, dh, copies):
+        at = pl.ds(i * tile, tile)
+        xf = x_ref[at].astype(F32)
+        r1 = rms_scale(xf)
+        u = dh * gain_ref[...]
+        slot = i % 2
+        tok_ref[slot] = dx2_ref[at] + r1 * (u - xf * (r1 * r1) * jnp.mean(u * xf, axis=-1, keepdims=True))
+        copy = pltpu.make_async_copy(tok_ref.at[slot], token_hbm.at[at], tok_sem.at[slot])
+        copy.start()
+        copies.append(copy)
+
+    if rows > 4 * width:
+        g_ref[4 * width:, :] = jnp.zeros((rows - 4 * width, width), BF)
+    norm_ref[...] = jnp.zeros_like(norm_ref)
+    tokens = []
+
+    def own_tokens(i):
+        at = pl.ds(i * tile, tile)
+        dh = dot(dq_ref[at], wq_ref[...], NT)
+        if i * tile >= block:
+            kv = pl.ds(prompt + i * tile - block, tile)
+            dh = dh + dot(dk_ref[kv], wk_ref[...], NT) + dot(dv_ref[kv], wv_ref[...], NT)
+        else:
+            inner = ds((x * 2 + c) * block + i * tile, tile)
+            dh = dh + dh_ref[inner].astype(F32) + rd0_ref[x, at].astype(F32) + rd1_ref[at].astype(F32)
+        if len(tokens) >= 2:
+            tokens[-2].wait()
+        put_tokens(i, dh, tokens)
+
+    hops = (4.5, 6.0, 5.0, 6.5, 6.5, 5.0, 6.0, 4.5)
+    due = []
+
+    def begin(now, k):
+        step(k, 0)
+        due.append([now + hops[0], k, 1])
+
+    def ready(now):
+        for entry in sorted(due, key=lambda entry: (entry[0], str(entry[1]))):
+            if entry[0] <= now:
+                _, k, s = entry
+                due.remove(entry)
+                if k == "small":
+                    small_step(s)
+                    last = 4
+                else:
+                    step(k, s)
+                    last = len(stages)
+                if s < last:
+                    due.append([max(now, entry[0]) + (hops[s] if k != "small" else 5.0), k, s + 1])
+
+    def wait_loads(*numbers):
+        for n in numbers:
+            loads[n].wait()
+
+    def first_turn():
+        wait_loads(0, 1, 2, 3, 4)
+        turned_ref[:, :own] = ho_ref[...].T
+        turned_ref[:, own:2 * own] = o_ref[...].T
+
+    def second_turn():
+        wait_loads(5, 6, 7, 8, 9)
+        turned_ref[:, :prompt] = hp_ref[...].T
+        turned_ref[:, prompt:] = ho_ref[block:].T
+
+    def first_grads(b):
+        gradient(b, [(0, own, dq_ref)], 0, wq_ref)
+        gradient(b, [(own, own, da_ref)], 2 * width, None)
+
+    def second_grads(b):
+        gradient(b, [(0, prompt + block, dk_ref)], width, wk_ref)
+        gradient(b, [(0, prompt + block, dv_ref)], 3 * width, wv_ref)
+
+    def mates():
+        prompt_rows(1 - c)
+        waiting["dh"] = [send(dh_ref.at[dh_rows(w, 1 - c)], rd0_ref.at[w], mate) for w in range(2)]
+
+    def over():
+        wait("dh")
         td_ref[...] = (dh_ref[dh_rows(1 - x, c)].astype(F32) + rd0_ref[1 - x].astype(F32)).astype(BF)
-        return [send(td_ref, rd1_ref, across)]
-
-    def dh2():
-        got_ref[...] = dh_ref[dh_rows(x, c)].astype(F32) + rd0_ref[x].astype(F32) + rd1_ref[...].astype(F32)
-        return []
-
-    def small_pair(n, peer):
-        def run():
-            if n:
-                sm_ref[n] = sm_ref[n - 1] + rs_ref[n - 1]
-            else:
-                sm_ref[0] = small_ref[...]
-            return [send(sm_ref.at[n], rs_ref.at[n], peer)]
-        return run
-
-    def small_rest():
-        sm_ref[3] = sm_ref[2] + rs_ref[2]
-        return [send(sm_ref.at[3], rs_ref.at[2 + d], ahead[d - 1]) for d in range(1, rest)]
-
-    def small_end():
-        total = sm_ref[3]
-        for d in range(1, rest):
-            total = total + rs_ref[2 + d]
-        small_out_ref[...] = total
-        return []
-
-    lines = [[functools.partial(f, k) for f in (stage0, stage1, stage2, stage3, stage4, stage5, stage6, stage7)]
-             for k in range(chunks)]
-    lines.insert(1, [dh0, dh1, dh2])
-    lines.append([small_pair(0, mate), small_pair(1, across), small_pair(2, beside), small_rest, small_end])
-    waiting = [[] for _ in lines]
-    for t in range(max(n + len(line) for n, line in enumerate(lines)) + 1):
-        for n, line in enumerate(lines):
-            s = t - n
-            if 0 <= s <= len(line):
-                for copy in waiting[n]:
-                    copy.wait_recv()
-                waiting[n] = line[s]() if s < len(line) else []
+        waiting["dh"] = [send(td_ref, rd1_ref, across)]
+
+    def prompt_tokens(i):
+        wait("dh")
+        own_tokens(i)
+
+    blocks = own // tile
+    tasks = [(4.0, first_turn)] + [(2.0, functools.partial(first_grads, b)) for b in range(3)] + [(3.0, second_turn)]
+    tasks += [(4.0, functools.partial(second_grads, b)) for b in range(3)]
+    tasks += [(4.0, mates), (4.0, lambda: prompt_rows(c)), (0.5, over)]
+    tasks += [(2.0, lambda: wait_loads(10, 11))] + [(2.0, functools.partial(own_tokens, i)) for i in range(blocks // 2, blocks)]
+    after = {1: [0], 2: [1], 3: [2], 5: [3], 6: [4], 7: [5]} if chunks == 6 else {7: list(range(chunks))}
+    now = 0.0
+    for n, (length, task) in enumerate(tasks):
+        task()
+        now += length
+        for k in after.get(n, []):
+            begin(now, k)
+        if n == 7:
+            small_step(0)
+            due.append([now + 5.0, "small", 1])
+        ready(now)
+    late = list(range(blocks // 2))
+    while due or late:
+        now = max(now, min(entry[0] for entry in due)) if due else now
+        ready(now)
+        if late and (now > 52.0 or not due):
+            prompt_tokens(late.pop(0))
+            now += 2.0
+    for copy in tokens[-2:]:
+        copy.wait()
     for copy in started:
         copy.wait_send()
 
 
-def device_sums(g, small, dh, rest, block, chunks):
-    rows, width = g.shape
-    half, lanes = rows // 2, width // 2
+def finale(small, gain, arrays, rest, norm_row, out_rows, tile=256):
+    own, width = arrays[0].shape
+    prompt = arrays[9].shape[0]
+    block = own // 2
+    half = out_rows // 2
+    chunks = 6 if half == 6 * 4 * rest * 16 else 1
+    lanes = (width // 3, width - width // 3)
     copies = chunks * (1 + 2 + 2 + 2 * (rest - 1) * 2 + 2 + 2 + 1) + 3 + 3 + rest - 1
-    vm = pltpu.VMEM
-    vmem = pl.BlockSpec(memory_space=pltpu.VMEM)
+    vm, dma = pltpu.VMEM, pltpu.SemaphoreType.DMA
+    vmem, hbm = pl.BlockSpec(memory_space=pltpu.VMEM), pl.BlockSpec(memory_space=pl.ANY)
     return pl.pallas_call(
-        functools.partial(sum_kernel, rest=rest, chunks=chunks),
-        in_specs=[vmem] * 3,
-        out_specs=[vmem] * 3,
-        out_shape=[jax.ShapeDtypeStruct(g.shape, BF), jax.ShapeDtypeStruct(small.shape, F32),
-                   jax.ShapeDtypeStruct((block, width), F32)],
-        scratch_shapes=[
-            vm((half, width), BF), vm((half, width), BF), vm((2, half // 2, lanes), BF), vm((2, half // 2, lanes), BF),
-            vm((2, half // 4, lanes), BF), vm((2, half // 4, lanes), BF), vm((2, rest - 1, half // 4 // rest, lanes), BF),
-            vm((4,) + small.shape, F32), vm((2 + rest,) + small.shape, F32), vm((2, block, width), BF), vm((block, width), BF),
-            vm((block, width), BF), pltpu.SemaphoreType.DMA((copies,)), pltpu.SemaphoreType.DMA((copies,)),
-        ],
-        compiler_params=params(collective_id=0, has_side_effects=True),
-        cost_estimate=pl.CostEstimate(flops=4 * rows * width, bytes_accessed=8 * rows * width, transcendentals=0),
-        name="device_sums",
-    )(g, small, dh)
+        functools.partial(finale_kernel, rest=rest, chunks=chunks, norm_row=norm_row, tile=tile),
+        in_specs=[vmem] * 2 + [hbm] * len(arrays),
+        out_specs=[vmem, vmem, hbm],
+        out_shape=[jax.ShapeDtypeStruct((out_rows, width), BF), jax.ShapeDtypeStruct(small.shape, F32),
+                   jax.ShapeDtypeStruct((own, width), F32)],
+        scratch_shapes=[vm(a.shape, a.dtype) for a in arrays] + [
+            vm((width, prompt + block), BF), vm((out_rows, width), BF), vm((width, 128), F32), vm((prompt, width), BF),
+            vm((half, width), BF), vm((4,) + small.shape, F32), vm((2 + rest,) + small.shape, F32),
+            vm((2, block, width), BF), vm((block, width), BF), vm((block, width), BF), vm((2, tile, width), F32),
+            dma((len(arrays),)), dma((2,)), dma((copies,)), dma((copies,)),
+        ] + [vm((half // n, k), BF) for n in (2, 4) for k in lanes]
+        + [vm((rest - 1, half // 4 // rest, k), BF) for k in lanes],
+        compiler_params=pltpu.CompilerParams(vmem_limit_bytes=62 << 20, collective_id=0, has_side_effects=True),
+        cost_estimate=pl.CostEstimate(flops=30 * own * width * width, bytes_accessed=8 * out_rows * width, transcendentals=0),
+        name="finale",
+    )(small, gain, *arrays)
 
 
 def slot_table(routes_t, priority, groups, capacity):
@@ -1076,9 +1046,9 @@
     slots_t = slot_table(routes.T, priority, pair, capacity)
     slots = slots_t.T
     grads_out = dispatch(slots_t, cotangent, members, capacity)
-    tokens, grads_out = lax.optimization_barrier((tokens, grads_out))
+    h_own, q, k_own, v_own = project(e, tokens, gain1, (w_query, w_key, w_value), cos, sin, True)
+    prompt_x, grads_out, h_own = lax.optimization_barrier((prompt_x, grads_out, h_own))
     grads_in = swap(grads_out).reshape(-1, width)
-    h_own, q, k_own, v_own = project(e, tokens, gain1, (w_query, w_key, w_value), cos, sin, True)
     h_prompt, k_prompt, v_prompt = project(e, prompt_x, gain1, (w_key, w_value), cos, sin, False)
     o, lse = attn_fwd(e, q, k_own, v_own, k_prompt, v_prompt)
 
@@ -1094,18 +1064,14 @@
         back, slots, routes, aux, x2, h2, cotangent, gain2, wcat, const_v, w_out, experts
     )
     dq, dk, dv = attn_bwd(e, q, do, o, lse, k_own, v_own, k_prompt, v_prompt, cos, sin)
-    dh_prompt, sum_p = prompt_back(dk, dv, w_key, w_value, prompt_x)
-    dh_own, sum_o = own_back(dq, dk, dv, w_query, w_key, w_value, tokens)
     rest = dp // 2
-    out_rows = padded_rows(4 * width, rest)
-    chunks = max(n for n in (1, 2, 3) if out_rows // 2 % (n * 4 * rest * 16) == 0)
-    grad_w = weight_back(h_prompt, h_own, o, da, dq, dk, dv, out_rows)
     n = experts
-    small = jnp.concatenate([cat[:n + 4], sums[:3], sum_p + sum_o, jnp.zeros((4, width), F32)], axis=0)
-    grad_w, small, got = device_sums(grad_w, small, dh_prompt, rest, prompt_dev, chunks)
+    small = jnp.concatenate([cat[:n + 4], sums[:3], jnp.zeros((5, width), F32)], axis=0)
+    grad_w, small, grad_tokens = finale(
+        small, gain1, (h_own, dq, o, da, w_query, dk, w_key, dv, w_value, h_prompt, tokens, dx2), rest, n + 7,
+        padded_rows(4 * width, rest),
+    )
     grad_w = grad_w.astype(F32)
-    grad_tokens = token_back(dh_own, got, tokens, dx2, gain1)
-
     mixed = mix(made, slots, routes, aux, x2, h2, const_v, experts)
     ffn_sum = ffn_sum.reshape(3, width, pair, -1).transpose(2, 0, 1, 3)
     ffn_sum = lax.all_to_all(ffn_sum, "dp", split_axis=0, concat_axis=0, axis_index_groups=pairs, tiled=True)
@@ -1117,8 +1083,8 @@
         small[n + 7],
         grad_w[:width],
         grad_w[width:2 * width],
+        grad_w[3 * width:4 * width],
         grad_w[2 * width:3 * width],
-        grad_w[3 * width:4 * width],
         small[n + 6],
         small[:n].T,
         small[n:n + 4].reshape(2, 2, width).transpose(0, 2, 1),

time: 493 us -> 468 us (0.949)
  Pallas kernels: 406 us -> 380 us
    pallas_call x5 -> x1, Pallas kernels: 144 us -> 118 us  [finale(): pl.pallas_call(functools.partial(finale_kernel, rest=rest, chunks=chunks,...]
  transfers between devices with their start and end apart: 5 -> 5, of which waited for: 2 -> 2; matrix products, arithmetic and copies ran while one was open for 4% -> 5% of each run, Pallas kernels for 66% -> 63%
where the time goes in v5:
time: 468 us; the launch traced here: 462 us
  Pallas kernels  380 us (81%)
  local copies, waits for them, and re-layouts  28.2 us (6%)
  waiting for transfers between devices  20.5 us (4%)
  between operations  14.6 us (3%)
  starting transfers between devices  13.5 us (3%)
    pallas_call x1, Pallas kernels, finale(): pl.pallas_call(functools.partial(finale_kernel, rest=rest, chunks=chunks,...  118 us
    pallas_call x1, Pallas kernels, experts_on_rows(): pl.pallas_call(functools.partial(expert_kernel, capacity=capacity, tile=t...  89.1 us
    pallas_call x1, Pallas kernels, attn_bwd(): pl.pallas_call(functools.partial(attn_bwd_kernel, tile=tile, scale=0.125)...  63.6 us
    pallas_call x1, Pallas kernels, attn_fwd(): pl.pallas_call(functools.partial(attn_fwd_kernel, chunk=chunk, tile=tile,...  44.6 us
    pallas_call x1, Pallas kernels, combine(): pl.pallas_call(functools.partial(combine_kernel, experts=experts), grid=(...  21.2 us
    pallas_call x2, Pallas kernels, project(): pl.pallas_call(functools.partial(project_kernel, count=len(weights)), gri...  20.9 us
    all_gather x1, waiting for transfers between devices, local(): prompt_x = lax.all_gather(tokens[:prompt_dev], 'expert', axis=0, tiled=True)  11.5 us
  transfers between devices with their start and end apart: 5, of which 2 were waited for; matrix products, arithmetic and copies ran while one was open for 5% of the time, Pallas kernels for 63%

profile of v5, /device:TPU:9, one launch (start us, length us, event | category | flops | bytes accessed | tf_op | source)
XLA Modules:
  0.0 462.1 jit_solution(8664639068116409128)
XLA Ops:
  7.3 2.1 slice.45
  12.9 6.8 %dispatch_grads.1 = bf16[8,192,768]{2,1,0:T(8,128)(2,1)} custom-call(s32[2,1024]{1,0:T(2,128)} %copy.132.slot_ref, bf16[1024,768]{1,0:T(8,128)(2,1)} %g_ref.1), custom_call_target="tpu_custom_call" | custom-call | flops 2415919104 | bytes 3145728 | tf_op jit(solution)/shard_map/dispatch_grads/pallas_call | solution.py:408
  19.7 9.2 %project_own.1 = (bf16[1024,768]{1,0:T(8,128)(2,1)}, bf16[1024,768]{1,0:T(8,128)(2,1)}, bf16[1024,768]{1,0:T(8,128)(2,1)}, bf16[1024,768]{1,0:T(8,128)(2,1)}) custom-call(s32[1]{0:T(128)} %bitcast.1.e_ref, bf16[1024,768]{1,0:T(8,128)(2,1)} %refs_10_.1, f32[1,768]{1,0:T(1,128)} %broadcast_in_dim.33.gain_ref, bf16[768,768]{1,0:T(8,128)(2,1)} %refs_4_.2, ...), custom_call_target="tpu_custom_call" | custom-call | flops 3623878656 | bytes 9437184 | tf_op jit(solution)/shard_map/project_own/pallas_call | solution.py:91
  28.9 11.5 %all-gather.2.cloned.1.call-done.x_ref = bf16[2048,768]{1,0:T(8,128)(2,1)} async-done(((bf16[512,768]{1,0:T(8,128)(2,1)}), bf16[2048,768]{1,0:T(8,128)(2,1)}) %all-gather.2.cloned.1.call-update) | async-done | bytes 3145744 | tf_op jit(solution)/shard_map/all_gather | solution.py:1045
  40.4 4.6 %all-to-all-start = ((bf16[8,192,768]{2,1,0:T(8,128)(2,1)}), bf16[8,192,768]{2,1,0:T(8,128)(2,1)}, u32[]{:S(2)}, u32[]{:S(2)}) async-start(bf16[8,192,768]{2,1,0:T(8,128)(2,1)} %dispatch_grads.1), calls=%async_computation | async-start | bytes 4718592 | tf_op jit(solution)/shard_map/all_to_all | solution.py:1040
  46.5 0.8 pad.4.prev_ref
  48.2 11.7 %project_prompt.1 = (bf16[2048,768]{1,0:T(8,128)(2,1)}, bf16[2048,768]{1,0:T(8,128)(2,1)}, bf16[2048,768]{1,0:T(8,128)(2,1)}) custom-call(s32[1]{0:T(128)} %bitcast.1.e_ref, bf16[2048,768]{1,0:T(8,128)(2,1)} %all-gather.2.cloned.1.call-done.x_ref, f32[1,768]{1,0:T(1,128)} %broadcast_in_dim.33.gain_ref, bf16[768,768]{1,0:T(8,128)(2,1)} %refs_6_.1, ...), custom_call_target="tpu_custom_call" | custom-call | flops 4831838208 | bytes 18874368 | tf_op jit(solution)/shard_map/project_prompt/pallas_call | solution.py:91
  59.8 44.6 %attn_fwd.1 = (bf16[1024,768]{1,0:T(8,128)(2,1)}, f32[6,2,1024]{2,1,0:T(2,128)}) custom-call(s32[1]{0:T(128)} %bitcast.1.e_ref, bf16[1024,768]{1,0:T(8,128)(2,1)} %get-tuple-element.46.q_ref, bf16[1024,768]{1,0:T(8,128)(2,1)} %get-tuple-element.47.ko_ref, bf16[1024,768]{1,0:T(8,128)(2,1)} %get-tuple-element.48.vo_ref, ...), custom_call_target="tpu_custom_call" | custom-call | flops 12884901888 | bytes 12582912 | tf_op jit(solution)/shard_map/attn_fwd/pallas_call | solution.py:188
  104.4 7.4 %gates.1 = (f32[1024,768]{1,0:T(8,128)}, bf16[1024,768]{1,0:T(8,128)(2,1)}, f32[1024,128]{1,0:T(8,128)}, bf16[1024,256]{1,0:T(8,128)(2,1)}) custom-call(bf16[1024,768]{1,0:T(8,128)(2,1)} %refs_10_.1, bf16[1024,768]{1,0:T(8,128)(2,1)} %get-tuple-element.53.o_ref.refs_2_, bf16[768,768]{1,0:T(8,128)(2,1)} %w_ref.3, f32[1,768]{1,0:T(1,128)} %broadcast_in_dim.34.gain_ref, ...), custom_call_target="tpu_custom_call" | custom-call | flops 1207959552 | bytes 9437184 | tf_op jit(solution)/shard_map/gates/pallas_call | solution.py:386
  111.8 89.1 %experts_on_rows.1 = (bf16[1536,768]{1,0:T(8,128)(2,1)}, bf16[1536,896]{1,0:T(8,128)(2,1)}, bf16[3,768,2048]{2,1,0:T(8,128)(2,1)}) custom-call(s32[2,1024]{1,0:T(2,128)} %copy.132.slot_ref, bf16[1024,768]{1,0:T(8,128)(2,1)} %get-tuple-element.54.h2_ref, bf16[1024,256]{1,0:T(8,128)(2,1)} %get-tuple-element.55.ext_ref, bf16[1536,768]{1,0:T(8,128)(2,1)} %bitcast.3.g_ref, ...), custom_call_target="tpu_custom_call" | custom-call | flops 43486543872 | bytes 28311552 | tf_op jit(solution)/shard_map/experts_on_rows/pallas_call | solution.py:551
  201.9 1.5 fusion.13.slot_ref
  203.4 4.7 %all-to-all-start.1 = ((bf16[8,192,768]{2,1,0:T(8,128)(2,1)}), bf16[8,192,768]{2,1,0:T(8,128)(2,1)}, u32[]{:S(2)}, u32[]{:S(2)}) async-start(bf16[8,192,768]{2,1,0:T(8,128)(2,1)} %bitcast.37), calls=%async_computation.1 | async-start | bytes 4718592 | tf_op jit(solution)/shard_map/all_to_all | solution.py:1040
  208.1 21.2 %combine.1 = (f32[1024,12]{1,0:T(8,128)}, f32[1024,768]{1,0:T(8,128)}, bf16[1024,768]{1,0:T(8,128)(2,1)}, bf16[1024,768]{1,0:T(8,128)(2,1)}, f32[128,768]{1,0:T(8,128)}, /*index=5*/f32[8,768]{1,0:T(8,128)}) custom-call(bf16[1536,896]{1,0:T(8,128)(2,1)} %get-tuple-element.60.back_ref, s32[1024,2]{1,0:T(8,128)} %fusion.13.slot_ref, s32[1024,2]{1,0:T(8,128)} %copy-done, ...), custom_call_target="tpu_custom_call" | custom-call | flops 4831838208 | bytes 20447232 | tf_op jit(solution)/shard_map/combine/pallas_call | solution.py:653
  229.3 63.6 %attn_bwd.1 = (bf16[1024,768]{1,0:T(8,128)(2,1)}, bf16[2560,768]{1,0:T(8,128)(2,1)}, bf16[2560,768]{1,0:T(8,128)(2,1)}) custom-call(s32[1]{0:T(128)} %bitcast.1.e_ref, bf16[1024,768]{1,0:T(8,128)(2,1)} %get-tuple-element.46.q_ref, bf16[1024,768]{1,0:T(8,128)(2,1)} %get-tuple-element.64.do_ref, bf16[1024,768]{1,0:T(8,128)(2,1)} %get-tuple-element.53.o_ref.refs_2_, ...), custom_call_target="tpu_custom_call" | custom-call | flops 32212254720 | bytes 25165824 | tf_op jit(solution)/shard_map/attn_bwd/pallas_call | solution.py:319
  294.4 117.7 %finale.1 = (bf16[3072,768]{1,0:T(8,128)(2,1)}, f32[24,768]{1,0:T(8,128)}, f32[1024,768]{1,0:T(8,128)}) custom-call(f32[24,768]{1,0:T(8,128)} %maximum_maximum_fusion.1.small_ref, f32[1,768]{1,0:T(1,128)} %broadcast_in_dim.33.gain_ref, bf16[1024,768]{1,0:T(8,128)(2,1)} %get-tuple-element.63.refs_0_, bf16[1024,768]{1,0:T(8,128)(2,1)} %get-tuple-element.66.refs_1_, ...), custom_call_target="tpu_custom_call" | custom-call | flops 18119393280 | bytes 18874368 | tf_op jit(solution)/shard_map/finale/pallas_call | solution.py:989
  412.2 3.2 copy.150
  415.4 3.9 all-to-all-start.2
  421.2 0.8 copy.145
  422.7 6.2 %fusion.25 = (f32[768,768]{1,0:T(8,128)}, f32[768,768]{1,0:T(8,128)}, f32[768,768]{1,0:T(8,128)}, f32[768,768]{1,0:T(8,128)}) fusion(bf16[3072,768]{1,0:T(8,128)(2,1)} %get-tuple-element.75), kind=kLoop, calls=%fused_computation.53 | loop fusion | bytes 18874368 | tf_op jit(solution)/shard_map/slice | solution.py:1087
  428.9 9.3 %mix.1 = bf16[1024,768]{1,0:T(8,128)(2,1)} custom-call(bf16[1536,768]{1,0:T(8,128)(2,1)} %bitcast.5.made_ref, s32[1024,2]{1,0:T(8,128)} %fusion.13.slot_ref, s32[1024,2]{1,0:T(8,128)} %copy-done, f32[1024,128]{1,0:T(8,128)} %get-tuple-element.58.aux_ref, f32[1024,768]{1,0:T(8,128)} %get-tuple-element.59.x2_ref, bf16[1024,768]{1,0:T(8,128)(2,1)} %get-tuple-element.54.h2_ref, ...), custom_call_target="tpu_custom_call" | custom-call | flops 4831838208 | bytes 9437184 | tf_op jit(solution)/shard_map/mix/pallas_call | solution.py:684
  438.1 8.9 %all-to-all-done.2 = bf16[2,3,768,256]{3,2,1,0:T(8,128)(2,1)S(1)} async-done(((bf16[2,3,768,256]{3,2,1,0:T(8,128)(2,1)}), bf16[2,3,768,256]{3,2,1,0:T(8,128)(2,1)S(1)}, u32[]{:S(2)}, u32[]{:S(2)}) %all-to-all-start.2) | async-done | bytes 2359328 | tf_op jit(solution)/shard_map/all_to_all | solution.py:1077
  447.4 2.2 slice_bitcast_fusion
  449.6 1.6 copy.146
  451.2 3.8 copy.152
  (62 shorter events, 11.2 us)
Async XLA Ops:
  7.2 2.2 copy-start.9
  7.2 2.8 copy-start.5
  7.2 3.2 copy-start.11
  7.2 33.2 %all-gather.2.cloned.1.call-start = ((), (), s32[]{:S(2)}) async-start(), calls=%async_computation.4 | async-start | bytes 3932160 | tf_op jit(solution)/shard_map/all_gather | solution.py:1045
  10.2 9.5 %copy-start = (s32[1024,2]{1,0:T(8,128)}, s32[1024,2]{1,0:T(8,128)S(1)}, u32[]{:S(2)}) copy-start(s32[1024,2]{1,0:T(8,128)S(1)} %copy.124.routes_ref) | copy-start | bytes 24580
  40.4 4.8 %copy-start.10 = (f32[768]{0:T(1024)S(1)}, f32[768]{0:T(1024)}, u32[]{:S(2)}) copy-start(f32[768]{0:T(1024)} %param.28) | copy-start | bytes 9220
  40.4 5.4 %copy-start.8 = (bf16[2,768,2]{1,2,0:T(2,128)(2,1)S(1)}, bf16[2,768,2]{1,2,0:T(2,128)(2,1)}, u32[]{:S(2)}) copy-start(bf16[2,768,2]{1,2,0:T(2,128)(2,1)} %param.30) | copy-start | bytes 18436
  40.4 5.6 %copy-start.6 = (bf16[768,12]{0,1:T(8,128)(2,1)S(1)}, bf16[768,12]{0,1:T(8,128)(2,1)}, u32[]{:S(2)}) copy-start(bf16[768,12]{0,1:T(8,128)(2,1)} %param.29) | copy-start | bytes 55300
  40.4 5.8 %copy-start.4 = (f32[1024,12]{0,1:T(8,128)S(1)}, f32[1024,12]{0,1:T(8,128)}, u32[]{:S(2)}) copy-start(f32[1024,12]{0,1:T(8,128)} %param.20) | copy-start | bytes 147460
  40.4 71.4 %all-to-all-start = ((bf16[8,192,768]{2,1,0:T(8,128)(2,1)}), bf16[8,192,768]{2,1,0:T(8,128)(2,1)}, u32[]{:S(2)}, u32[]{:S(2)}) async-start(bf16[8,192,768]{2,1,0:T(8,128)(2,1)} %dispatch_grads.1), calls=%async_computation | async-start | bytes 4718592 | tf_op jit(solution)/shard_map/all_to_all | solution.py:1040
  45.0 367.1 %reduce-scatter.2.cloned.1.call-start = ((), (), s32[]{:S(2)}) async-start(), calls=%async_computation.5 | async-start | bytes 11796480 | tf_op jit(solution)/shard_map/reduce_scatter | solution.py:1061
  200.9 1.0 copy-start.1
  203.4 212.0 %all-to-all-start.1 = ((bf16[8,192,768]{2,1,0:T(8,128)(2,1)}), bf16[8,192,768]{2,1,0:T(8,128)(2,1)}, u32[]{:S(2)}, u32[]{:S(2)}) async-start(bf16[8,192,768]{2,1,0:T(8,128)(2,1)} %bitcast.37), calls=%async_computation.1 | async-start | bytes 4718592 | tf_op jit(solution)/shard_map/all_to_all | solution.py:1040
  229.2 64.5 %copy-start.7 = (f32[8,768]{1,0:T(8,128)S(1)}, f32[8,768]{1,0:T(8,128)}, u32[]{:S(2)}) copy-start(f32[8,768]{1,0:T(8,128)} %get-tuple-element.62) | copy-start | bytes 73732
  415.4 4.0 copy-start.3
  415.4 5.8 %copy-start.2 = (f32[1024,12]{1,0:T(8,128)S(1)}, f32[1024,12]{1,0:T(8,128)}, u32[]{:S(2)}) copy-start(f32[1024,12]{1,0:T(8,128)} %get-tuple-element.139) | copy-start | bytes 147460
  415.4 31.6 %all-to-all-start.2 = ((bf16[2,3,768,256]{3,2,1,0:T(8,128)(2,1)}), bf16[2,3,768,256]{3,2,1,0:T(8,128)(2,1)S(1)}, u32[]{:S(2)}, u32[]{:S(2)}) async-start(bf16[2,3,768,256]{3,2,1,0:T(8,128)(2,1)} %bitcast.36), calls=%async_computation.3 | async-start | bytes 4718592 | tf_op jit(solution)/shard_map/all_to_all | solution.py:1077
Sparse Core Ops, SparseCore 0:
  10.2 30.1 all-gather.1
  201.0 190.9 reduce-scatter.1

commit v6 on v5

--- a/solution.py
+++ b/solution.py
@@ -40,17 +40,19 @@
 
 
 def angle_tables():
-    positions = np.arange(PROMPT + CONT, dtype=np.float32)
-    frequency = np.exp(
-        np.float32(-np.log(10000.0)) * np.arange(32, dtype=np.float32) * np.float32(2.0) / np.float32(64)
-    ).astype(np.float32)
-    angle = (positions[:, None] * frequency[None, :]).astype(np.float64)
-    cosine = np.cos(angle).astype(np.float32)
-    sine = np.sin(angle).astype(np.float32)
-    return (
-        np.concatenate([cosine] * 4, axis=1),
-        np.concatenate([-sine, sine, -sine, sine], axis=1),
+    fine = 64
+    frequency = np.exp(-np.log(10000.0) * np.arange(32) * 2.0 / 64)
+    frequency = np.tile(frequency.astype(np.float32).astype(np.float64), 4)
+    near = np.arange(fine)[:, None] * frequency
+    far = (np.arange((PROMPT + CONT) // fine) * fine)[:, None] * frequency
+    near_cos, near_sin, far_cos, far_sin = (
+        jnp.asarray(table.astype(np.float32)) for table in (np.cos(near), np.sin(near), np.cos(far), np.sin(far))
     )
+    near_cos, near_sin, far_cos, far_sin = near_cos[None], near_sin[None], far_cos[:, None], far_sin[:, None]
+    sign = jnp.where(jnp.arange(128) % 64 < 32, -1.0, 1.0)
+    cosine = far_cos * near_cos - far_sin * near_sin
+    sine = (far_sin * near_cos + far_cos * near_sin) * sign
+    return cosine.reshape(-1, 128), sine.reshape(-1, 128)
 
 
 def lane_iota(width=128):
@@ -452,7 +454,7 @@
         return copy
 
     rows = {}
-    for r in (4, 5, 6, 7, 2, 3, 1, 0):
+    for r in (4, 5, 2, 3, 6, 7, 1, 0):
         ids = place(r) * capacity + lax.broadcasted_iota(jnp.int32, (capacity, 1), 0)
         hot = [jnp.where(ids == slot_ref[k:k + 1, :], 1.0, 0.0).astype(BF) for k in range(2)]
         into = s_ref if r else a_ref
@@ -466,7 +468,7 @@
     returned = []
     mine = pl.ds(pl.multiple_of(place(0) * capacity, 16), capacity)
     two = 2 * capacity
-    for n, first in enumerate((0, 4, 6, 2)):
+    for n, first in enumerate((0, 4, 2, 6)):
         for r in (first, first + 1):
             if r:
                 rows[r].wait_recv()
@@ -666,34 +668,6 @@
     )(back, slots, routes, aux, x2, h2, g, gain, wcat, const_v, w_out)
 
 
-def mix_kernel(made_ref, slot_ref, routes_ref, aux_ref, x2_ref, h2_ref, v_ref, out_ref, *, experts):
-    route = [routes_ref[:, k:k + 1] for k in range(2)]
-    gate, alpha, _, const, on_h2 = pick_parts(aux_ref[...], route, experts)
-    out = x2_ref[...] + (gate[0] * on_h2[0] + gate[1] * on_h2[1]) * h2_ref[...].astype(F32)
-    for c in range(2):
-        out = out + ((gate[0] * const[0][c] + gate[1] * const[1][c]) * alpha[c][1]) * v_ref[c:c + 1, :]
-    for k in range(2):
-        out = out + gate[k] * dot(one_hot(slot_ref[:, k:k + 1], made_ref.shape[0]), made_ref[...])
-    out_ref[...] = out.astype(BF)
-
-
-def mix(made, slots, routes, aux, x2, h2, const_v, experts, tile=256):
-    rows, width = x2.shape
-    block = pl.BlockSpec((tile, width), lambda i: (i, 0))
-    two = pl.BlockSpec((tile, 2), lambda i: (i, 0))
-    return pl.pallas_call(
-        functools.partial(mix_kernel, experts=experts),
-        grid=(rows // tile,),
-        in_specs=[whole(made.shape), two, two, pl.BlockSpec((tile, 128), lambda i: (i, 0)), block, block, whole(const_v.shape)],
-        out_specs=block,
-        out_shape=jax.ShapeDtypeStruct((rows, width), BF),
-        compiler_params=params(),
-        cost_estimate=pl.CostEstimate(flops=4 * rows * width * made.shape[0], bytes_accessed=12 * rows * width,
-                                      transcendentals=0),
-        name="mix",
-    )(made, slots, routes, aux, x2, h2, const_v)
-
-
 def padded_rows(rows, rest):
     unit = 8 * rest * 16
     return -(-rows // unit) * unit
@@ -701,11 +675,11 @@
 
 def finale_kernel(small_ref, gain_ref, *refs, rest, chunks, norm_row, tile):
     hbm, refs = refs[:12], refs[12:]
-    out_ref, small_out_ref, token_hbm = refs[:3]
-    local, refs = refs[3:15], refs[15:]
+    shard_refs, (small_out_ref, token_hbm) = refs[:2], refs[2:4]
+    local, refs = refs[4:16], refs[16:]
     (turned_ref, g_ref, norm_ref, dh_ref, r0_ref, sm_ref, rs_ref, rd0_ref, td_ref, rd1_ref, tok_ref,
      load_sem, tok_sem, send_sem, recv_sem) = refs[:15]
-    r1_ref, r2_ref, r3_ref = (refs[15 + 2 * n:17 + 2 * n] for n in range(3))
+    r1_ref, r2_ref = (refs[15 + 2 * n:17 + 2 * n] for n in range(2))
     ho_ref, dq_ref, o_ref, da_ref, wq_ref, dk_ref, wk_ref, dv_ref, wv_ref, hp_ref, x_ref, dx2_ref = local[:12]
 
     loads = [pltpu.make_async_copy(src, dst, load_sem.at[n]) for n, (src, dst) in enumerate(zip(hbm, local))]
@@ -738,8 +712,8 @@
     prompt = hp_ref.shape[0]
     half = rows // 2
     size = half // chunks
-    q1, q2, q3 = size // 2, size // 4, size // 4 // rest
-    cut = width // 3
+    q1, q2 = size // 2, size // 4
+    cut = width // 2
     part = [pl.ds(0, cut), pl.ds(cut, width - cut)]
     first, second = [across, beside], [beside, across]
     bit1, bit2 = [x, y], [y, x]
@@ -749,9 +723,6 @@
 
     def at1(k, p, bit):
         return k * size + bit * q1
-
-    def spot2(k, p, bit):
-        return k * size + bit1[p] * q1 + bit * q2
 
     def stage0(k):
         return [send(g_ref.at[ds((1 - c) * half + k * size, size)], r0_ref.at[ds(k * size, size)], mate)]
@@ -771,46 +742,12 @@
         return out
 
     def stage3(k):
-        out = []
         for p in range(2):
             sl = pl.ds(k * q2, q2)
-            r2_ref[p][sl] = (r1_ref[p][ds(k * q1 + bit2[p] * q2, q2)].astype(F32) + r2_ref[p][sl].astype(F32)).astype(BF)
-            for d in range(1, rest):
-                to = (z + d) % rest
-                out.append(send(r2_ref[p].at[ds(k * q2 + to * q3, q3)], r3_ref[p].at[d - 1, pl.ds(k * q3, q3)], ahead[d - 1]))
-        return out
-
-    def stage4(k):
-        out = []
-        for p in range(2):
-            total = r2_ref[p][ds(k * q2 + z * q3, q3)].astype(F32)
-            for d in range(1, rest):
-                total = total + r3_ref[p][d - 1, pl.ds(k * q3, q3)].astype(F32)
-            mine = ds(c * half + spot2(k, p, bit2[p]) + z * q3, q3)
-            out_ref[mine, part[p]] = total.astype(BF)
-            for d in range(1, rest):
-                out.append(send(out_ref.at[mine, part[p]], out_ref.at[mine, part[p]], ahead[d - 1]))
-        return out
-
-    def stage5(k):
-        out = []
-        for p in range(2):
-            mine = ds(c * half + spot2(k, p, bit2[p]), q2)
-            out.append(send(out_ref.at[mine, part[p]], out_ref.at[mine, part[p]], second[p]))
-        return out
-
-    def stage6(k):
-        out = []
-        for p in range(2):
-            mine = ds(c * half + at1(k, p, bit1[p]), q1)
-            out.append(send(out_ref.at[mine, part[p]], out_ref.at[mine, part[p]], first[p]))
-        return out
-
-    def stage7(k):
-        mine = ds(c * half + k * size, size)
-        return [send(out_ref.at[mine], out_ref.at[mine], mate)]
-
-    stages = (stage0, stage1, stage2, stage3, stage4, stage5, stage6, stage7)
+            shard_refs[p][sl] = (r1_ref[p][ds(k * q1 + bit2[p] * q2, q2)].astype(F32) + r2_ref[p][sl].astype(F32)).astype(BF)
+        return []
+
+    stages = (stage0, stage1, stage2, stage3)
     waiting = {}
 
     def wait(line):
@@ -891,7 +828,7 @@
             tokens[-2].wait()
         put_tokens(i, dh, tokens)
 
-    hops = (4.5, 6.0, 5.0, 6.5, 6.5, 5.0, 6.0, 4.5)
+    hops = (4.5, 6.0, 5.0)
     due = []
 
     def begin(now, k):
@@ -908,7 +845,7 @@
                     last = 4
                 else:
                     step(k, s)
-                    last = len(stages)
+                    last = len(stages) - 1
                 if s < last:
                     due.append([max(now, entry[0]) + (hops[s] if k != "small" else 5.0), k, s + 1])
 
@@ -967,9 +904,8 @@
     while due or late:
         now = max(now, min(entry[0] for entry in due)) if due else now
         ready(now)
-        if late and (now > 52.0 or not due):
+        if late and not due:
             prompt_tokens(late.pop(0))
-            now += 2.0
     for copy in tokens[-2:]:
         copy.wait()
     for copy in started:
@@ -982,27 +918,162 @@
     block = own // 2
     half = out_rows // 2
     chunks = 6 if half == 6 * 4 * rest * 16 else 1
-    lanes = (width // 3, width - width // 3)
-    copies = chunks * (1 + 2 + 2 + 2 * (rest - 1) * 2 + 2 + 2 + 1) + 3 + 3 + rest - 1
+    lanes = (width // 2, width // 2)
+    copies = chunks * (1 + 2 + 2) + 3 + 3 + rest - 1
     vm, dma = pltpu.VMEM, pltpu.SemaphoreType.DMA
     vmem, hbm = pl.BlockSpec(memory_space=pltpu.VMEM), pl.BlockSpec(memory_space=pl.ANY)
     return pl.pallas_call(
         functools.partial(finale_kernel, rest=rest, chunks=chunks, norm_row=norm_row, tile=tile),
         in_specs=[vmem] * 2 + [hbm] * len(arrays),
-        out_specs=[vmem, vmem, hbm],
-        out_shape=[jax.ShapeDtypeStruct((out_rows, width), BF), jax.ShapeDtypeStruct(small.shape, F32),
-                   jax.ShapeDtypeStruct((own, width), F32)],
+        out_specs=[vmem, vmem, vmem, hbm],
+        out_shape=[jax.ShapeDtypeStruct((half // 4, k), BF) for k in lanes]
+        + [jax.ShapeDtypeStruct(small.shape, F32), jax.ShapeDtypeStruct((own, width), F32)],
         scratch_shapes=[vm(a.shape, a.dtype) for a in arrays] + [
             vm((width, prompt + block), BF), vm((out_rows, width), BF), vm((width, 128), F32), vm((prompt, width), BF),
             vm((half, width), BF), vm((4,) + small.shape, F32), vm((2 + rest,) + small.shape, F32),
             vm((2, block, width), BF), vm((block, width), BF), vm((block, width), BF), vm((2, tile, width), F32),
             dma((len(arrays),)), dma((2,)), dma((copies,)), dma((copies,)),
-        ] + [vm((half // n, k), BF) for n in (2, 4) for k in lanes]
-        + [vm((rest - 1, half // 4 // rest, k), BF) for k in lanes],
+        ] + [vm((half // n, k), BF) for n in (2, 4) for k in lanes],
         compiler_params=pltpu.CompilerParams(vmem_limit_bytes=62 << 20, collective_id=0, has_side_effects=True),
         cost_estimate=pl.CostEstimate(flops=30 * own * width * width, bytes_accessed=8 * out_rows * width, transcendentals=0),
         name="finale",
     )(small, gain, *arrays)
+
+
+def spread_kernel(shard0_ref, shard1_ref, v_ref, *refs, rest, chunks, experts, tile):
+    shards = (shard0_ref, shard1_ref)
+    hbm, (out_ref, mixed_ref), refs = refs[:6], refs[6:8], refs[8:]
+    local, (r3a_ref, r3b_ref, load_sem, send_sem, recv_sem) = refs[:6], refs[6:]
+    r3_ref = (r3a_ref, r3b_ref)
+    made_ref, slot_ref, routes_ref, aux_ref, x2_ref, h2_ref = local
+    loads = [pltpu.make_async_copy(src, dst, load_sem.at[n]) for n, (src, dst) in enumerate(zip(hbm, local))]
+    for copy in loads:
+        copy.start()
+    dp, ex = lax.axis_index("dp"), lax.axis_index("expert")
+    c, x, y, z = ex % 2, ex // 2, dp % 2, dp // 2
+    mate = (dp, x * 2 + 1 - c)
+    across = (dp, (1 - x) * 2 + c)
+    beside = (z * 2 + 1 - y, ex)
+    ahead = [((z + d) % rest * 2 + y, ex) for d in range(1, rest)]
+    barrier = pltpu.get_barrier_semaphore()
+    for peer in [mate, across, beside] + ahead:
+        pl.semaphore_signal(barrier, inc=1, device_id=peer, device_id_type=MESH)
+    pl.semaphore_wait(barrier, 2 + rest)
+
+    started = []
+    rows, width = out_ref.shape
+    half = rows // 2
+    size = half // chunks
+    q1, q2, q3 = size // 2, size // 4, size // 4 // rest
+    cut = width // 2
+    part = [pl.ds(0, cut), pl.ds(cut, width - cut)]
+    first, second = [across, beside], [beside, across]
+    bit1, bit2 = [x, y], [y, x]
+
+    def copy_to(src, dst, peer):
+        n = len(started)
+        copy = pltpu.make_async_remote_copy(src_ref=src, dst_ref=dst, send_sem=send_sem.at[n], recv_sem=recv_sem.at[n],
+                                            device_id=peer, device_id_type=MESH)
+        copy.start()
+        started.append(copy)
+        return copy
+
+    def send(at, count, lanes, peer):
+        spot = out_ref.at[pl.ds(pl.multiple_of(at, 16), count), lanes]
+        return copy_to(spot, spot, peer)
+
+    def base(k, p, depth):
+        at = c * half + k * size
+        if depth > 0:
+            at = at + bit1[p] * q1
+        if depth > 1:
+            at = at + bit2[p] * q2
+        if depth > 2:
+            at = at + z * q3
+        return at
+
+    def stage0(k):
+        out = []
+        for p in range(2):
+            at = base(k, p, 3)
+            total = shards[p][pl.ds(pl.multiple_of(k * q2 + z * q3, 16), q3)].astype(F32)
+            for d in range(1, rest):
+                total = total + r3_ref[p][d - 1, pl.ds(k * q3, q3)].astype(F32)
+            out_ref[pl.ds(pl.multiple_of(at, 16), q3), part[p]] = total.astype(BF)
+            out += [send(at, q3, part[p], peer) for peer in ahead]
+        return out
+
+    def reduce(k):
+        out = []
+        for p in range(2):
+            for d in range(1, rest):
+                to = pl.ds(pl.multiple_of(k * q2 + (z + d) % rest * q3, 16), q3)
+                out.append(copy_to(shards[p].at[to], r3_ref[p].at[d - 1, pl.ds(k * q3, q3)], ahead[d - 1]))
+        return out
+
+    def stage1(k):
+        return [send(base(k, p, 2), q2, part[p], second[p]) for p in range(2)]
+
+    def stage2(k):
+        return [send(base(k, p, 1), q1, part[p], first[p]) for p in range(2)]
+
+    def stage3(k):
+        return [send(base(k, 0, 0), size, pl.ds(0, width), mate)]
+
+    def end(k):
+        return []
+
+    stages = (reduce, stage0, stage1, stage2, stage3, end)
+    waiting = {k: [] for k in range(chunks)}
+
+    def mixing(i):
+        at = pl.ds(i * tile, tile)
+        if i == 0:
+            for copy in loads:
+                copy.wait()
+        route = [routes_ref[at, k:k + 1] for k in range(2)]
+        gate, alpha, _, const, on_h2 = pick_parts(aux_ref[at], route, experts)
+        out = x2_ref[at] + (gate[0] * on_h2[0] + gate[1] * on_h2[1]) * h2_ref[at].astype(F32)
+        for n in range(2):
+            out = out + ((gate[0] * const[0][n] + gate[1] * const[1][n]) * alpha[n][1]) * v_ref[n:n + 1, :]
+        for k in range(2):
+            out = out + gate[k] * dot(one_hot(slot_ref[at, k:k + 1], made_ref.shape[0]), made_ref[...])
+        mixed_ref[at] = out.astype(BF)
+
+    blocks = list(range(x2_ref.shape[0] // tile))
+    for t in range(len(stages) + (chunks + 1) // 2 - 1):
+        for k in range(chunks):
+            s = t - k // 2
+            if 0 <= s < len(stages):
+                for copy in waiting[k]:
+                    copy.wait_recv()
+                waiting[k] = stages[s](k)
+        if blocks:
+            mixing(blocks.pop(0))
+    for i in blocks:
+        mixing(i)
+    for copy in started:
+        copy.wait_send()
+
+
+def spread_sums(shards, const_v, arrays, rest, out_rows, experts, tile=256):
+    rows, width = arrays[4].shape
+    half = out_rows // 2
+    chunks = 6 if half == 6 * 4 * rest * 16 else 1
+    copies = chunks * (4 * (rest - 1) + 2 + 2 + 1)
+    vm, dma = pltpu.VMEM, pltpu.SemaphoreType.DMA
+    vmem, hbm = pl.BlockSpec(memory_space=pltpu.VMEM), pl.BlockSpec(memory_space=pl.ANY)
+    return pl.pallas_call(
+        functools.partial(spread_kernel, rest=rest, chunks=chunks, experts=experts, tile=tile),
+        in_specs=[vmem] * 3 + [hbm] * len(arrays),
+        out_specs=[vmem, vmem],
+        out_shape=[jax.ShapeDtypeStruct((out_rows, width), BF), jax.ShapeDtypeStruct((rows, width), BF)],
+        scratch_shapes=[vm(a.shape, a.dtype) for a in arrays] + [vm((rest - 1, half // 4 // rest, width // 2), BF)] * 2
+        + [dma((len(arrays),)), dma((copies,)), dma((copies,))],
+        compiler_params=params(collective_id=2, has_side_effects=True),
+        cost_estimate=pl.CostEstimate(flops=4 * rows * width * 1536, bytes_accessed=8 * out_rows * width, transcendentals=0),
+        name="spread_sums",
+    )(*shards, const_v, *arrays)
 
 
 def slot_table(routes_t, priority, groups, capacity):
@@ -1039,7 +1110,7 @@
     def swap(x):
         return lax.all_to_all(x, everyone, split_axis=0, concat_axis=0, axis_index_groups=exchange, tiled=True)
 
-    cos, sin = (jnp.asarray(t) for t in angle_tables())
+    cos, sin = angle_tables()
     gain1, gain2 = norm_attn[None, :], norm_ffn[None, :]
 
     prompt_x = lax.all_gather(tokens[:prompt_dev], "expert", axis=0, tiled=True)
@@ -1067,14 +1138,15 @@
     rest = dp // 2
     n = experts
     small = jnp.concatenate([cat[:n + 4], sums[:3], jnp.zeros((5, width), F32)], axis=0)
-    grad_w, small, grad_tokens = finale(
-        small, gain1, (h_own, dq, o, da, w_query, dk, w_key, dv, w_value, h_prompt, tokens, dx2), rest, n + 7,
-        padded_rows(4 * width, rest),
+    out_rows = padded_rows(4 * width, rest)
+    *shards, small, grad_tokens = finale(
+        small, gain1, (h_own, dq, o, da, w_query, dk, w_key, dv, w_value, h_prompt, tokens, dx2), rest, n + 7, out_rows
     )
+    ffn_sum = ffn_sum.reshape(3, width, pair, -1).transpose(2, 0, 1, 3)
+    ffn_sum, small, shards = lax.optimization_barrier((ffn_sum, small, shards))
+    ffn_sum = lax.all_to_all(ffn_sum, "dp", split_axis=0, concat_axis=0, axis_index_groups=pairs, tiled=True)
+    grad_w, mixed = spread_sums(shards, const_v, (made, slots, routes, aux, x2, h2), rest, out_rows, experts)
     grad_w = grad_w.astype(F32)
-    mixed = mix(made, slots, routes, aux, x2, h2, const_v, experts)
-    ffn_sum = ffn_sum.reshape(3, width, pair, -1).transpose(2, 0, 1, 3)
-    ffn_sum = lax.all_to_all(ffn_sum, "dp", split_axis=0, concat_axis=0, axis_index_groups=pairs, tiled=True)
     ffn_sum = ffn_sum.astype(F32)
     return (
         mixed,

time: 468 us -> 461 us (0.985)
  waiting for transfers between devices: 20.5 us -> 9.45 us
    pallas_call x1, Pallas kernels: 9.26 us -> 55.1 us  [spread_sums(): pl.pallas_call(functools.partial(spread_kernel, rest=rest, chunks=chunks,...]
    pallas_call x1, Pallas kernels: 118 us -> 77.3 us  [finale(): pl.pallas_call(functools.partial(finale_kernel, rest=rest, chunks=chunks,...]
    all_to_all x1, waiting for transfers between devices: 8.89 us -> 0.01 us  [local(): lax.all_to_all(ffn_sum, 'dp', split_axis=0, concat_axis=0, axis_index_gro...]
  transfers between devices with their start and end apart: 5 -> 5, of which waited for: 2 -> 1; matrix products, arithmetic and copies ran while one was open for 5% -> 6% of each run, Pallas kernels for 63% -> 65%
where the time goes in v6:
time: 461 us; the launch traced here: 457 us
  Pallas kernels  383 us (83%)
  local copies, waits for them, and re-layouts  28.6 us (6%)
  between operations  14.8 us (3%)
  starting transfers between devices  13.5 us (3%)
  waiting for transfers between devices  9.45 us (2%)
  other arithmetic  6.54 us (1%)
    pallas_call x1, Pallas kernels, experts_on_rows(): pl.pallas_call(functools.partial(expert_kernel, capacity=capacity, tile=t...  87.3 us
    pallas_call x1, Pallas kernels, finale(): pl.pallas_call(functools.partial(finale_kernel, rest=rest, chunks=chunks,...  77.3 us
    pallas_call x1, Pallas kernels, attn_bwd(): pl.pallas_call(functools.partial(attn_bwd_kernel, tile=tile, scale=0.125)...  63.6 us
    pallas_call x1, Pallas kernels, spread_sums(): pl.pallas_call(functools.partial(spread_kernel, rest=rest, chunks=chunks,...  55.1 us
    pallas_call x1, Pallas kernels, attn_fwd(): pl.pallas_call(functools.partial(attn_fwd_kernel, chunk=chunk, tile=tile,...  44.6 us
    pallas_call x1, Pallas kernels, combine(): pl.pallas_call(functools.partial(combine_kernel, experts=experts), grid=(...  20.6 us
    pallas_call x2, Pallas kernels, project(): pl.pallas_call(functools.partial(project_kernel, count=len(weights)), gri...  20.4 us
    all_gather x1, waiting for transfers between devices, local(): prompt_x = lax.all_gather(tokens[:prompt_dev], 'expert', axis=0, tiled=True)  9.41 us
  transfers between devices with their start and end apart: 5, of which 1 were waited for; matrix products, arithmetic and copies ran while one was open for 6% of the time, Pallas kernels for 65%

profile of v6, /device:TPU:9, one launch (start us, length us, event | category | flops | bytes accessed | tf_op | source)
XLA Modules:
  0.0 456.7 jit_solution(8355815399824264946)
XLA Ops:
  7.2 2.1 slice.45
  12.9 6.8 %dispatch_grads.1 = bf16[8,192,768]{2,1,0:T(8,128)(2,1)} custom-call(s32[2,1024]{1,0:T(2,128)} %copy.134.slot_ref, bf16[1024,768]{1,0:T(8,128)(2,1)} %g_ref.1), custom_call_target="tpu_custom_call" | custom-call | flops 2415919104 | bytes 3145728 | tf_op jit(solution)/shard_map/dispatch_grads/pallas_call | solution.py:410
  19.7 1.4 multiply_add_fusion
  22.2 8.7 %project_own.1 = (bf16[1024,768]{1,0:T(8,128)(2,1)}, bf16[1024,768]{1,0:T(8,128)(2,1)}, bf16[1024,768]{1,0:T(8,128)(2,1)}, bf16[1024,768]{1,0:T(8,128)(2,1)}) custom-call(s32[1]{0:T(128)} %bitcast.1.e_ref, bf16[1024,768]{1,0:T(8,128)(2,1)} %refs_10_.1, f32[1,768]{1,0:T(1,128)} %broadcast_in_dim.46.gain_ref, bf16[768,768]{1,0:T(8,128)(2,1)} %refs_4_.1, ...), custom_call_target="tpu_custom_call" | custom-call | flops 3623878656 | bytes 9437184 | tf_op jit(solution)/shard_map/project_own/pallas_call | solution.py:93
  30.9 9.4 %all-gather.2.cloned.1.call-done.x_ref = bf16[2048,768]{1,0:T(8,128)(2,1)} async-done(((bf16[512,768]{1,0:T(8,128)(2,1)}), bf16[2048,768]{1,0:T(8,128)(2,1)}) %all-gather.2.cloned.1.call-update) | async-done | bytes 3145744 | tf_op jit(solution)/shard_map/all_gather | solution.py:1116
  40.3 4.7 %all-to-all-start = ((bf16[8,192,768]{2,1,0:T(8,128)(2,1)}), bf16[8,192,768]{2,1,0:T(8,128)(2,1)}, u32[]{:S(2)}, u32[]{:S(2)}) async-start(bf16[8,192,768]{2,1,0:T(8,128)(2,1)} %dispatch_grads.1), calls=%async_computation | async-start | bytes 4718592 | tf_op jit(solution)/shard_map/all_to_all | solution.py:1111
  48.1 11.7 %project_prompt.1 = (bf16[2048,768]{1,0:T(8,128)(2,1)}, bf16[2048,768]{1,0:T(8,128)(2,1)}, bf16[2048,768]{1,0:T(8,128)(2,1)}) custom-call(s32[1]{0:T(128)} %bitcast.1.e_ref, bf16[2048,768]{1,0:T(8,128)(2,1)} %all-gather.2.cloned.1.call-done.x_ref, f32[1,768]{1,0:T(1,128)} %broadcast_in_dim.46.gain_ref, bf16[768,768]{1,0:T(8,128)(2,1)} %refs_6_.1, ...), custom_call_target="tpu_custom_call" | custom-call | flops 4831838208 | bytes 18874368 | tf_op jit(solution)/shard_map/project_prompt/pallas_call | solution.py:93
  59.8 44.6 %attn_fwd.1 = (bf16[1024,768]{1,0:T(8,128)(2,1)}, f32[6,2,1024]{2,1,0:T(2,128)}) custom-call(s32[1]{0:T(128)} %bitcast.1.e_ref, bf16[1024,768]{1,0:T(8,128)(2,1)} %get-tuple-element.53.q_ref, bf16[1024,768]{1,0:T(8,128)(2,1)} %get-tuple-element.54.ko_ref, bf16[1024,768]{1,0:T(8,128)(2,1)} %get-tuple-element.55.vo_ref, ...), custom_call_target="tpu_custom_call" | custom-call | flops 12884901888 | bytes 12582912 | tf_op jit(solution)/shard_map/attn_fwd/pallas_call | solution.py:190
  104.4 7.4 %gates.1 = (f32[1024,768]{1,0:T(8,128)}, bf16[1024,768]{1,0:T(8,128)(2,1)}, f32[1024,128]{1,0:T(8,128)}, bf16[1024,256]{1,0:T(8,128)(2,1)}) custom-call(bf16[1024,768]{1,0:T(8,128)(2,1)} %refs_10_.1, bf16[1024,768]{1,0:T(8,128)(2,1)} %get-tuple-element.60.o_ref.refs_2_, bf16[768,768]{1,0:T(8,128)(2,1)} %w_ref.3, f32[1,768]{1,0:T(1,128)} %broadcast_in_dim.49.gain_ref, ...), custom_call_target="tpu_custom_call" | custom-call | flops 1207959552 | bytes 9437184 | tf_op jit(solution)/shard_map/gates/pallas_call | solution.py:388
  111.8 87.3 %experts_on_rows.1 = (bf16[1536,768]{1,0:T(8,128)(2,1)}, bf16[1536,896]{1,0:T(8,128)(2,1)}, bf16[3,768,2048]{2,1,0:T(8,128)(2,1)}) custom-call(s32[2,1024]{1,0:T(2,128)} %copy.134.slot_ref, bf16[1024,768]{1,0:T(8,128)(2,1)} %get-tuple-element.61.h2_ref.refs_5_, bf16[1024,256]{1,0:T(8,128)(2,1)} %get-tuple-element.62.ext_ref, ...), custom_call_target="tpu_custom_call" | custom-call | flops 43486543872 | bytes 28311552 | tf_op jit(solution)/shard_map/experts_on_rows/pallas_call | solution.py:553
  200.2 1.5 fusion.13.slot_ref.refs_1_
  201.7 4.7 %all-to-all-start.1 = ((bf16[8,192,768]{2,1,0:T(8,128)(2,1)}), bf16[8,192,768]{2,1,0:T(8,128)(2,1)}, u32[]{:S(2)}, u32[]{:S(2)}) async-start(bf16[8,192,768]{2,1,0:T(8,128)(2,1)} %bitcast.40), calls=%async_computation.2 | async-start | bytes 4718592 | tf_op jit(solution)/shard_map/all_to_all | solution.py:1111
  206.4 20.6 %combine.1 = (f32[1024,12]{1,0:T(8,128)}, f32[1024,768]{1,0:T(8,128)}, bf16[1024,768]{1,0:T(8,128)(2,1)}, bf16[1024,768]{1,0:T(8,128)(2,1)}, f32[128,768]{1,0:T(8,128)}, /*index=5*/f32[8,768]{1,0:T(8,128)}) custom-call(bf16[1536,896]{1,0:T(8,128)(2,1)} %get-tuple-element.65.back_ref, s32[1024,2]{1,0:T(8,128)} %fusion.13.slot_ref.refs_1_, s32[1024,2]{1,0:T(8,128)} %copy-done, ...), custom_call_target="tpu_custom_call" | custom-call | flops 4831838208 | bytes 20447232 | tf_op jit(solution)/shard_map/combine/pallas_call | solution.py:655
  227.0 63.6 %attn_bwd.1 = (bf16[1024,768]{1,0:T(8,128)(2,1)}, bf16[2560,768]{1,0:T(8,128)(2,1)}, bf16[2560,768]{1,0:T(8,128)(2,1)}) custom-call(s32[1]{0:T(128)} %bitcast.1.e_ref, bf16[1024,768]{1,0:T(8,128)(2,1)} %get-tuple-element.53.q_ref, bf16[1024,768]{1,0:T(8,128)(2,1)} %get-tuple-element.71.do_ref, bf16[1024,768]{1,0:T(8,128)(2,1)} %get-tuple-element.60.o_ref.refs_2_, ...), custom_call_target="tpu_custom_call" | custom-call | flops 32212254720 | bytes 25165824 | tf_op jit(solution)/shard_map/attn_bwd/pallas_call | solution.py:321
  292.2 77.3 %finale.1 = (bf16[384,384]{1,0:T(8,128)(2,1)}, bf16[384,384]{1,0:T(8,128)(2,1)}, f32[24,768]{1,0:T(8,128)}, f32[1024,768]{1,0:T(8,128)}) custom-call(f32[24,768]{1,0:T(8,128)} %maximum_maximum_fusion.1.small_ref, f32[1,768]{1,0:T(1,128)} %broadcast_in_dim.46.gain_ref, bf16[1024,768]{1,0:T(8,128)(2,1)} %get-tuple-element.70.refs_0_, ...), custom_call_target="tpu_custom_call" | custom-call | flops 18119393280 | bytes 18874368 | tf_op jit(solution)/shard_map/finale/pallas_call | solution.py:925
  370.3 3.3 copy.152
  374.2 3.8 all-to-all-start.2
  378.0 55.1 %spread_sums.1 = (bf16[3072,768]{1,0:T(8,128)(2,1)}, bf16[1024,768]{1,0:T(8,128)(2,1)}) custom-call(bf16[384,384]{1,0:T(8,128)(2,1)} %get-tuple-element.82.shard0_ref, bf16[384,384]{1,0:T(8,128)(2,1)} %get-tuple-element.83.shard1_ref, f32[2,768]{1,0:T(2,128)} %v_ref.3, bf16[1536,768]{1,0:T(8,128)(2,1)} %bitcast.9.refs_0_, ...), custom_call_target="tpu_custom_call" | custom-call | flops 4831838208 | bytes 18874368 | tf_op jit(solution)/shard_map/spread_sums/pallas_call | solution.py:1066
  434.9 6.2 %fusion.25 = (f32[768,768]{1,0:T(8,128)}, f32[768,768]{1,0:T(8,128)}, f32[768,768]{1,0:T(8,128)}, f32[768,768]{1,0:T(8,128)}) fusion(bf16[3072,768]{1,0:T(8,128)(2,1)} %get-tuple-element.89), kind=kLoop, calls=%fused_computation.58 | loop fusion | bytes 18874368 | tf_op jit(solution)/shard_map/slice | solution.py:1159
  441.5 2.2 slice_bitcast_fusion
  443.7 1.6 copy.148
  445.3 1.1 copy.155
  446.5 1.3 copy-done.2
  447.8 1.7 copy.156
  (78 shorter events, 14.0 us)
Async XLA Ops:
  7.2 2.2 copy-start.9
  7.2 2.6 copy-start.17
  7.2 33.1 %all-gather.2.cloned.1.call-start = ((), (), s32[]{:S(2)}) async-start(), calls=%async_computation.4 | async-start | bytes 3932160 | tf_op jit(solution)/shard_map/all_gather | solution.py:1116
  9.6 1.9 copy-start
  10.6 1.7 copy-start.15
  12.9 6.9 %copy-start.7 = (f32[64,128]{1,0:T(8,128)S(1)}, f32[64,128]{1,0:T(8,128)}, u32[]{:S(2)}) copy-start(f32[64,128]{1,0:T(8,128)} %constant.78.clone) | copy-start | bytes 98308
  12.9 6.9 %copy-start.8 = (f32[64,128]{1,0:T(8,128)S(1)}, f32[64,128]{1,0:T(8,128)}, u32[]{:S(2)}) copy-start(f32[64,128]{1,0:T(8,128)} %constant.77.clone) | copy-start | bytes 98308
  12.9 6.9 %copy-start.11 = (f32[36,128]{1,0:T(8,128)S(1)}, f32[36,128]{1,0:T(8,128)}, u32[]{:S(2)}) copy-start(f32[36,128]{1,0:T(8,128)} %constant.80.clone) | copy-start | bytes 55300
  12.9 6.8 %copy-start.12 = (f32[36,128]{1,0:T(8,128)S(1)}, f32[36,128]{1,0:T(8,128)}, u32[]{:S(2)}) copy-start(f32[36,128]{1,0:T(8,128)} %constant.79.clone) | copy-start | bytes 55300
  40.3 4.9 %copy-start.16 = (f32[768]{0:T(1024)S(1)}, f32[768]{0:T(1024)}, u32[]{:S(2)}) copy-start(f32[768]{0:T(1024)} %param.30) | copy-start | bytes 9220
  40.3 5.5 %copy-start.14 = (bf16[2,768,2]{1,2,0:T(2,128)(2,1)S(1)}, bf16[2,768,2]{1,2,0:T(2,128)(2,1)}, u32[]{:S(2)}) copy-start(bf16[2,768,2]{1,2,0:T(2,128)(2,1)} %param.32) | copy-start | bytes 18436
  40.3 5.7 %copy-start.10 = (bf16[768,12]{0,1:T(8,128)(2,1)S(1)}, bf16[768,12]{0,1:T(8,128)(2,1)}, u32[]{:S(2)}) copy-start(bf16[768,12]{0,1:T(8,128)(2,1)} %param.31) | copy-start | bytes 55300
  40.3 5.9 %copy-start.6 = (f32[1024,12]{0,1:T(8,128)S(1)}, f32[1024,12]{0,1:T(8,128)}, u32[]{:S(2)}) copy-start(f32[1024,12]{0,1:T(8,128)} %param.22) | copy-start | bytes 147460
  40.3 71.5 %all-to-all-start = ((bf16[8,192,768]{2,1,0:T(8,128)(2,1)}), bf16[8,192,768]{2,1,0:T(8,128)(2,1)}, u32[]{:S(2)}, u32[]{:S(2)}) async-start(bf16[8,192,768]{2,1,0:T(8,128)(2,1)} %dispatch_grads.1), calls=%async_computation | async-start | bytes 4718592 | tf_op jit(solution)/shard_map/all_to_all | solution.py:1111
  45.0 325.3 %reduce-scatter.2.cloned.1.call-start = ((), (), s32[]{:S(2)}) async-start(), calls=%async_computation.5 | async-start | bytes 11796480 | tf_op jit(solution)/shard_map/reduce_scatter | solution.py:1132
  199.1 1.0 copy-start.1
  201.7 172.5 %all-to-all-start.1 = ((bf16[8,192,768]{2,1,0:T(8,128)(2,1)}), bf16[8,192,768]{2,1,0:T(8,128)(2,1)}, u32[]{:S(2)}, u32[]{:S(2)}) async-start(bf16[8,192,768]{2,1,0:T(8,128)(2,1)} %bitcast.40), calls=%async_computation.2 | async-start | bytes 4718592 | tf_op jit(solution)/shard_map/all_to_all | solution.py:1111
  227.0 63.6 %copy-start.13 = (f32[8,768]{1,0:T(8,128)S(1)}, f32[8,768]{1,0:T(8,128)}, u32[]{:S(2)}) copy-start(f32[8,768]{1,0:T(8,128)} %get-tuple-element.69) | copy-start | bytes 73732
  292.2 77.3 %copy-start.4 = (f32[1024,12]{1,0:T(8,128)S(1)}, f32[1024,12]{1,0:T(8,128)}, u32[]{:S(2)}) copy-start(f32[1024,12]{1,0:T(8,128)} %get-tuple-element.153) | copy-start | bytes 147460
  370.3 3.3 copy-start.5
  374.2 66.9 %all-to-all-start.2 = ((bf16[2,3,768,256]{3,2,1,0:T(8,128)(2,1)}), bf16[2,3,768,256]{3,2,1,0:T(8,128)(2,1)S(1)}, u32[]{:S(2)}, u32[]{:S(2)}) async-start(bf16[2,3,768,256]{3,2,1,0:T(8,128)(2,1)} %bitcast.39), calls=%async_computation.3 | async-start | bytes 4718592 | tf_op jit(solution)/shard_map/all_to_all | solution.py:1147
  443.7 1.6 copy-start.3
  445.3 2.5 copy-start.2
Sparse Core Ops, SparseCore 0:
  10.2 30.0 all-gather.1
  199.3 160.0 reduce-scatter.1

commit v7 on v6

--- a/solution.py
+++ b/solution.py
@@ -105,6 +105,60 @@
         ),
         name="project_own" if own else "project_prompt",
     )(e, x, gain, *weights, cos, sin)
+
+
+MESH = pl.DeviceIdType.MESH
+
+
+def eight():
+    dp, ex = lax.axis_index("dp"), lax.axis_index("expert")
+    j, c, x = dp % 2, ex % 2, ex // 2
+
+    def flip(bit, by):
+        return bit + by * (1 - 2 * bit)
+
+    def peer(r):
+        return dp + (r // 2 % 2) * (1 - 2 * j), flip(x, r // 4) * 2 + flip(c, r % 2)
+
+    def place(r):
+        return flip(j, r // 2 % 2) * 4 + flip(x, r // 4) * 2 + flip(c, r % 2)
+
+    return peer, place
+
+
+def return_outputs(made_hbm, got_hbm, send_sem, recv_sem, local_sem, capacity):
+    peer, place = eight()
+    step = pl.program_id(0)
+
+    def spot(r):
+        return pl.ds(pl.multiple_of(place(r) * capacity, 16), capacity)
+
+    def copies():
+        return [
+            pltpu.make_async_remote_copy(
+                src_ref=made_hbm.at[spot(r)], dst_ref=got_hbm.at[spot(0)], send_sem=send_sem.at[r], recv_sem=recv_sem.at[r],
+                device_id=peer(r), device_id_type=MESH,
+            )
+            for r in range(1, 8)
+        ] + [pltpu.make_async_copy(made_hbm.at[spot(0)], got_hbm.at[spot(0)], local_sem.at[0])]
+
+    barrier = pltpu.get_barrier_semaphore()
+
+    @pl.when(step == 0)
+    def _():
+        for r in range(1, 8):
+            pl.semaphore_signal(barrier, inc=1, device_id=peer(r), device_id_type=MESH)
+
+    @pl.when(step == 1)
+    def _():
+        pl.semaphore_wait(barrier, 7)
+        for copy in copies():
+            copy.start()
+
+    @pl.when(step == pl.num_programs(0) - 1)
+    def _():
+        for copy in copies():
+            copy.wait()
 
 
 def attn_fwd_kernel(e_ref, q_ref, ko_ref, vo_ref, kp_ref, vp_ref, o_ref, lse_ref, vt_ref, qm_ref, m_ref, acc_ref, *, chunk, tile, scale):
@@ -202,10 +256,12 @@
     )(e, q, ko, vo, kp, vp)
 
 
-def attn_bwd_kernel(e_ref, q_ref, do_ref, o_ref, lse_ref, ko_ref, vo_ref, kp_ref, vp_ref, cos_ref, sin_ref,
-               dq_ref, dk_ref, dv_ref,
-               kt_ref, dqt_ref, qm_ref, dom_ref, dl_ref, dks_ref, dvs_ref, *, tile, scale):
-    e = e_ref[0]
+def attn_bwd_kernel(q_ref, do_ref, o_ref, lse_ref, ko_ref, vo_ref, kp_ref, vp_ref, cos_ref, sin_ref, made_hbm,
+               dq_ref, dk_ref, dv_ref, got_hbm,
+               kt_ref, dqt_ref, qm_ref, dom_ref, dl_ref, dks_ref, dvs_ref, send_sem, recv_sem, local_sem, *, tile, scale,
+               capacity):
+    e = lax.axis_index("expert")
+    return_outputs(made_hbm, got_hbm, send_sem, recv_sem, local_sem, capacity)
     rows = q_ref.shape[0]
     half = rows // 2
     chunk = half
@@ -309,7 +365,7 @@
         dq_ref[r:r + cont, :] = (unrope(dq[r:r + cont], npr, cont) * scale).astype(BF)
 
 
-def attn_bwd(e, q, do, o, lse, ko, vo, kp, vp, cos, sin, *, tile=256):
+def attn_bwd(q, do, o, lse, ko, vo, kp, vp, cos, sin, made, capacity, *, tile=256):
     rows, width = q.shape
     npr = kp.shape[0]
     keys = npr + rows // 2
@@ -317,26 +373,25 @@
     own = pl.BlockSpec((rows, 128), lambda i, *_: (0, i))
     pr = pl.BlockSpec((npr, 128), lambda i, *_: (0, i))
     al = pl.BlockSpec((keys, 128), lambda i, *_: (0, i))
+    hbm = pl.BlockSpec(memory_space=pl.ANY)
     tab = pl.BlockSpec(cos.shape, lambda i, *_: (0, 0))
     return pl.pallas_call(
-        functools.partial(attn_bwd_kernel, tile=tile, scale=0.125),
-        grid_spec=pltpu.PrefetchScalarGridSpec(
-            num_scalar_prefetch=1, grid=(pairs,),
-            in_specs=[own, own, own, pl.BlockSpec((1, 2, rows), lambda i, *_: (i, 0, 0)), own, own, pr, pr, tab, tab],
-            out_specs=[own, al, al],
+        functools.partial(attn_bwd_kernel, tile=tile, scale=0.125, capacity=capacity),
+        grid_spec=pl.GridSpec(
+            grid=(pairs,),
+            in_specs=[own, own, own, pl.BlockSpec((1, 2, rows), lambda i, *_: (i, 0, 0)), own, own, pr, pr, tab, tab, hbm],
+            out_specs=[own, al, al, hbm],
             scratch_shapes=[pltpu.VMEM((128, npr + rows), BF), pltpu.VMEM((128, rows), F32),
                             pltpu.VMEM((2, rows, 128), BF), pltpu.VMEM((2, rows, 128), BF),
                             pltpu.VMEM((8, rows), F32),
-                            pltpu.VMEM((rows // 2, 128), F32), pltpu.VMEM((rows // 2, 128), F32)]),
+                            pltpu.VMEM((rows // 2, 128), F32), pltpu.VMEM((rows // 2, 128), F32),
+                            pltpu.SemaphoreType.DMA((8,)), pltpu.SemaphoreType.DMA((8,)), pltpu.SemaphoreType.DMA((1,))]),
         out_shape=[jax.ShapeDtypeStruct((rows, width), BF), jax.ShapeDtypeStruct((keys, width), BF),
-                   jax.ShapeDtypeStruct((keys, width), BF)],
-        compiler_params=params(),
+                   jax.ShapeDtypeStruct((keys, width), BF), jax.ShapeDtypeStruct(made.shape, BF)],
+        compiler_params=params(collective_id=3, has_side_effects=True),
         cost_estimate=pl.CostEstimate(flops=10 * rows * npr * width * 2, bytes_accessed=2 * npr * width * 8, transcendentals=rows * npr * 12),
         name="attn_bwd",
-    )(e, q, do, o, lse, ko, vo, kp, vp, cos, sin)
-
-
-MESH = pl.DeviceIdType.MESH
+    )(q, do, o, lse, ko, vo, kp, vp, cos, sin, made)
 
 
 def pick(values, lane, index):
@@ -1130,11 +1185,10 @@
     x2, h2, aux, ext = gates(tokens, o, w_out, gain2, wcat, prev, routes, experts)
     made, back, ffn_sum = experts_on_rows(slots_t, h2, ext, grads_in, w_gate, w_up, w_down, capacity)
     ffn_sum = lax.psum_scatter(ffn_sum, "dp", scatter_dimension=2, axis_index_groups=alike, tiled=True)
-    made = swap(made.reshape(members, capacity, width)).reshape(-1, width)
     grad_prev, dx2, da, do, cat, sums = combine(
         back, slots, routes, aux, x2, h2, cotangent, gain2, wcat, const_v, w_out, experts
     )
-    dq, dk, dv = attn_bwd(e, q, do, o, lse, k_own, v_own, k_prompt, v_prompt, cos, sin)
+    dq, dk, dv, made = attn_bwd(q, do, o, lse, k_own, v_own, k_prompt, v_prompt, cos, sin, made, capacity)
     rest = dp // 2
     n = experts
     small = jnp.concatenate([cat[:n + 4], sums[:3], jnp.zeros((5, width), F32)], axis=0)

time: 461 us -> 460 us (level)
  starting transfers between devices: 13.5 us -> 8.73 us
    all_to_all x2 -> x1, starting transfers between devices: 9.41 us -> 4.67 us  [swap(): lax.all_to_all(x, everyone, split_axis=0, concat_axis=0, axis_index_group...]
  transfers between devices with their start and end apart: 5 -> 4, of which waited for: 1 -> 1; matrix products, arithmetic and copies ran while one was open for 6% -> 5% of each run, Pallas kernels for 65% -> 65%
where the time goes in v7:
time: 460 us; the launch traced here: 455 us
  Pallas kernels  385 us (84%)
  local copies, waits for them, and re-layouts  29.3 us (6%)
  between operations  14.8 us (3%)
  waiting for transfers between devices  9.45 us (2%)
  starting transfers between devices  8.73 us (2%)
  other arithmetic  6.54 us (1%)
    pallas_call x1, Pallas kernels, experts_on_rows(): pl.pallas_call(functools.partial(expert_kernel, capacity=capacity, tile=t...  87.3 us
    pallas_call x1, Pallas kernels, finale(): pl.pallas_call(functools.partial(finale_kernel, rest=rest, chunks=chunks,...  79.6 us
    pallas_call x1, Pallas kernels, attn_bwd(): pl.pallas_call(functools.partial(attn_bwd_kernel, tile=tile, scale=0.125,...  64.3 us
    pallas_call x1, Pallas kernels, spread_sums(): pl.pallas_call(functools.partial(spread_kernel, rest=rest, chunks=chunks,...  54.1 us
    pallas_call x1, Pallas kernels, attn_fwd(): pl.pallas_call(functools.partial(attn_fwd_kernel, chunk=chunk, tile=tile,...  44.6 us
    pallas_call x1, Pallas kernels, combine(): pl.pallas_call(functools.partial(combine_kernel, experts=experts), grid=(...  20.6 us
    pallas_call x2, Pallas kernels, project(): pl.pallas_call(functools.partial(project_kernel, count=len(weights)), gri...  20.4 us
    all_gather x1, waiting for transfers between devices, local(): prompt_x = lax.all_gather(tokens[:prompt_dev], 'expert', axis=0, tiled=True)  9.41 us
  transfers between devices with their start and end apart: 4, of which 1 were waited for; matrix products, arithmetic and copies ran while one was open for 5% of the time, Pallas kernels for 65%

profile of v7, /device:TPU:9, one launch (start us, length us, event | category | flops | bytes accessed | tf_op | source)
XLA Modules:
  0.0 454.7 jit_solution(8091408428702298908)
XLA Ops:
  7.2 2.1 slice.45
  12.9 6.8 %dispatch_grads.1 = bf16[8,192,768]{2,1,0:T(8,128)(2,1)} custom-call(s32[2,1024]{1,0:T(2,128)} %copy.134.slot_ref, bf16[1024,768]{1,0:T(8,128)(2,1)} %g_ref.1), custom_call_target="tpu_custom_call" | custom-call | flops 2415919104 | bytes 3145728 | tf_op jit(solution)/shard_map/dispatch_grads/pallas_call | solution.py:465
  19.7 1.3 multiply_add_fusion
  21.1 1.1 bitcast_multiply_fusion.refs_4_.refs_3_.sin_ref
  22.2 8.7 %project_own.1 = (bf16[1024,768]{1,0:T(8,128)(2,1)}, bf16[1024,768]{1,0:T(8,128)(2,1)}, bf16[1024,768]{1,0:T(8,128)(2,1)}, bf16[1024,768]{1,0:T(8,128)(2,1)}) custom-call(s32[1]{0:T(128)} %bitcast.1.e_ref, bf16[1024,768]{1,0:T(8,128)(2,1)} %refs_10_.1, f32[1,768]{1,0:T(1,128)} %broadcast_in_dim.46.gain_ref, bf16[768,768]{1,0:T(8,128)(2,1)} %refs_4_.1, ...), custom_call_target="tpu_custom_call" | custom-call | flops 3623878656 | bytes 9437184 | tf_op jit(solution)/shard_map/project_own/pallas_call | solution.py:93
  30.9 9.4 %all-gather.2.cloned.1.call-done.x_ref = bf16[2048,768]{1,0:T(8,128)(2,1)} async-done(((bf16[512,768]{1,0:T(8,128)(2,1)}), bf16[2048,768]{1,0:T(8,128)(2,1)}) %all-gather.2.cloned.1.call-update) | async-done | bytes 3145744 | tf_op jit(solution)/shard_map/all_gather | solution.py:1171
  40.3 4.7 %all-to-all-start = ((bf16[8,192,768]{2,1,0:T(8,128)(2,1)}), bf16[8,192,768]{2,1,0:T(8,128)(2,1)}, u32[]{:S(2)}, u32[]{:S(2)}) async-start(bf16[8,192,768]{2,1,0:T(8,128)(2,1)} %dispatch_grads.1), calls=%async_computation | async-start | bytes 4718592 | tf_op jit(solution)/shard_map/all_to_all | solution.py:1166
  48.2 11.7 %project_prompt.1 = (bf16[2048,768]{1,0:T(8,128)(2,1)}, bf16[2048,768]{1,0:T(8,128)(2,1)}, bf16[2048,768]{1,0:T(8,128)(2,1)}) custom-call(s32[1]{0:T(128)} %bitcast.1.e_ref, bf16[2048,768]{1,0:T(8,128)(2,1)} %all-gather.2.cloned.1.call-done.x_ref, f32[1,768]{1,0:T(1,128)} %broadcast_in_dim.46.gain_ref, bf16[768,768]{1,0:T(8,128)(2,1)} %refs_6_.1, ...), custom_call_target="tpu_custom_call" | custom-call | flops 4831838208 | bytes 18874368 | tf_op jit(solution)/shard_map/project_prompt/pallas_call | solution.py:93
  59.8 44.6 %attn_fwd.1 = (bf16[1024,768]{1,0:T(8,128)(2,1)}, f32[6,2,1024]{2,1,0:T(2,128)}) custom-call(s32[1]{0:T(128)} %bitcast.1.e_ref, bf16[1024,768]{1,0:T(8,128)(2,1)} %get-tuple-element.54.q_ref, bf16[1024,768]{1,0:T(8,128)(2,1)} %get-tuple-element.55.ko_ref, bf16[1024,768]{1,0:T(8,128)(2,1)} %get-tuple-element.56.vo_ref, ...), custom_call_target="tpu_custom_call" | custom-call | flops 12884901888 | bytes 12582912 | tf_op jit(solution)/shard_map/attn_fwd/pallas_call | solution.py:244
  104.4 7.4 %gates.1 = (f32[1024,768]{1,0:T(8,128)}, bf16[1024,768]{1,0:T(8,128)(2,1)}, f32[1024,128]{1,0:T(8,128)}, bf16[1024,256]{1,0:T(8,128)(2,1)}) custom-call(bf16[1024,768]{1,0:T(8,128)(2,1)} %refs_10_.1, bf16[1024,768]{1,0:T(8,128)(2,1)} %get-tuple-element.61.o_ref.refs_2_, bf16[768,768]{1,0:T(8,128)(2,1)} %w_ref.3, f32[1,768]{1,0:T(1,128)} %broadcast_in_dim.49.gain_ref, ...), custom_call_target="tpu_custom_call" | custom-call | flops 1207959552 | bytes 9437184 | tf_op jit(solution)/shard_map/gates/pallas_call | solution.py:443
  111.8 87.3 %experts_on_rows.1 = (bf16[1536,768]{1,0:T(8,128)(2,1)}, bf16[1536,896]{1,0:T(8,128)(2,1)}, bf16[3,768,2048]{2,1,0:T(8,128)(2,1)}) custom-call(s32[2,1024]{1,0:T(2,128)} %copy.134.slot_ref, bf16[1024,768]{1,0:T(8,128)(2,1)} %get-tuple-element.62.h2_ref.refs_5_, bf16[1024,256]{1,0:T(8,128)(2,1)} %get-tuple-element.63.ext_ref, ...), custom_call_target="tpu_custom_call" | custom-call | flops 43486543872 | bytes 28311552 | tf_op jit(solution)/shard_map/experts_on_rows/pallas_call | solution.py:608
  200.2 1.5 fusion.13.slot_ref.refs_1_
  201.7 20.6 %combine.1 = (f32[1024,12]{1,0:T(8,128)}, f32[1024,768]{1,0:T(8,128)}, bf16[1024,768]{1,0:T(8,128)(2,1)}, bf16[1024,768]{1,0:T(8,128)(2,1)}, f32[128,768]{1,0:T(8,128)}, /*index=5*/f32[8,768]{1,0:T(8,128)}) custom-call(bf16[1536,896]{1,0:T(8,128)(2,1)} %get-tuple-element.66.back_ref, s32[1024,2]{1,0:T(8,128)} %fusion.13.slot_ref.refs_1_, s32[1024,2]{1,0:T(8,128)} %copy-done, ...), custom_call_target="tpu_custom_call" | custom-call | flops 4831838208 | bytes 20447232 | tf_op jit(solution)/shard_map/combine/pallas_call | solution.py:710
  224.6 64.3 %attn_bwd.1 = (bf16[1024,768]{1,0:T(8,128)(2,1)}, bf16[2560,768]{1,0:T(8,128)(2,1)}, bf16[2560,768]{1,0:T(8,128)(2,1)}, bf16[1536,768]{1,0:T(8,128)(2,1)}) custom-call(bf16[1024,768]{1,0:T(8,128)(2,1)} %get-tuple-element.54.q_ref, bf16[1024,768]{1,0:T(8,128)(2,1)} %get-tuple-element.72.do_ref, bf16[1024,768]{1,0:T(8,128)(2,1)} %get-tuple-element.61.o_ref.refs_2_, ...), custom_call_target="tpu_custom_call" | custom-call | flops 32212254720 | bytes 25165824 | tf_op jit(solution)/shard_map/attn_bwd/pallas_call | solution.py:378
  288.8 79.6 %finale.1 = (bf16[384,384]{1,0:T(8,128)(2,1)}, bf16[384,384]{1,0:T(8,128)(2,1)}, f32[24,768]{1,0:T(8,128)}, f32[1024,768]{1,0:T(8,128)}) custom-call(f32[24,768]{1,0:T(8,128)} %maximum_maximum_fusion.1.small_ref, f32[1,768]{1,0:T(1,128)} %broadcast_in_dim.46.gain_ref, bf16[1024,768]{1,0:T(8,128)(2,1)} %get-tuple-element.71.refs_0_, ...), custom_call_target="tpu_custom_call" | custom-call | flops 18119393280 | bytes 18874368 | tf_op jit(solution)/shard_map/finale/pallas_call | solution.py:980
  369.3 3.3 copy.152
  373.1 3.8 all-to-all-start.1
  376.9 54.1 %spread_sums.1 = (bf16[3072,768]{1,0:T(8,128)(2,1)}, bf16[1024,768]{1,0:T(8,128)(2,1)}) custom-call(bf16[384,384]{1,0:T(8,128)(2,1)} %get-tuple-element.84.shard0_ref, bf16[384,384]{1,0:T(8,128)(2,1)} %get-tuple-element.85.shard1_ref, f32[2,768]{1,0:T(2,128)} %v_ref.3, bf16[1536,768]{1,0:T(8,128)(2,1)} %get-tuple-element.86.refs_0_, ...), custom_call_target="tpu_custom_call" | custom-call | flops 4831838208 | bytes 18874368 | tf_op jit(solution)/shard_map/spread_sums/pallas_call | solution.py:1121
  432.9 6.2 %fusion.25 = (f32[768,768]{1,0:T(8,128)}, f32[768,768]{1,0:T(8,128)}, f32[768,768]{1,0:T(8,128)}, f32[768,768]{1,0:T(8,128)}) fusion(bf16[3072,768]{1,0:T(8,128)(2,1)} %get-tuple-element.91), kind=kLoop, calls=%fused_computation.58 | loop fusion | bytes 18874368 | tf_op jit(solution)/shard_map/slice | solution.py:1213
  439.6 2.2 slice_bitcast_fusion
  441.7 1.6 copy.148
  443.3 1.1 copy.155
  444.5 1.3 copy-done.2
  445.8 1.7 copy.156
  (74 shorter events, 13.6 us)
Async XLA Ops:
  7.2 2.2 copy-start.9
  7.2 2.6 copy-start.16
  7.2 33.1 %all-gather.2.cloned.1.call-start = ((), (), s32[]{:S(2)}) async-start(), calls=%async_computation.3 | async-start | bytes 3932160 | tf_op jit(solution)/shard_map/all_gather | solution.py:1171
  9.6 1.9 copy-start
  10.6 1.7 copy-start.14
  12.9 6.9 %copy-start.7 = (f32[64,128]{1,0:T(8,128)S(1)}, f32[64,128]{1,0:T(8,128)}, u32[]{:S(2)}) copy-start(f32[64,128]{1,0:T(8,128)} %constant.78.clone) | copy-start | bytes 98308
  12.9 6.9 %copy-start.8 = (f32[64,128]{1,0:T(8,128)S(1)}, f32[64,128]{1,0:T(8,128)}, u32[]{:S(2)}) copy-start(f32[64,128]{1,0:T(8,128)} %constant.77.clone) | copy-start | bytes 98308
  12.9 6.9 %copy-start.11 = (f32[36,128]{1,0:T(8,128)S(1)}, f32[36,128]{1,0:T(8,128)}, u32[]{:S(2)}) copy-start(f32[36,128]{1,0:T(8,128)} %constant.80.clone) | copy-start | bytes 55300
  12.9 6.8 %copy-start.12 = (f32[36,128]{1,0:T(8,128)S(1)}, f32[36,128]{1,0:T(8,128)}, u32[]{:S(2)}) copy-start(f32[36,128]{1,0:T(8,128)} %constant.79.clone) | copy-start | bytes 55300
  40.3 4.9 %copy-start.15 = (f32[768]{0:T(1024)S(1)}, f32[768]{0:T(1024)}, u32[]{:S(2)}) copy-start(f32[768]{0:T(1024)} %param.30) | copy-start | bytes 9220
  40.3 5.5 %copy-start.13 = (bf16[2,768,2]{1,2,0:T(2,128)(2,1)S(1)}, bf16[2,768,2]{1,2,0:T(2,128)(2,1)}, u32[]{:S(2)}) copy-start(bf16[2,768,2]{1,2,0:T(2,128)(2,1)} %param.32) | copy-start | bytes 18436
  40.3 5.7 %copy-start.10 = (bf16[768,12]{0,1:T(8,128)(2,1)S(1)}, bf16[768,12]{0,1:T(8,128)(2,1)}, u32[]{:S(2)}) copy-start(bf16[768,12]{0,1:T(8,128)(2,1)} %param.31) | copy-start | bytes 55300
  40.3 5.9 %copy-start.6 = (f32[1024,12]{0,1:T(8,128)S(1)}, f32[1024,12]{0,1:T(8,128)}, u32[]{:S(2)}) copy-start(f32[1024,12]{0,1:T(8,128)} %param.22) | copy-start | bytes 147460
  40.3 71.5 %all-to-all-start = ((bf16[8,192,768]{2,1,0:T(8,128)(2,1)}), bf16[8,192,768]{2,1,0:T(8,128)(2,1)}, u32[]{:S(2)}, u32[]{:S(2)}) async-start(bf16[8,192,768]{2,1,0:T(8,128)(2,1)} %dispatch_grads.1), calls=%async_computation | async-start | bytes 4718592 | tf_op jit(solution)/shard_map/all_to_all | solution.py:1166
  45.0 324.3 %reduce-scatter.2.cloned.1.call-start = ((), (), s32[]{:S(2)}) async-start(), calls=%async_computation.4 | async-start | bytes 11796480 | tf_op jit(solution)/shard_map/reduce_scatter | solution.py:1187
  199.2 1.0 copy-start.1
  288.8 79.6 %copy-start.4 = (f32[1024,12]{1,0:T(8,128)S(1)}, f32[1024,12]{1,0:T(8,128)}, u32[]{:S(2)}) copy-start(f32[1024,12]{1,0:T(8,128)} %get-tuple-element.155) | copy-start | bytes 147460
  369.3 3.3 copy-start.5
  373.1 66.0 %all-to-all-start.1 = ((bf16[2,3,768,256]{3,2,1,0:T(8,128)(2,1)}), bf16[2,3,768,256]{3,2,1,0:T(8,128)(2,1)S(1)}, u32[]{:S(2)}, u32[]{:S(2)}) async-start(bf16[2,3,768,256]{3,2,1,0:T(8,128)(2,1)} %bitcast.37), calls=%async_computation.2 | async-start | bytes 4718592 | tf_op jit(solution)/shard_map/all_to_all | solution.py:1201
  441.7 1.6 copy-start.3
  443.3 2.5 copy-start.2
Sparse Core Ops, SparseCore 0:
  10.2 30.0 all-gather.1
  199.3 166.3 reduce-scatter.1

commit v8 on v7

--- a/solution.py
+++ b/solution.py
@@ -126,7 +126,7 @@
     return peer, place
 
 
-def return_outputs(made_hbm, got_hbm, send_sem, recv_sem, local_sem, capacity):
+def exchange_rows(rows_hbm, got_hbm, send_sem, recv_sem, local_sem, capacity):
     peer, place = eight()
     step = pl.program_id(0)
 
@@ -136,11 +136,11 @@
     def copies():
         return [
             pltpu.make_async_remote_copy(
-                src_ref=made_hbm.at[spot(r)], dst_ref=got_hbm.at[spot(0)], send_sem=send_sem.at[r], recv_sem=recv_sem.at[r],
+                src_ref=rows_hbm.at[spot(r)], dst_ref=got_hbm.at[spot(0)], send_sem=send_sem.at[r], recv_sem=recv_sem.at[r],
                 device_id=peer(r), device_id_type=MESH,
             )
             for r in range(1, 8)
-        ] + [pltpu.make_async_copy(made_hbm.at[spot(0)], got_hbm.at[spot(0)], local_sem.at[0])]
+        ] + [pltpu.make_async_copy(rows_hbm.at[spot(0)], got_hbm.at[spot(0)], local_sem.at[0])]
 
     barrier = pltpu.get_barrier_semaphore()
 
@@ -161,8 +161,10 @@
             copy.wait()
 
 
-def attn_fwd_kernel(e_ref, q_ref, ko_ref, vo_ref, kp_ref, vp_ref, o_ref, lse_ref, vt_ref, qm_ref, m_ref, acc_ref, *, chunk, tile, scale):
-    e = e_ref[0]
+def attn_fwd_kernel(q_ref, ko_ref, vo_ref, kp_ref, vp_ref, rows_hbm, o_ref, lse_ref, got_hbm, vt_ref, qm_ref, m_ref, acc_ref,
+                    send_sem, recv_sem, local_sem, *, chunk, tile, scale, capacity):
+    e = lax.axis_index("expert")
+    exchange_rows(rows_hbm, got_hbm, send_sem, recv_sem, local_sem, capacity)
     rows = q_ref.shape[0]
     half = rows // 2
     npr = kp_ref.shape[0]
@@ -235,33 +237,36 @@
     o_ref[...] = jnp.concatenate(outs, axis=0).T.astype(BF)
 
 
-def attn_fwd(e, q, ko, vo, kp, vp, *, chunk=512, tile=256):
+def attn_fwd(q, ko, vo, kp, vp, made, capacity, *, chunk=512, tile=256):
     rows, width = q.shape
     npr = kp.shape[0]
     pairs = width // 128
+    hbm = pl.BlockSpec(memory_space=pl.ANY)
     own = pl.BlockSpec((rows, 128), lambda i, *_: (0, i))
     pr = pl.BlockSpec((npr, 128), lambda i, *_: (0, i))
     return pl.pallas_call(
-        functools.partial(attn_fwd_kernel, chunk=chunk, tile=tile, scale=0.125),
-        grid_spec=pltpu.PrefetchScalarGridSpec(
-            num_scalar_prefetch=1, grid=(pairs,),
-            in_specs=[own, own, own, pr, pr],
-            out_specs=[own, pl.BlockSpec((1, 2, rows), lambda i, *_: (i, 0, 0))],
+        functools.partial(attn_fwd_kernel, chunk=chunk, tile=tile, scale=0.125, capacity=capacity),
+        grid_spec=pl.GridSpec(
+            grid=(pairs,),
+            in_specs=[own, own, own, pr, pr, hbm],
+            out_specs=[own, pl.BlockSpec((1, 2, rows), lambda i, *_: (i, 0, 0)), hbm],
             scratch_shapes=[pltpu.VMEM((2, 80, npr + rows), BF), pltpu.VMEM((2, rows, 128), BF),
-            pltpu.VMEM((2, 8, rows), F32), pltpu.VMEM((2, 80, rows), F32)]),
-        out_shape=[jax.ShapeDtypeStruct((rows, width), BF), jax.ShapeDtypeStruct((pairs, 2, rows), F32)],
-        compiler_params=params(),
+            pltpu.VMEM((2, 8, rows), F32), pltpu.VMEM((2, 80, rows), F32),
+            pltpu.SemaphoreType.DMA((8,)), pltpu.SemaphoreType.DMA((8,)), pltpu.SemaphoreType.DMA((1,))]),
+        out_shape=[jax.ShapeDtypeStruct((rows, width), BF), jax.ShapeDtypeStruct((pairs, 2, rows), F32),
+                   jax.ShapeDtypeStruct(made.shape, BF)],
+        compiler_params=params(collective_id=4, has_side_effects=True),
         cost_estimate=pl.CostEstimate(flops=4 * rows * npr * width * 2, bytes_accessed=2 * npr * width * 4, transcendentals=rows * npr * 12),
         name="attn_fwd",
-    )(e, q, ko, vo, kp, vp)
-
-
-def attn_bwd_kernel(q_ref, do_ref, o_ref, lse_ref, ko_ref, vo_ref, kp_ref, vp_ref, cos_ref, sin_ref, made_hbm,
+    )(q, ko, vo, kp, vp, made)
+
+
+def attn_bwd_kernel(q_ref, do_ref, o_ref, lse_ref, ko_ref, vo_ref, kp_ref, vp_ref, cos_ref, sin_ref, rows_hbm,
                dq_ref, dk_ref, dv_ref, got_hbm,
                kt_ref, dqt_ref, qm_ref, dom_ref, dl_ref, dks_ref, dvs_ref, send_sem, recv_sem, local_sem, *, tile, scale,
                capacity):
     e = lax.axis_index("expert")
-    return_outputs(made_hbm, got_hbm, send_sem, recv_sem, local_sem, capacity)
+    exchange_rows(rows_hbm, got_hbm, send_sem, recv_sem, local_sem, capacity)
     rows = q_ref.shape[0]
     half = rows // 2
     chunk = half
@@ -1157,13 +1162,8 @@
     e = lax.axis_index("expert").astype(jnp.int32).reshape(1)
     j = (lax.axis_index("dp") % pair).astype(jnp.int32).reshape(1)
     members = pair * expert_devices
-    everyone = ("dp", "expert")
-    exchange = [list(range(p * members, (p + 1) * members)) for p in range(dp // pair)]
     alike = [list(range(q, dp, pair)) for q in range(pair)]
     pairs = [list(range(p * pair, (p + 1) * pair)) for p in range(dp // pair)]
-
-    def swap(x):
-        return lax.all_to_all(x, everyone, split_axis=0, concat_axis=0, axis_index_groups=exchange, tiled=True)
 
     cos, sin = angle_tables()
     gain1, gain2 = norm_attn[None, :], norm_ffn[None, :]
@@ -1174,9 +1174,8 @@
     grads_out = dispatch(slots_t, cotangent, members, capacity)
     h_own, q, k_own, v_own = project(e, tokens, gain1, (w_query, w_key, w_value), cos, sin, True)
     prompt_x, grads_out, h_own = lax.optimization_barrier((prompt_x, grads_out, h_own))
-    grads_in = swap(grads_out).reshape(-1, width)
     h_prompt, k_prompt, v_prompt = project(e, prompt_x, gain1, (w_key, w_value), cos, sin, False)
-    o, lse = attn_fwd(e, q, k_own, v_own, k_prompt, v_prompt)
+    o, lse, grads_in = attn_fwd(q, k_own, v_own, k_prompt, v_prompt, grads_out.reshape(-1, width), capacity)
 
     wcat = jnp.concatenate(
         [router, const_w.transpose(1, 0, 2).reshape(width, -1), jnp.zeros((width, 128 - experts - 4), BF)], axis=1

time: 460 us -> 456 us (level)
  starting transfers between devices: 8.73 us -> 3.89 us
    all_to_all x1 -> x0, starting transfers between devices: 4.67 us -> none  [swap(): lax.all_to_all(x, everyone, split_axis=0, concat_axis=0, axis_index_group...]
  transfers between devices with their start and end apart: 4 -> 3, of which waited for: 1 -> 1; matrix products, arithmetic and copies ran while one was open for 5% -> 5% of each run, Pallas kernels for 65% -> 52%
where the time goes in v8:
time: 456 us; the launch traced here: 447 us
  Pallas kernels  385 us (84%)
  local copies, waits for them, and re-layouts  29.3 us (6%)
  between operations  14.8 us (3%)
  other arithmetic  6.56 us (1%)
  waiting for transfers between devices  6.41 us (1%)
    pallas_call x1, Pallas kernels, experts_on_rows(): pl.pallas_call(functools.partial(expert_kernel, capacity=capacity, tile=t...  86.2 us
    pallas_call x1, Pallas kernels, finale(): pl.pallas_call(functools.partial(finale_kernel, rest=rest, chunks=chunks,...  79.2 us
    pallas_call x1, Pallas kernels, attn_bwd(): pl.pallas_call(functools.partial(attn_bwd_kernel, tile=tile, scale=0.125,...  64.5 us
    pallas_call x1, Pallas kernels, spread_sums(): pl.pallas_call(functools.partial(spread_kernel, rest=rest, chunks=chunks,...  54.2 us
    pallas_call x1, Pallas kernels, attn_fwd(): pl.pallas_call(functools.partial(attn_fwd_kernel, chunk=chunk, tile=tile,...  45.5 us
    pallas_call x1, Pallas kernels, combine(): pl.pallas_call(functools.partial(combine_kernel, experts=experts), grid=(...  20.7 us
    pallas_call x2, Pallas kernels, project(): pl.pallas_call(functools.partial(project_kernel, count=len(weights)), gri...  20.4 us
  transfers between devices with their start and end apart: 3, of which 1 were waited for; matrix products, arithmetic and copies ran while one was open for 5% of the time, Pallas kernels for 52%

profile of v8, /device:TPU:9, one launch (start us, length us, event | category | flops | bytes accessed | tf_op | source)
XLA Modules:
  0.0 446.8 jit_solution(16792933395034285957)
XLA Ops:
  7.2 2.1 slice.45
  14.2 0.8 pad.4.prev_ref
  15.1 6.8 %dispatch_grads.1 = bf16[8,192,768]{2,1,0:T(8,128)(2,1)} custom-call(s32[2,1024]{1,0:T(2,128)} %copy.134.slot_ref, bf16[1024,768]{1,0:T(8,128)(2,1)} %g_ref.1), custom_call_target="tpu_custom_call" | custom-call | flops 2415919104 | bytes 3145728 | tf_op jit(solution)/shard_map/dispatch_grads/pallas_call | solution.py:470
  22.7 1.4 multiply_add_fusion
  24.1 1.1 bitcast_multiply_fusion.refs_4_.refs_3_.sin_ref
  25.2 8.7 %project_own.1 = (bf16[1024,768]{1,0:T(8,128)(2,1)}, bf16[1024,768]{1,0:T(8,128)(2,1)}, bf16[1024,768]{1,0:T(8,128)(2,1)}, bf16[1024,768]{1,0:T(8,128)(2,1)}) custom-call(s32[1]{0:T(128)} %bitcast.1.e_ref, bf16[1024,768]{1,0:T(8,128)(2,1)} %refs_10_.1, f32[1,768]{1,0:T(1,128)} %broadcast_in_dim.46.gain_ref, bf16[768,768]{1,0:T(8,128)(2,1)} %refs_4_.1, ...), custom_call_target="tpu_custom_call" | custom-call | flops 3623878656 | bytes 9437184 | tf_op jit(solution)/shard_map/project_own/pallas_call | solution.py:93
  33.9 6.4 %all-gather.2.cloned.1.call-done.x_ref = bf16[2048,768]{1,0:T(8,128)(2,1)} async-done(((bf16[512,768]{1,0:T(8,128)(2,1)}), bf16[2048,768]{1,0:T(8,128)(2,1)}) %all-gather.2.cloned.1.call-update) | async-done | bytes 3145744 | tf_op jit(solution)/shard_map/all_gather | solution.py:1171
  40.3 11.7 %project_prompt.1 = (bf16[2048,768]{1,0:T(8,128)(2,1)}, bf16[2048,768]{1,0:T(8,128)(2,1)}, bf16[2048,768]{1,0:T(8,128)(2,1)}) custom-call(s32[1]{0:T(128)} %bitcast.1.e_ref, bf16[2048,768]{1,0:T(8,128)(2,1)} %all-gather.2.cloned.1.call-done.x_ref, f32[1,768]{1,0:T(1,128)} %broadcast_in_dim.46.gain_ref, bf16[768,768]{1,0:T(8,128)(2,1)} %refs_6_.1, ...), custom_call_target="tpu_custom_call" | custom-call | flops 4831838208 | bytes 18874368 | tf_op jit(solution)/shard_map/project_prompt/pallas_call | solution.py:93
  52.0 45.5 %attn_fwd.1 = (bf16[1024,768]{1,0:T(8,128)(2,1)}, f32[6,2,1024]{2,1,0:T(2,128)}, bf16[1536,768]{1,0:T(8,128)(2,1)}) custom-call(bf16[1024,768]{1,0:T(8,128)(2,1)} %get-tuple-element.55.q_ref, bf16[1024,768]{1,0:T(8,128)(2,1)} %get-tuple-element.56.ko_ref, bf16[1024,768]{1,0:T(8,128)(2,1)} %get-tuple-element.57.vo_ref, ...), custom_call_target="tpu_custom_call" | custom-call | flops 12884901888 | bytes 12582912 | tf_op jit(solution)/shard_map/attn_fwd/pallas_call | solution.py:247
  97.5 7.6 %gates.1 = (f32[1024,768]{1,0:T(8,128)}, bf16[1024,768]{1,0:T(8,128)(2,1)}, f32[1024,128]{1,0:T(8,128)}, bf16[1024,256]{1,0:T(8,128)(2,1)}) custom-call(bf16[1024,768]{1,0:T(8,128)(2,1)} %refs_10_.1, bf16[1024,768]{1,0:T(8,128)(2,1)} %get-tuple-element.63.o_ref.refs_2_, bf16[768,768]{1,0:T(8,128)(2,1)} %w_ref.3, f32[1,768]{1,0:T(1,128)} %broadcast_in_dim.49.gain_ref, ...), custom_call_target="tpu_custom_call" | custom-call | flops 1207959552 | bytes 9437184 | tf_op jit(solution)/shard_map/gates/pallas_call | solution.py:448
  105.1 86.2 %experts_on_rows.1 = (bf16[1536,768]{1,0:T(8,128)(2,1)}, bf16[1536,896]{1,0:T(8,128)(2,1)}, bf16[3,768,2048]{2,1,0:T(8,128)(2,1)}) custom-call(s32[2,1024]{1,0:T(2,128)} %copy.134.slot_ref, bf16[1024,768]{1,0:T(8,128)(2,1)} %get-tuple-element.64.h2_ref.refs_5_, bf16[1024,256]{1,0:T(8,128)(2,1)} %get-tuple-element.65.ext_ref, ...), custom_call_target="tpu_custom_call" | custom-call | flops 43486543872 | bytes 28311552 | tf_op jit(solution)/shard_map/experts_on_rows/pallas_call | solution.py:613
  192.3 1.5 fusion.13.slot_ref.refs_1_
  193.8 20.7 %combine.1 = (f32[1024,12]{1,0:T(8,128)}, f32[1024,768]{1,0:T(8,128)}, bf16[1024,768]{1,0:T(8,128)(2,1)}, bf16[1024,768]{1,0:T(8,128)(2,1)}, f32[128,768]{1,0:T(8,128)}, /*index=5*/f32[8,768]{1,0:T(8,128)}) custom-call(bf16[1536,896]{1,0:T(8,128)(2,1)} %get-tuple-element.68.back_ref, s32[1024,2]{1,0:T(8,128)} %fusion.13.slot_ref.refs_1_, s32[1024,2]{1,0:T(8,128)} %copy-done, ...), custom_call_target="tpu_custom_call" | custom-call | flops 4831838208 | bytes 20447232 | tf_op jit(solution)/shard_map/combine/pallas_call | solution.py:715
  216.8 64.5 %attn_bwd.1 = (bf16[1024,768]{1,0:T(8,128)(2,1)}, bf16[2560,768]{1,0:T(8,128)(2,1)}, bf16[2560,768]{1,0:T(8,128)(2,1)}, bf16[1536,768]{1,0:T(8,128)(2,1)}) custom-call(bf16[1024,768]{1,0:T(8,128)(2,1)} %get-tuple-element.55.q_ref, bf16[1024,768]{1,0:T(8,128)(2,1)} %get-tuple-element.74.do_ref, bf16[1024,768]{1,0:T(8,128)(2,1)} %get-tuple-element.63.o_ref.refs_2_, ...), custom_call_target="tpu_custom_call" | custom-call | flops 32212254720 | bytes 25165824 | tf_op jit(solution)/shard_map/attn_bwd/pallas_call | solution.py:383
  281.2 79.2 %finale.1 = (bf16[384,384]{1,0:T(8,128)(2,1)}, bf16[384,384]{1,0:T(8,128)(2,1)}, f32[24,768]{1,0:T(8,128)}, f32[1024,768]{1,0:T(8,128)}) custom-call(f32[24,768]{1,0:T(8,128)} %maximum_maximum_fusion.1.small_ref, f32[1,768]{1,0:T(1,128)} %broadcast_in_dim.46.gain_ref, bf16[1024,768]{1,0:T(8,128)(2,1)} %get-tuple-element.73.refs_0_, ...), custom_call_target="tpu_custom_call" | custom-call | flops 18119393280 | bytes 18874368 | tf_op jit(solution)/shard_map/finale/pallas_call | solution.py:985
  361.3 3.3 copy.152
  365.2 3.8 all-to-all-start
  369.0 54.2 %spread_sums.1 = (bf16[3072,768]{1,0:T(8,128)(2,1)}, bf16[1024,768]{1,0:T(8,128)(2,1)}) custom-call(bf16[384,384]{1,0:T(8,128)(2,1)} %get-tuple-element.86.shard0_ref, bf16[384,384]{1,0:T(8,128)(2,1)} %get-tuple-element.87.shard1_ref, f32[2,768]{1,0:T(2,128)} %v_ref.3, bf16[1536,768]{1,0:T(8,128)(2,1)} %get-tuple-element.88.refs_0_, ...), custom_call_target="tpu_custom_call" | custom-call | flops 4831838208 | bytes 18874368 | tf_op jit(solution)/shard_map/spread_sums/pallas_call | solution.py:1126
  425.0 6.2 %fusion.25 = (f32[768,768]{1,0:T(8,128)}, f32[768,768]{1,0:T(8,128)}, f32[768,768]{1,0:T(8,128)}, f32[768,768]{1,0:T(8,128)}) fusion(bf16[3072,768]{1,0:T(8,128)(2,1)} %get-tuple-element.93), kind=kLoop, calls=%fused_computation.58 | loop fusion | bytes 18874368 | tf_op jit(solution)/shard_map/slice | solution.py:1212
  431.7 2.2 slice_bitcast_fusion
  433.8 1.6 copy.148
  435.4 1.1 copy.155
  436.6 1.3 copy-done.2
  437.9 1.7 copy.156
  (72 shorter events, 12.6 us)
Async XLA Ops:
  7.2 2.2 copy-start.9
  7.2 2.7 copy-start.16
  7.2 33.1 %all-gather.2.cloned.1.call-start = ((), (), s32[]{:S(2)}) async-start(), calls=%async_computation.2 | async-start | bytes 3932160 | tf_op jit(solution)/shard_map/all_gather | solution.py:1171
  9.3 352.0 %reduce-scatter.2.cloned.1.call-start = ((), (), s32[]{:S(2)}) async-start(), calls=%async_computation.3 | async-start | bytes 11796480 | tf_op jit(solution)/shard_map/reduce_scatter | solution.py:1186
  9.6 1.9 copy-start
  10.7 1.7 copy-start.14
  10.7 2.3 copy-start.15
  10.7 2.9 copy-start.13
  10.7 3.1 copy-start.10
  10.7 3.3 copy-start.6
  15.1 7.7 %copy-start.7 = (f32[64,128]{1,0:T(8,128)S(1)}, f32[64,128]{1,0:T(8,128)}, u32[]{:S(2)}) copy-start(f32[64,128]{1,0:T(8,128)} %constant.78.clone) | copy-start | bytes 98308
  15.1 7.7 %copy-start.8 = (f32[64,128]{1,0:T(8,128)S(1)}, f32[64,128]{1,0:T(8,128)}, u32[]{:S(2)}) copy-start(f32[64,128]{1,0:T(8,128)} %constant.77.clone) | copy-start | bytes 98308
  15.1 7.7 %copy-start.11 = (f32[36,128]{1,0:T(8,128)S(1)}, f32[36,128]{1,0:T(8,128)}, u32[]{:S(2)}) copy-start(f32[36,128]{1,0:T(8,128)} %constant.80.clone) | copy-start | bytes 55300
  15.1 7.7 %copy-start.12 = (f32[36,128]{1,0:T(8,128)S(1)}, f32[36,128]{1,0:T(8,128)}, u32[]{:S(2)}) copy-start(f32[36,128]{1,0:T(8,128)} %constant.79.clone) | copy-start | bytes 55300
  191.3 1.0 copy-start.1
  281.2 79.3 %copy-start.4 = (f32[1024,12]{1,0:T(8,128)S(1)}, f32[1024,12]{1,0:T(8,128)}, u32[]{:S(2)}) copy-start(f32[1024,12]{1,0:T(8,128)} %get-tuple-element.157) | copy-start | bytes 147460
  361.3 3.3 copy-start.5
  365.2 66.1 %all-to-all-start = ((bf16[2,3,768,256]{3,2,1,0:T(8,128)(2,1)}), bf16[2,3,768,256]{3,2,1,0:T(8,128)(2,1)S(1)}, u32[]{:S(2)}, u32[]{:S(2)}) async-start(bf16[2,3,768,256]{3,2,1,0:T(8,128)(2,1)} %bitcast.37), calls=%async_computation.1 | async-start | bytes 4718592 | tf_op jit(solution)/shard_map/all_to_all | solution.py:1200
  433.8 1.6 copy-start.3
  435.4 2.5 copy-start.2
Sparse Core Ops, SparseCore 0:
  10.2 30.0 all-gather.1
  191.5 166.3 reduce-scatter.1
